TPU v7x, 256 devices: a whole 4x4x8 slice. The times are simulated.
256 devices in a mesh: seq: 64 (over z, x, core), head: 4 (over y).
Axes of the slice: x: 4, y: 4, z: 8, core: 2. Of those that a mesh axis runs over, the one named last changes fastest.
Arguments:
- queries: bfloat16 [768, 65536], P('head', 'seq'), may hold values from -6 to 6
- keys: bfloat16 [768, 65536], P('head', 'seq'), may hold values from -6 to 6
- values: bfloat16 [768, 65536], P('head', 'seq'), may hold values from -36 to 36
- slide_lengths: int32 [64], replicated, may hold values from 1 to 16384, 65536 in all
- norm_gain: float32 [768], P('head'), may hold values from 0.1 to 1.9
- norm_bias: float32 [768], P('head'), may hold values from -3 to 3
Outputs:
- encoded: bfloat16 [768, 65536], P('head', 'seq')
Inputs may be any that keep to these rules, and one draw needn't show every extreme that they name: `slide_lengths`: positive slide lengths that sum to 65536; the longest is exactly 16384.
All inputs are finite; a program needn't handle non-finite values.
Results may differ from a plain program's by a relative error of at most 0.0041.
Values may be sent and summed in bfloat16 or wider, within the bound.
A program may use at most 128 MiB of HBM per device.

v0:
```python
import math

import jax
import jax.numpy as jnp
from jax import lax
from jax.sharding import PartitionSpec as P

D = 768
HD = 48
SEG = 1024


def partner_2(value, axis, distance):
    mask = 2**distance
    pairs = [(source, source ^ mask) for source in range(lax.axis_size(axis))]
    return lax.ppermute(value, axis, pairs)


def slide_of(positions, slide_ends):
    return jnp.sum((positions[..., None] >= slide_ends).astype(jnp.int32), axis=-1)


def attend(query_rows, key_rows, value_rows, query_slide, key_slide):
    score_scale = 1.0 / math.sqrt(HD)
    scores = (
        jnp.einsum("nhd,khd->hnk", query_rows, key_rows, preferred_element_type=jnp.float32)
        * score_scale
    )
    same_slide = query_slide.T[:, :, None] == key_slide.T[:, None, :]
    scores = jnp.where(same_slide, scores, -1e30)
    row_peak = jnp.max(scores, axis=-1)
    probabilities = jnp.exp(scores - row_peak[..., None])
    totals = jnp.sum(probabilities, axis=-1)
    weighted = jnp.einsum(
        "hnk,khd->nhd",
        probabilities.astype(jnp.bfloat16),
        value_rows,
        preferred_element_type=jnp.float32,
    )
    return (row_peak.T, totals.T, weighted)


def attend_segment(segment_items):
    return attend(*segment_items)


def pick_rows(shaped, dilation, chosen):
    leading = shaped.shape[:-3]
    row_count, head_count, head_size = shaped.shape[-3:]
    split = shaped.reshape(leading + (row_count // dilation, dilation, head_count, head_size))
    return jnp.sum(jnp.where(chosen[:, :, None], split, jnp.zeros((), shaped.dtype)), axis=-3)


def spread(compact, dilation, chosen, filler):
    extra = compact.ndim - 2
    widened = chosen.reshape(chosen.shape + (1,) * extra)
    full = jnp.where(widened[None], compact[:, None], filler)
    return full.reshape((compact.shape[0] * dilation,) + compact.shape[1:])


def collect(flat_pairs, first_bit, last_bit, seq_place):
    for bit_index in range(first_bit, last_bit):
        partner = partner_2(flat_pairs, "seq", bit_index)
        is_upper = seq_place // 2**bit_index % 2 == 1
        flat_pairs = jnp.where(
            is_upper,
            jnp.concatenate([partner, flat_pairs], axis=1),
            jnp.concatenate([flat_pairs, partner], axis=1),
        )
    return flat_pairs


def per_device(queries, keys, values, slide_lengths, norm_gain, norm_bias):
    queries = queries.T
    keys = keys.T
    values = values.T
    row_count, col_count = queries.shape
    head_count = col_count // HD
    seq_place = lax.axis_index("seq")
    total_rows = row_count * lax.axis_size("seq")
    slide_ends = jnp.cumsum(slide_lengths)
    head_ids = lax.axis_index("head") * head_count + jnp.arange(head_count, dtype=jnp.int32)
    row_start = seq_place * row_count
    q_shaped = queries.reshape(row_count, head_count, HD)
    kv_shaped = jnp.stack(
        [keys.reshape(row_count, head_count, HD), values.reshape(row_count, head_count, HD)]
    )
    running_peak = None
    weight = None
    accumulated = None
    for branch in range(4):
        dilation = 4**branch
        seg_span = min(SEG * dilation, total_rows)
        seg_keys = seg_span // dilation
        local_rows = row_count // dilation
        offsets = head_ids % dilation
        chosen = jnp.arange(dilation, dtype=jnp.int32)[:, None] == offsets[None, :]
        query_rows = pick_rows(q_shaped, dilation, chosen)
        query_pos = (
            row_start
            + dilation * jnp.arange(local_rows, dtype=jnp.int32)[:, None]
            + offsets[None, :]
        )
        query_slide = slide_of(query_pos, slide_ends)
        if seg_span <= row_count:
            key_value = pick_rows(kv_shaped, dilation, chosen)
            segment_count = row_count // seg_span
            items = (
                query_rows.reshape(segment_count, seg_keys, head_count, HD),
                key_value[0].reshape(segment_count, seg_keys, head_count, HD),
                key_value[1].reshape(segment_count, seg_keys, head_count, HD),
                query_slide.reshape(segment_count, seg_keys, head_count),
                query_slide.reshape(segment_count, seg_keys, head_count),
            )
            row_peak, totals, weighted = lax.map(attend_segment, items)
            row_peak = row_peak.reshape(local_rows, head_count)
            totals = totals.reshape(local_rows, head_count)
            weighted = weighted.reshape(local_rows, head_count, HD)
        else:
            group_size = seg_span // row_count
            bit_count = group_size.bit_length() - 1
            source = pick_rows(kv_shaped, dilation, chosen)
            first_bit = 0
            source_rows = source.shape[1]
            flat_pairs = collect(
                source.reshape(2, source_rows, col_count), first_bit, bit_count, seq_place
            )
            key_value = flat_pairs.reshape(2, seg_keys, head_count, HD)
            group_start = seq_place // group_size * seg_span
            key_pos = (
                group_start
                + dilation * jnp.arange(seg_keys, dtype=jnp.int32)[:, None]
                + offsets[None, :]
            )
            key_slide = slide_of(key_pos, slide_ends)
            row_peak, totals, weighted = attend(
                query_rows, key_value[0], key_value[1], query_slide, key_slide
            )
        peak_full = spread(row_peak, dilation, chosen, jnp.float32(-1e30))
        total_full = spread(totals, dilation, chosen, jnp.float32(0.0))
        mixed_full = spread(weighted, dilation, chosen, jnp.float32(0.0))
        if running_peak is None:
            running_peak, weight, accumulated = (peak_full, total_full, mixed_full)
        else:
            newest = jnp.maximum(running_peak, peak_full)
            keep_old = jnp.exp(running_peak - newest)
            keep_new = jnp.exp(peak_full - newest)
            weight = weight * keep_old + total_full * keep_new
            accumulated = accumulated * keep_old[..., None] + mixed_full * keep_new[..., None]
            running_peak = newest
    attended = (accumulated / weight[..., None]).reshape(row_count, col_count)
    feature_sums = lax.psum(
        (jnp.sum(attended, axis=1), jnp.sum(attended * attended, axis=1)), "head"
    )
    row_mean = feature_sums[0] / D
    variance = feature_sums[1] / D - row_mean * row_mean
    normed = (attended - row_mean[:, None]) * lax.rsqrt(variance + 1e-05)[:, None]
    return (normed * norm_gain + norm_bias).astype(jnp.bfloat16).T


def solution(mesh):
    placed = (P("head", "seq"), P("head", "seq"), P("head", "seq"), P(), P("head"), P("head"))
    return jax.shard_map(
        per_device, mesh=mesh, in_specs=placed, out_specs=P("head", "seq"), check_vma=False
    )
```

profile of v0, /device:TPU:4, one launch (start us, length us, event | category | flops | bytes accessed | tf_op | source)
XLA Modules:
  0.0 137.4 jit_solution(9462733910838847863)
XLA Ops:
  0.1 1.7 %stack.25 = bf16[1,16,64,4,48]{2,1,4,3,0:T(8,128)(2,1)S(1)} reshape(bf16[1024,192]{0,1:T(8,128)(2,1)} %bitcast.165) | data formatting | bytes 786432 | tf_op jit(solution)/shard_map/stack | solution.py:85
  1.8 1.6 %stack.26 = bf16[1,16,64,4,48]{2,1,4,3,0:T(8,128)(2,1)S(1)} reshape(bf16[1024,192]{0,1:T(8,128)(2,1)} %bitcast.171) | data formatting | bytes 786432 | tf_op jit(solution)/shard_map/stack | solution.py:85
  3.5 0.9 fusion.11
  6.6 3.0 %fusion.8 = bf16[2,64,4,48]{3,2,1,0:T(4,128)(2,1)} fusion(bf16[1,64,16,4,48]{4,3,2,1,0:T(4,128)(2,1)S(1)} %stack.23, bf16[1,64,16,4,48]{4,3,2,1,0:T(4,128)(2,1)S(1)} %stack.22, pred[16,4]{1,0:T(8,128)(4,1)S(1)} %iota_compare_fusion), kind=kLoop, calls=%fused_computation.12 | loop fusion | flops 1155072 | bytes 835648 | tf_op jit(solution)/shard_map/reduce_sum | solution.py:51
  9.6 1.7 %copy.252 = bf16[2,64,4,48]{1,3,2,0:T(8,128)(2,1)} copy(bf16[2,64,4,48]{3,2,1,0:T(4,128)(2,1)} %fusion.8) | data formatting | bytes 98304 | tf_op jit(solution)/shard_map/reduce_sum | solution.py:51
  15.6 0.9 fusion.25
  19.0 1.6 %reshape_reshape.12 = bf16[16,64,4,48]{1,0,3,2:T(8,128)(2,1)S(1)} reshape(bf16[1024,192]{0,1:T(8,128)(2,1)} %bitcast.168) | data formatting | bytes 786432 | tf_op jit(solution)/shard_map/reshape;reshape | solution.py:50
  25.8 1.1 select_reduce_fusion.2
  26.9 1.4 %select_reduce_fusion = bf16[64,4,48]{2,1,0:T(4,128)(2,1)} fusion(bf16[64,16,4,48]{3,2,1,0:T(4,128)(2,1)S(1)} %reshape_reshape.11, pred[16,4]{1,0:T(8,128)(4,1)S(1)} %iota_compare_fusion), kind=kLoop, calls=%fused_computation.28 | loop fusion | flops 380928 | bytes 417856 | tf_op jit(solution)/shard_map/reduce_sum | solution.py:51
  28.3 0.9 select_reduce_fusion.1
  29.2 1.1 convert_reduce_fusion.3
  30.4 4.8 %fusion.2 = (f32[4,1024]{1,0:T(4,128)S(1)}, f32[4,1024,1024]{1,2,0:T(8,128)S(1)}) fusion(s32[4,1024]{1,0:T(4,128)S(1)} %bitcast.181, bf16[1024,4,48]{0,2,1:T(8,128)(2,1)} %bitcast.169, bf16[1024,4,48]{0,2,1:T(8,128)(2,1)} %bitcast.166), kind=kOutput, calls=%fused_computation.4 | convolution fusion | flops 419426304 | bytes 17596416 | tf_op jit(solution)/shard_map/while/body/eval_jaxpr/nhd,khd->hnk/dot_general | solution.py:26
  35.3 5.5 %fusion = f32[4,1024]{1,0:T(4,128)} fusion(f32[4,1024,1024]{1,2,0:T(8,128)S(1)} %get-tuple-element.78, f32[4,1024]{1,0:T(4,128)S(1)} %get-tuple-element.77, s32[4,1024]{1,0:T(4,128)S(1)} %bitcast.182), kind=kLoop, calls=%fused_computation.2 | loop fusion | flops 20967424 | bytes 16826368 | tf_op jit(solution)/shard_map/while/body/eval_jaxpr/reduce_sum | solution.py:33
  41.9 1.3 collective-permute-start.7
  45.7 0.9 broadcast_in_dim.405
  46.7 1.6 %collective-permute-start.8 = (bf16[2,64,192]{2,1,0:T(8,128)(2,1)S(1)}, bf16[2,64,192]{2,1,0:T(8,128)(2,1)S(1)}, u32[]{:S(2)}, u32[]{:S(2)}) collective-permute-start(bf16[2,64,192]{2,1,0:T(8,128)(2,1)S(1)} %maximum_select_fusion.13), channel_id=1, source_target_pairs={{0,16},{4,20},{8,24},{12,28},{16,0},{20,4},{24,8},{28,12},{32,48},... | collective-permute-start | bytes 147464 | tf_op jit(solution)/shard_map/ppermute | solution.py:16
  48.3 1.2 maximum_select_fusion.12
  49.4 2.2 %collective-permute-start.3 = (bf16[2,128,192]{1,2,0:T(8,128)(2,1)S(1)}, bf16[2,128,192]{1,2,0:T(8,128)(2,1)S(1)}, u32[]{:S(2)}, u32[]{:S(2)}) collective-permute-start(bf16[2,128,192]{1,2,0:T(8,128)(2,1)S(1)} %maximum_select_fusion.12), channel_id=1, source_target_pairs={{0,8},{4,12},{8,0},{12,4},{16,24},{20,28},{24,16},{28,20},{32,40},... | collective-permute-start | bytes 294920 | tf_op jit(solution)/shard_map/ppermute | solution.py:16
  51.7 1.1 collective-permute-done.8
  52.8 2.0 %collective-permute-start.9 = (bf16[2,128,192]{2,1,0:T(8,128)(2,1)S(1)}, bf16[2,128,192]{2,1,0:T(8,128)(2,1)S(1)}, u32[]{:S(2)}, u32[]{:S(2)}) collective-permute-start(bf16[2,128,192]{2,1,0:T(8,128)(2,1)S(1)} %maximum_select_fusion.11), channel_id=1, source_target_pairs={{0,32},{4,36},{8,40},{12,44},{16,48},{20,52},{24,56},{28,60},{32,0... | collective-permute-start | bytes 294920 | tf_op jit(solution)/shard_map/ppermute | solution.py:16
  54.9 1.5 %collective-permute-start.4 = (bf16[2,256,192]{1,2,0:T(8,128)(2,1)S(1)}, bf16[2,256,192]{1,2,0:T(8,128)(2,1)S(1)}, u32[]{:S(2)}, u32[]{:S(2)}) collective-permute-start(bf16[2,256,192]{1,2,0:T(8,128)(2,1)S(1)} %maximum_select_fusion.10), channel_id=1, source_target_pairs={{0,16},{4,20},{8,24},{12,28},{16,0},{20,4},{24,8},{28,12},{32,48},... | collective-permute-start | bytes 589832 | tf_op jit(solution)/shard_map/ppermute | solution.py:16
  56.3 1.3 maximum_select_fusion.7
  57.7 1.4 %collective-permute-start.1 = (bf16[2,512,192]{1,2,0:T(8,128)(2,1)S(1)}, bf16[2,512,192]{1,2,0:T(8,128)(2,1)S(1)}, u32[]{:S(2)}, u32[]{:S(2)}) collective-permute-start(bf16[2,512,192]{1,2,0:T(8,128)(2,1)S(1)} %maximum_select_fusion.7), channel_id=1, source_target_pairs={{0,8},{4,12},{8,0},{12,4},{16,24},{20,28},{24,16},{28,20},{32,40},... | collective-permute-start | bytes 1179656 | tf_op jit(solution)/shard_map/ppermute | solution.py:16
  59.1 3.4 %collective-permute-start.10 = (bf16[2,256,192]{2,1,0:T(8,128)(2,1)S(1)}, bf16[2,256,192]{2,1,0:T(8,128)(2,1)S(1)}, u32[]{:S(2)}, u32[]{:S(2)}) collective-permute-start(bf16[2,256,192]{2,1,0:T(8,128)(2,1)S(1)} %maximum_select_fusion.9), channel_id=1, source_target_pairs={{0,64},{4,68},{8,72},{12,76},{16,80},{20,84},{24,88},{28,92},{32,9... | collective-permute-start | bytes 589832 | tf_op jit(solution)/shard_map/ppermute | solution.py:16
  63.3 1.0 collective-permute-done.4
  64.4 1.0 collective-permute-start.5
  65.4 8.1 %collective-permute-done.10 = bf16[2,256,192]{2,1,0:T(8,128)(2,1)S(1)} collective-permute-done((bf16[2,256,192]{2,1,0:T(8,128)(2,1)S(1)}, bf16[2,256,192]{2,1,0:T(8,128)(2,1)S(1)}, u32[]{:S(2)}, u32[]{:S(2)}) %collective-permute-start.10) | collective-permute-done | bytes 196640 | tf_op jit(solution)/shard_map/ppermute | solution.py:16
  73.5 1.0 maximum_select_fusion.6
  74.5 6.5 %collective-permute-start.11 = (bf16[2,512,192]{2,1,0:T(8,128)(2,1)}, bf16[2,512,192]{2,1,0:T(8,128)(2,1)}, u32[]{:S(2)}, u32[]{:S(2)}) collective-permute-start(bf16[2,512,192]{2,1,0:T(8,128)(2,1)} %maximum_select_fusion.6), channel_id=1, source_target_pairs={{0,128},{4,132},{8,136},{12,140},{16,144},{20,148},{24,152},{28,15... | collective-permute-start | bytes 1179656 | tf_op jit(solution)/shard_map/ppermute | solution.py:16
  81.3 1.1 fusion.7
  82.4 1.9 %copy-done.1 = f32[4,256,1024]{2,1,0:T(8,128)} copy-done((f32[4,256,1024]{2,1,0:T(8,128)}, f32[4,256,1024]{2,1,0:T(8,128)S(1)}, u32[]{:S(2)}) %copy-start.1) | copy-done | bytes 4194328
  84.3 1.8 %fusion.20 = f32[256,4,48]{0,2,1:T(8,128)S(1)} fusion(bf16[1024,4,48]{0,2,1:T(8,128)(2,1)S(1)} %bitcast.178, f32[4,256,1024]{2,1,0:T(8,128)S(1)} %get-tuple-element.76, f32[4,256]{1,0:T(4,128)S(1)} %get-tuple-element.75, s32[4,1024]{1,0:T(4,128)S(1)} %bitcast.185, s32[4,256]{1,0:T(4,128)S(1)} %bitcast.193), kind=kOutput, calls=%fused_computation.22 | convolution fusion | flops 105906176 | bytes 4808704 | tf_op jit(solution)/shard_map/hnk,khd->nhd/dot_general | solution.py:34
  86.8 0.9 broadcast_in_dim.412
  87.7 2.9 %fusion.5 = f32[4,256]{1,0:T(4,128)S(1)} fusion(f32[4,256,1024]{2,1,0:T(8,128)} %copy-done.1, f32[4,256]{1,0:T(4,128)S(1)} %get-tuple-element.75, s32[4,1024]{1,0:T(4,128)S(1)} %bitcast.186, s32[4,256]{1,0:T(4,128)S(1)} %bitcast.194), kind=kLoop, calls=%fused_computation.8 | loop fusion | flops 5241856 | bytes 4222976 | tf_op jit(solution)/shard_map/reduce_sum | solution.py:33
  90.7 0.9 broadcast_in_dim.446
  92.0 1.5 %copy.264 = f32[1024,4,48]{0,2,1:T(8,128)} copy(f32[1024,4,48]{2,0,1:T(8,128)S(1)} %bitcast.163) | data formatting | bytes 1572864 | tf_op jit(solution)/shard_map/jit(_where)/broadcast_in_dim | solution.py:57
  93.7 0.9 broadcast_in_dim.417
  94.7 1.2 copy.247
  95.9 1.3 maximum_select_fusion.5
  100.4 1.5 %copy.265 = f32[1024,4,48]{0,2,1:T(8,128)} copy(f32[1024,4,48]{2,0,1:T(8,128)S(1)} %bitcast.164) | data formatting | bytes 1572864 | tf_op jit(solution)/shard_map/jit(_where)/broadcast_in_dim | solution.py:57
  102.1 0.9 broadcast_in_dim.431
  103.0 1.2 copy.256
  104.3 1.8 %maximum_select_fusion.2 = bf16[2,1024,192]{2,1,0:T(8,128)(2,1)S(1)} fusion(bf16[2,512,192]{2,1,0:T(8,128)(2,1)} %maximum_select_fusion.6, bf16[2,512,192]{2,1,0:T(8,128)(2,1)} %collective-permute-done.11, pred[]{:T(512)S(6)} %eq.199), kind=kLoop, calls=%fused_computation.25 | loop fusion | flops 3538944 | bytes 1572865 | tf_op jit(solution)/shard_map/jit(_where)/select_n | solution.py:65
  108.6 1.3 broadcast_in_dim.455
  112.0 0.9 fusion.49
  113.0 10.7 %fusion.56 = (f32[1024]{0:T(1024)}, f32[1024]{0:T(1024)}, f32[1024,4,48]{0,2,1:T(8,128)}) fusion(f32[1024,4]{0,1:T(4,128)S(1)} %get-tuple-element.56, f32[1024,4]{0,1:T(4,128)S(1)} %get-tuple-element.59, f32[1024,4,48]{0,2,1:T(8,128)} %broadcast_in_dim.455, pred[1024,4]{0,1:T(4,128)(4,1)} %broadcast_in_dim.433, f32[1024,4]{0,1:T(4,128)S(1)} %get-tuple-element.61, ...), kind=kOutput, calls=%fused_computation.124 | convolution fusion | flops 426768384 | bytes 20484096 | tf_op jit(solution)/shard_map/while/body/eval_jaxpr/hnk,khd->nhd/dot_general | solution.py:34
  123.8 11.0 %all-reduce = (f32[1024]{0:T(1024)S(1)}, f32[1024]{0:T(1024)S(1)}) all-reduce(f32[1024]{0:T(1024)} %get-tuple-element.49, f32[1024]{0:T(1024)} %get-tuple-element.48), channel_id=1, replica_groups=mesh['seq'=64,'head'=4] {'head'}, use_global_device_ids=true, to_apply=%region_25.26 | all-reduce | flops 2048 | bytes 16384 | tf_op jit(solution)/shard_map/psum | solution.py:152
  134.8 2.6 %fusion.33 = bf16[1024,192]{0,1:T(8,128)(2,1)} fusion(f32[1024,192]{0,1:T(8,128)S(1)} %broadcast_in_dim.444, f32[1024,192]{0,1:T(8,128)S(1)} %copy-done.3, f32[1024,192]{0,1:T(8,128)S(1)} %copy-done.2, f32[1024,4,48]{0,2,1:T(8,128)} %get-tuple-element.81, f32[192]{0:T(256)} %param.11, f32[192]{0:T(256)} %param.10, f32[1024]{0:T(1024)S(1)} %get-tuple-element.70, ...), kind=kLoop, calls=%fused_computation.55 | loop fusion | flops 3342336 | bytes 3659264 | tf_op jit(solution)/shard_map/convert_element_type | solution.py:158
  (162 shorter events, 28.3 us)
Async XLA Ops:
  0.0 5.1 %copy-start.4 = (bf16[192,1024]{1,0:T(8,128)(2,1)S(1)}, bf16[192,1024]{1,0:T(8,128)(2,1)}, u32[]{:S(2)}) copy-start(bf16[192,1024]{1,0:T(8,128)(2,1)} %param.7) | copy-start | bytes 1179652
  0.0 5.3 %copy-start.6 = (bf16[192,1024]{1,0:T(8,128)(2,1)S(1)}, bf16[192,1024]{1,0:T(8,128)(2,1)}, u32[]{:S(2)}) copy-start(bf16[192,1024]{1,0:T(8,128)(2,1)} %param.8) | copy-start | bytes 1179652
  0.0 1.8 %copy-start.30 = (s32[4]{0:T(128)}, s32[4]{0:T(128)S(1)}, u32[]{:S(2)}) copy-start(s32[4]{0:T(128)S(1)} %get-tuple-element.82) | copy-start | bytes 52
  0.1 25.6 %copy-start.25 = (pred[64,4]{0,1:T(4,128)(4,1)}, pred[64,4]{0,1:T(4,128)(4,1)S(1)}, u32[]{:S(2)}) copy-start(pred[64,4]{0,1:T(4,128)(4,1)S(1)} %iota_compare_fusion.1) | copy-start | bytes 772
  5.1 36.0 %collective-permute-start.6 = (bf16[2,16,192]{2,1,0:T(8,128)(2,1)}, bf16[2,16,192]{2,1,0:T(8,128)(2,1)}, u32[]{:S(2)}, u32[]{:S(2)}) collective-permute-start(bf16[2,16,192]{2,1,0:T(8,128)(2,1)} %copy.257), channel_id=1, source_target_pairs={{0,4},{4,0},{8,12},{12,8},{16,20},{20,16},{24,28},{28,24},{32,36},... | collective-permute-start | bytes 36872 | tf_op jit(solution)/shard_map/ppermute | solution.py:16
  5.5 21.4 %copy-start.20 = (pred[16,4]{1,0:T(8,128)(4,1)}, pred[16,4]{1,0:T(8,128)(4,1)S(1)}, u32[]{:S(2)}) copy-start(pred[16,4]{1,0:T(8,128)(4,1)S(1)} %iota_compare_fusion) | copy-start | bytes 196
  9.6 9.2 %copy-start.5 = (bf16[192,1024]{1,0:T(8,128)(2,1)S(1)}, bf16[192,1024]{1,0:T(8,128)(2,1)}, u32[]{:S(2)}) copy-start(bf16[192,1024]{1,0:T(8,128)(2,1)} %param.6) | copy-start | bytes 1179652
  11.3 37.0 %collective-permute-start.2 = (bf16[2,64,192]{1,2,0:T(8,128)(2,1)}, bf16[2,64,192]{1,2,0:T(8,128)(2,1)}, u32[]{:S(2)}, u32[]{:S(2)}) collective-permute-start(bf16[2,64,192]{1,2,0:T(8,128)(2,1)} %bitcast.22), channel_id=1, source_target_pairs={{0,4},{4,0},{8,12},{12,8},{16,20},{20,16},{24,28},{28,24},{32,36},... | collective-permute-start | bytes 147464 | tf_op jit(solution)/shard_map/ppermute | solution.py:16
  14.0 14.3 %copy-start.27 = (pred[4,4]{1,0:T(4,128)(4,1)}, pred[4,4]{1,0:T(4,128)(4,1)S(1)}, u32[]{:S(2)}) copy-start(pred[4,4]{1,0:T(4,128)(4,1)S(1)} %iota_compare_fusion.2) | copy-start | bytes 52
  16.5 39.8 %collective-permute-start = (bf16[2,256,192]{1,2,0:T(8,128)(2,1)}, bf16[2,256,192]{1,2,0:T(8,128)(2,1)}, u32[]{:S(2)}, u32[]{:S(2)}) collective-permute-start(bf16[2,256,192]{1,2,0:T(8,128)(2,1)} %bitcast.12), channel_id=1, source_target_pairs={{0,4},{4,0},{8,12},{12,8},{16,20},{20,16},{24,28},{28,24},{32,36},... | collective-permute-start | bytes 589832 | tf_op jit(solution)/shard_map/ppermute | solution.py:16
  19.0 2.8 %copy-start.33 = (s32[16]{0:T(128)S(1)}, s32[16]{0:T(128)}, u32[]{:S(2)}) copy-start(s32[16]{0:T(128)} %multiply_add_fusion.4) | copy-start | bytes 196
  19.0 3.5 %copy-start.32 = (s32[64]{0:T(128)S(1)}, s32[64]{0:T(128)}, u32[]{:S(2)}) copy-start(s32[64]{0:T(128)} %multiply_add_fusion.5) | copy-start | bytes 772
  19.0 3.6 %copy-start.31 = (s32[256]{0:T(256)S(1)}, s32[256]{0:T(256)}, u32[]{:S(2)}) copy-start(s32[256]{0:T(256)} %multiply_add_fusion.3) | copy-start | bytes 3076
  19.0 10.2 %copy-start.23 = (s32[1024]{0:T(1024)S(1)}, s32[1024]{0:T(1024)}, u32[]{:S(2)}) copy-start(s32[1024]{0:T(1024)} %iota_add_fusion) | copy-start | bytes 12292
  35.2 5.7 %copy-start = (f32[4,1024,1024]{1,2,0:T(8,128)}, f32[4,1024,1024]{1,2,0:T(8,128)S(1)}, u32[]{:S(2)}) copy-start(f32[4,1024,1024]{1,2,0:T(8,128)S(1)} %get-tuple-element.78) | copy-start | bytes 50331652
  35.2 5.7 %copy-start.18 = (f32[4,1024]{1,0:T(4,128)}, f32[4,1024]{1,0:T(4,128)S(1)}, u32[]{:S(2)}) copy-start(f32[4,1024]{1,0:T(4,128)S(1)} %get-tuple-element.77) | copy-start | bytes 49156
  35.3 8.8 %copy-start.28 = (pred[4,4]{1,0:T(4,128)(4,1)S(1)}, pred[4,4]{1,0:T(4,128)(4,1)}, u32[]{:S(2)}) copy-start(pred[4,4]{1,0:T(4,128)(4,1)} %copy-done.27) | copy-start | bytes 52
  35.3 8.9 %copy-start.21 = (pred[16,4]{1,0:T(8,128)(4,1)S(1)}, pred[16,4]{1,0:T(8,128)(4,1)}, u32[]{:S(2)}) copy-start(pred[16,4]{1,0:T(8,128)(4,1)} %copy-done.20) | copy-start | bytes 196
  35.3 9.0 %copy-start.26 = (pred[64,4]{0,1:T(4,128)(4,1)S(1)}, pred[64,4]{0,1:T(4,128)(4,1)}, u32[]{:S(2)}) copy-start(pred[64,4]{0,1:T(4,128)(4,1)} %copy-done.25) | copy-start | bytes 772
  41.9 4.7 %collective-permute-start.7 = (bf16[2,32,192]{2,1,0:T(8,128)(2,1)S(1)}, bf16[2,32,192]{2,1,0:T(8,128)(2,1)S(1)}, u32[]{:S(2)}, u32[]{:S(2)}) collective-permute-start(bf16[2,32,192]{2,1,0:T(8,128)(2,1)S(1)} %maximum_select_fusion.14), channel_id=1, source_target_pairs={{0,8},{4,12},{8,0},{12,4},{16,24},{20,28},{24,16},{28,20},{32,40},... | collective-permute-start | bytes 73736 | tf_op jit(solution)/shard_map/ppermute | solution.py:16
  46.7 6.1 %collective-permute-start.8 = (bf16[2,64,192]{2,1,0:T(8,128)(2,1)S(1)}, bf16[2,64,192]{2,1,0:T(8,128)(2,1)S(1)}, u32[]{:S(2)}, u32[]{:S(2)}) collective-permute-start(bf16[2,64,192]{2,1,0:T(8,128)(2,1)S(1)} %maximum_select_fusion.13), channel_id=1, source_target_pairs={{0,16},{4,20},{8,24},{12,28},{16,0},{20,4},{24,8},{28,12},{32,48},... | collective-permute-start | bytes 147464 | tf_op jit(solution)/shard_map/ppermute | solution.py:16
  49.4 5.4 %collective-permute-start.3 = (bf16[2,128,192]{1,2,0:T(8,128)(2,1)S(1)}, bf16[2,128,192]{1,2,0:T(8,128)(2,1)S(1)}, u32[]{:S(2)}, u32[]{:S(2)}) collective-permute-start(bf16[2,128,192]{1,2,0:T(8,128)(2,1)S(1)} %maximum_select_fusion.12), channel_id=1, source_target_pairs={{0,8},{4,12},{8,0},{12,4},{16,24},{20,28},{24,16},{28,20},{32,40},... | collective-permute-start | bytes 294920 | tf_op jit(solution)/shard_map/ppermute | solution.py:16
  52.8 6.2 %collective-permute-start.9 = (bf16[2,128,192]{2,1,0:T(8,128)(2,1)S(1)}, bf16[2,128,192]{2,1,0:T(8,128)(2,1)S(1)}, u32[]{:S(2)}, u32[]{:S(2)}) collective-permute-start(bf16[2,128,192]{2,1,0:T(8,128)(2,1)S(1)} %maximum_select_fusion.11), channel_id=1, source_target_pairs={{0,32},{4,36},{8,40},{12,44},{16,48},{20,52},{24,56},{28,60},{32,0... | collective-permute-start | bytes 294920 | tf_op jit(solution)/shard_map/ppermute | solution.py:16
  54.9 9.4 %collective-permute-start.4 = (bf16[2,256,192]{1,2,0:T(8,128)(2,1)S(1)}, bf16[2,256,192]{1,2,0:T(8,128)(2,1)S(1)}, u32[]{:S(2)}, u32[]{:S(2)}) collective-permute-start(bf16[2,256,192]{1,2,0:T(8,128)(2,1)S(1)} %maximum_select_fusion.10), channel_id=1, source_target_pairs={{0,16},{4,20},{8,24},{12,28},{16,0},{20,4},{24,8},{28,12},{32,48},... | collective-permute-start | bytes 589832 | tf_op jit(solution)/shard_map/ppermute | solution.py:16
  57.7 23.4 %collective-permute-start.1 = (bf16[2,512,192]{1,2,0:T(8,128)(2,1)S(1)}, bf16[2,512,192]{1,2,0:T(8,128)(2,1)S(1)}, u32[]{:S(2)}, u32[]{:S(2)}) collective-permute-start(bf16[2,512,192]{1,2,0:T(8,128)(2,1)S(1)} %maximum_select_fusion.7), channel_id=1, source_target_pairs={{0,8},{4,12},{8,0},{12,4},{16,24},{20,28},{24,16},{28,20},{32,40},... | collective-permute-start | bytes 1179656 | tf_op jit(solution)/shard_map/ppermute | solution.py:16
  59.1 14.3 %collective-permute-start.10 = (bf16[2,256,192]{2,1,0:T(8,128)(2,1)S(1)}, bf16[2,256,192]{2,1,0:T(8,128)(2,1)S(1)}, u32[]{:S(2)}, u32[]{:S(2)}) collective-permute-start(bf16[2,256,192]{2,1,0:T(8,128)(2,1)S(1)} %maximum_select_fusion.9), channel_id=1, source_target_pairs={{0,64},{4,68},{8,72},{12,76},{16,80},{20,84},{24,88},{28,92},{32,9... | collective-permute-start | bytes 589832 | tf_op jit(solution)/shard_map/ppermute | solution.py:16
  64.4 31.5 %collective-permute-start.5 = (bf16[2,512,192]{1,2,0:T(8,128)(2,1)S(1)}, bf16[2,512,192]{1,2,0:T(8,128)(2,1)}, u32[]{:S(2)}, u32[]{:S(2)}) collective-permute-start(bf16[2,512,192]{1,2,0:T(8,128)(2,1)S(1)} %maximum_select_fusion.8), channel_id=1, source_target_pairs={{0,32},{4,36},{8,40},{12,44},{16,48},{20,52},{24,56},{28,60},{32,0... | collective-permute-start | bytes 1179656 | tf_op jit(solution)/shard_map/ppermute | solution.py:16
  74.5 29.8 %collective-permute-start.11 = (bf16[2,512,192]{2,1,0:T(8,128)(2,1)}, bf16[2,512,192]{2,1,0:T(8,128)(2,1)}, u32[]{:S(2)}, u32[]{:S(2)}) collective-permute-start(bf16[2,512,192]{2,1,0:T(8,128)(2,1)} %maximum_select_fusion.6), channel_id=1, source_target_pairs={{0,128},{4,132},{8,136},{12,140},{16,144},{20,148},{24,152},{28,15... | collective-permute-start | bytes 1179656 | tf_op jit(solution)/shard_map/ppermute | solution.py:16
  82.4 1.9 %copy-start.1 = (f32[4,256,1024]{2,1,0:T(8,128)}, f32[4,256,1024]{2,1,0:T(8,128)S(1)}, u32[]{:S(2)}) copy-start(f32[4,256,1024]{2,1,0:T(8,128)S(1)} %get-tuple-element.76) | copy-start | bytes 12582916
  94.7 2.6 %copy-start.16 = (bf16[64,4,48]{2,1,0:T(4,128)(2,1)S(1)}, bf16[64,4,48]{2,1,0:T(4,128)(2,1)}, u32[]{:S(2)}) copy-start(bf16[64,4,48]{2,1,0:T(4,128)(2,1)} %select_reduce_fusion) | copy-start | bytes 73732
  94.7 2.6 %copy-start.22 = (s32[1024,4]{0,1:T(4,128)S(1)}, s32[1024,4]{0,1:T(4,128)}, u32[]{:S(2)}) copy-start(s32[1024,4]{0,1:T(4,128)} %get-tuple-element.52) | copy-start | bytes 49156
  94.7 2.6 %copy-start.29 = (s32[64,4]{0,1:T(4,128)S(1)}, s32[64,4]{0,1:T(4,128)}, u32[]{:S(2)}) copy-start(s32[64,4]{0,1:T(4,128)} %convert_reduce_fusion.5) | copy-start | bytes 3076
  103.0 3.6 %copy-start.9 = (bf16[16,4,48]{0,2,1:T(8,128)(2,1)S(1)}, bf16[16,4,48]{0,2,1:T(8,128)(2,1)}, u32[]{:S(2)}) copy-start(bf16[16,4,48]{0,2,1:T(8,128)(2,1)} %select_reduce_fusion.2) | copy-start | bytes 18436
  103.0 3.6 %copy-start.17 = (s32[1024,4]{0,1:T(4,128)S(1)}, s32[1024,4]{0,1:T(4,128)}, u32[]{:S(2)}) copy-start(s32[1024,4]{0,1:T(4,128)} %get-tuple-element.53) | copy-start | bytes 49156
  103.0 3.6 %copy-start.24 = (s32[16,4]{0,1:T(4,128)S(1)}, s32[16,4]{0,1:T(4,128)}, u32[]{:S(2)}) copy-start(s32[16,4]{0,1:T(4,128)} %convert_reduce_fusion.6) | copy-start | bytes 772
  106.6 6.3 %copy-start.7 = (bf16[192,1024]{1,0:T(8,128)(2,1)S(1)}, bf16[192,1024]{1,0:T(8,128)(2,1)}, u32[]{:S(2)}) copy-start(bf16[192,1024]{1,0:T(8,128)(2,1)} %param.8) | copy-start | bytes 1179652
  106.6 6.3 %copy-start.8 = (f32[1024,4,48]{0,2,1:T(8,128)S(1)}, f32[1024,4,48]{0,2,1:T(8,128)}, u32[]{:S(2)}) copy-start(f32[1024,4,48]{0,2,1:T(8,128)} %copy.264) | copy-start | bytes 2359300
  106.9 1.1 copy-start.19
  112.9 10.9 %copy-start.10 = (f32[1024,4]{0,1:T(4,128)}, f32[1024,4]{0,1:T(4,128)S(1)}, u32[]{:S(2)}) copy-start(f32[1024,4]{0,1:T(4,128)S(1)} %get-tuple-element.56) | copy-start | bytes 49156
  112.9 10.8 %copy-start.11 = (f32[1024,4]{0,1:T(4,128)}, f32[1024,4]{0,1:T(4,128)S(1)}, u32[]{:S(2)}) copy-start(f32[1024,4]{0,1:T(4,128)S(1)} %get-tuple-element.57) | copy-start | bytes 49156
  112.9 10.8 %copy-start.12 = (f32[1024,4]{0,1:T(4,128)}, f32[1024,4]{0,1:T(4,128)S(1)}, u32[]{:S(2)}) copy-start(f32[1024,4]{0,1:T(4,128)S(1)} %get-tuple-element.58) | copy-start | bytes 49156
  112.9 10.8 %copy-start.13 = (f32[1024,4]{0,1:T(4,128)}, f32[1024,4]{0,1:T(4,128)S(1)}, u32[]{:S(2)}) copy-start(f32[1024,4]{0,1:T(4,128)S(1)} %get-tuple-element.59) | copy-start | bytes 49156
  112.9 10.8 %copy-start.14 = (f32[1024,4]{0,1:T(4,128)}, f32[1024,4]{0,1:T(4,128)S(1)}, u32[]{:S(2)}) copy-start(f32[1024,4]{0,1:T(4,128)S(1)} %get-tuple-element.60) | copy-start | bytes 49156
  112.9 10.8 %copy-start.15 = (f32[1024,4]{0,1:T(4,128)}, f32[1024,4]{0,1:T(4,128)S(1)}, u32[]{:S(2)}) copy-start(f32[1024,4]{0,1:T(4,128)S(1)} %get-tuple-element.61) | copy-start | bytes 49156
  113.0 21.8 %copy-start.2 = (f32[1024,192]{0,1:T(8,128)S(1)}, f32[1024,192]{0,1:T(8,128)}, u32[]{:S(2)}) copy-start(f32[1024,192]{0,1:T(8,128)} %copy.247) | copy-start | bytes 2359300
  113.0 21.8 %copy-start.3 = (f32[1024,192]{0,1:T(8,128)S(1)}, f32[1024,192]{0,1:T(8,128)}, u32[]{:S(2)}) copy-start(f32[1024,192]{0,1:T(8,128)} %copy.256) | copy-start | bytes 2359300
where the time goes:
time: 139 us; the launch traced here: 137 us
  other arithmetic  38.8 us (28%)
  local copies, waits for them, and re-layouts  35.4 us (25%)
  starting transfers between devices  21.4 us (15%)
  matrix products  19.8 us (14%)
  blocking collectives  11 us (8%)
  waiting for transfers between devices  10.2 us (7%)
    ppermute x12, starting transfers between devices, partner_2(): return lax.ppermute(value, axis, pairs)  21.4 us
    broadcast_in_dim x31, local copies, waits for them, and re-layouts, spread(): full = jnp.where(widened[None], compact[:, None], filler)  18.3 us
    dot_general x4, matrix products, attend(): jnp.einsum('hnk,khd->nhd', probabilities.astype(jnp.bfloat16), value_rows...  13.2 us
    psum x1, blocking collectives, per_device(): lax.psum((jnp.sum(attended, axis=1), jnp.sum(attended * attended, axis=1)...  11 us
    ppermute x12, waiting for transfers between devices, partner_2(): return lax.ppermute(value, axis, pairs)  10.2 us
    reduce_sum x4, other arithmetic, attend(): totals = jnp.sum(probabilities, axis=-1)  9.43 us
    reduce_sum x6, other arithmetic, pick_rows(): jnp.sum(jnp.where(chosen[:, :, None], split, jnp.zeros((), shaped.dtype))...  8.34 us
    select_n x12, other arithmetic, collect(): jnp.where(is_upper, jnp.concatenate([partner, flat_pairs], axis=1), jnp.c...  7.95 us
  transfers between devices with their start and end apart: 12, of which 3 were waited for; matrix products, arithmetic and copies ran while one was open for 47% of the time, Pallas kernels for 0%

commit v1 on v0

v1 whole, which is shorter than its diff:
```python
import math

import jax
import jax.numpy as jnp
import numpy as np
from jax import lax
from jax.sharding import Mesh
from jax.sharding import PartitionSpec as P

D = 768
HD = 48
SEG = 1024
SEQ_AXES = ("zh", "zl", "xh", "xl", "c")


def to_digit_order(x):
    lead = x.shape[:-1]
    x = x.reshape(lead + (16, 4, 4, 4))
    n = len(lead)
    x = jnp.transpose(x, tuple(range(n)) + (n + 3, n + 2, n + 1, n))
    return x.reshape(lead + (1024,))


def from_digit_order(x):
    lead = x.shape[:-1]
    x = x.reshape(lead + (4, 4, 4, 16))
    n = len(lead)
    x = jnp.transpose(x, tuple(range(n)) + (n + 3, n + 2, n + 1, n))
    return x.reshape(lead + (1024,))


def slide_of(positions, slide_ends):
    return jnp.sum((positions[..., None] >= slide_ends).astype(jnp.int32), axis=-1)


def attend(q, k, v, q_slide, k_slide):
    scale = 1.0 / math.sqrt(HD)
    s = jnp.einsum("hdq,hdk->hqk", q, k, preferred_element_type=jnp.float32) * scale
    s = jnp.where(q_slide[:, :, None] == k_slide[:, None, :], s, -1e30)
    m = jnp.max(s, axis=-1)
    p = jnp.exp(s - m[..., None])
    l = jnp.sum(p, axis=-1)
    o = jnp.einsum("hqk,hdk->hdq", p.astype(jnp.bfloat16), v, preferred_element_type=jnp.float32)
    return m, l, o


def merge(a, b):
    ma, la, oa = a
    mb, lb, ob = b
    mn = jnp.maximum(ma, mb)
    ea = jnp.exp(ma - mn)
    eb = jnp.exp(mb - mn)
    return mn, la * ea + lb * eb, oa * ea[:, None, :] + ob * eb[:, None, :]


def per_device(queries, keys, values, slide_lengths, norm_gain, norm_bias):
    heads = queries.shape[0] // HD
    seq = lax.axis_index(SEQ_AXES)
    hy = lax.axis_index("head")
    slide_ends = jnp.cumsum(slide_lengths)
    q = to_digit_order(queries).reshape(heads, HD, 1024)
    k = to_digit_order(keys).reshape(heads, HD, 1024)
    v = to_digit_order(values).reshape(heads, HD, 1024)
    local_pos = to_digit_order(jnp.arange(1024, dtype=jnp.int32))

    def pos_of(device, index):
        return device * 1024 + local_pos[index]

    base0 = pos_of(seq, jnp.arange(1024))
    slide0 = slide_of(base0, slide_ends)
    r0 = attend(q, k, v, jnp.broadcast_to(slide0, (heads, 1024)), jnp.broadcast_to(slide0, (heads, 1024)))

    results = []
    for branch, (count, axes) in enumerate(
        [(256, ("xl", "c")), (64, ("zl", "xh", "xl", "c")), (16, SEQ_AXES)], start=1
    ):
        group = 1024 // count
        starts = [j * 256 + (hy * 64 if branch >= 2 else 0) for j in range(heads)]
        qs = jnp.stack([lax.dynamic_slice_in_dim(q[j], starts[j], count, 1) for j in range(heads)])
        ks = jnp.stack([lax.dynamic_slice_in_dim(k[j], starts[j], count, 1) for j in range(heads)])
        vs = jnp.stack([lax.dynamic_slice_in_dim(v[j], starts[j], count, 1) for j in range(heads)])
        kv = lax.all_gather(jnp.stack([ks, vs]), axes, axis=3, tiled=True)
        idx = jnp.stack([starts[j] + jnp.arange(count) for j in range(heads)])
        q_slide = slide_of(pos_of(seq, idx), slide_ends)
        first = seq // group * group
        members = first + jnp.arange(group)
        k_pos = pos_of(members[None, :, None], idx[:, None, :]).reshape(heads, 1024)
        k_slide = slide_of(k_pos, slide_ends)
        results.append((attend(qs, kv[0], kv[1], q_slide, k_slide), starts, count))

    (r3, _, _), (r2, _, _), (r1, _, _) = results[2], results[1], results[0]
    head2 = tuple(x[..., :16] for x in r2)
    m23 = merge(head2, r3)
    r2 = tuple(jnp.concatenate([a, b[..., 16:]], axis=-1) for a, b in zip(m23, r2))
    mid1 = tuple(lax.dynamic_slice_in_dim(x, hy * 64, 64, x.ndim - 1) for x in r1)
    m12 = merge(mid1, r2)
    r1 = tuple(lax.dynamic_update_slice_in_dim(x, y, hy * 64, x.ndim - 1) for x, y in zip(r1, m12))
    blocks0 = tuple(x.reshape(x.shape[:-1] + (4, 256)) for x in r0)
    out_m, out_l, out_o = [], [], []
    for j in range(heads):
        parts = []
        for blk in range(4):
            cur = (blocks0[0][j : j + 1, blk], blocks0[1][j : j + 1, blk], blocks0[2][j : j + 1, :, blk])
            if blk == j:
                cur = merge(cur, (r1[0][j : j + 1], r1[1][j : j + 1], r1[2][j : j + 1]))
            parts.append(cur)
        out_l.append(jnp.concatenate([p_[1] for p_ in parts], axis=-1))
        out_o.append(jnp.concatenate([p_[2] for p_ in parts], axis=-1))
    total = jnp.concatenate(out_l, axis=0)
    part = jnp.concatenate(out_o, axis=0)
    attended = (part / total[:, None, :]).reshape(heads * HD, 1024)
    sums = lax.psum(
        jnp.stack([jnp.sum(attended, axis=0), jnp.sum(attended * attended, axis=0)]), "head"
    )
    mean = sums[0] / D
    var = sums[1] / D - mean * mean
    normed = (attended - mean[None, :]) * lax.rsqrt(var + 1e-05)[None, :]
    out = (normed * norm_gain[:, None] + norm_bias[:, None]).astype(jnp.bfloat16)
    return from_digit_order(out)


def solution(mesh):
    devices = np.asarray(mesh.devices).reshape(4, 2, 2, 2, 2, mesh.devices.shape[1])
    fine = Mesh(devices, SEQ_AXES + ("head",))
    placed = (P("head", SEQ_AXES),) * 3 + (P(), P("head"), P("head"))
    return jax.shard_map(
        per_device, mesh=fine, in_specs=placed, out_specs=P("head", SEQ_AXES), check_vma=False
    )
```

time: 139 us -> 198 us (1.42)
  blocking collectives: 11 us -> 97.4 us
  local copies, waits for them, and re-layouts: 35.4 us -> 68.2 us
  other arithmetic: 38.8 us -> 10.1 us
  starting transfers between devices: 21.4 us -> 0 us
  waiting for transfers between devices: 10.2 us -> 0 us
    all_gather x0 -> x3, blocking collectives: none -> 85.9 us  [per_device(): kv = lax.all_gather(jnp.stack([ks, vs]), axes, axis=3, tiled=True)]
    ppermute x12 -> x0, starting transfers between devices: 21.4 us -> none  [partner_2(): return lax.ppermute(value, axis, pairs)]
    broadcast_in_dim x31 -> x0, local copies, waits for them, and re-layouts: 18.3 us -> none  [spread(): full = jnp.where(widened[None], compact[:, None], filler)]
    gather x0 -> x7, local copies, waits for them, and re-layouts: none -> 17.8 us  [pos_of(): return device * 1024 + local_pos[index]]
    unnamed x70 -> x59, local copies, waits for them, and re-layouts: 2.57 us -> 16.2 us
    dynamic_slice x0 -> x32, local copies, waits for them, and re-layouts: none -> 11.3 us  [the longest x12 3.78 us: per_device(): lax.dynamic_slice_in_dim(v[j], starts[j], count, 1)]
    reduce_sum x10 -> x5, other arithmetic: 17.8 us -> 7.57 us  [the longest x4 7.41 us: attend(): l = jnp.sum(p, axis=-1)]
    ppermute x12 -> x0, waiting for transfers between devices: 10.2 us -> none  [partner_2(): return lax.ppermute(value, axis, pairs)]
  transfers between devices with their start and end apart: 12 -> 0, of which waited for: 3 -> 0; matrix products, arithmetic and copies ran while one was open for 47% -> 0% of each run, Pallas kernels for 0% -> 0%
where the time goes in v1:
time: 198 us; the launch traced here: 196 us
  blocking collectives  97.4 us (49%)
  local copies, waits for them, and re-layouts  68.2 us (34%)
  matrix products  19.6 us (10%)
  other arithmetic  10.1 us (5%)
    all_gather x3, blocking collectives, per_device(): kv = lax.all_gather(jnp.stack([ks, vs]), axes, axis=3, tiled=True)  85.9 us
    gather x7, local copies, waits for them, and re-layouts, pos_of(): return device * 1024 + local_pos[index]  17.8 us
    unnamed x59, local copies, waits for them, and re-layouts  16.2 us
    dot_general x4, matrix products, attend(): jnp.einsum('hqk,hdk->hdq', p.astype(jnp.bfloat16), v, preferred_element_t...  12 us
    psum x1, blocking collectives, per_device(): lax.psum(jnp.stack([jnp.sum(attended, axis=0), jnp.sum(attended * attende...  11.5 us
    dot_general x4, matrix products, attend(): jnp.einsum('hdq,hdk->hqk', q, k, preferred_element_type=jnp.float32) * scale  7.55 us
    reduce_sum x4, other arithmetic, attend(): l = jnp.sum(p, axis=-1)  7.41 us

profile of v1, /device:TPU:4, one launch (start us, length us, event | category | flops | bytes accessed | tf_op | source)
XLA Modules:
  0.0 196.4 jit_solution(15239477995717562915)
XLA Ops:
  0.0 1.2 copy.245
  6.5 24.2 %all_gather.10 = bf16[2,4,48,1024]{2,1,0,3:T(4,128)(2,1)S(1)} all-gather(bf16[2,4,48,64]{2,1,0,3:T(4,128)(2,1)S(1)} %copy.290), channel_id=1, replica_groups=mesh['zh'=4,'zl'=2,'xh'=2,'xl'=2,'c'=2,'head'=4] {'zl','xh','xl','c'}, dimensions={3}, use_global_device_ids=true | all-gather | bytes 835584 | tf_op jit(solution)/shard_map/all_gather | solution.py:82
  30.7 1.7 fusion.142
  33.3 4.5 %gather_fusion.2 = s32[1024]{0:T(1024)S(1)} fusion(s32[1024]{0:T(1024)S(1)} %reshape.1167, s32[1024]{0:T(1024)S(1)} %broadcast_clamp_fusion), kind=kCustom, calls=%fused_computation.2 | custom fusion | bytes 12288 | tf_op jit(solution)/shard_map/gather | solution.py:67
  38.2 1.4 gather_fusion.4
  40.1 0.7 gather_fusion.6
  42.0 1.4 gather_fusion.3
  44.9 0.7 copy-done.9
  47.6 1.6 copy.332
  49.6 0.7 fusion.75
  50.3 0.7 fusion.73
  51.0 0.7 fusion.66
  51.6 0.7 fusion.68
  52.3 0.7 fusion.67
  53.0 0.7 fusion.65
  53.8 53.0 %all_gather.11 = bf16[2,4,48,1024]{2,1,0,3:T(4,128)(2,1)S(1)} all-gather(bf16[2,4,48,16]{2,1,0,3:T(4,128)(2,1)S(1)} %copy.292), channel_id=1, replica_groups=mesh['zh'=4,'zl'=2,'xh'=2,'xl'=2,'c'=2,'head'=4] {'zh','zl','xh','xl','c'}, dimensions={3}, use_global_device_ids=true | all-gather | bytes 798720 | tf_op jit(solution)/shard_map/all_gather | solution.py:82
  106.8 2.1 %fusion.141 = (bf16[1,4,48,1024]{2,1,0,3:T(4,128)(2,1)}, bf16[1,4,48,1024]{2,1,0,3:T(4,128)(2,1)}) fusion(bf16[2,4,48,1024]{2,1,0,3:T(4,128)(2,1)S(1)} %all_gather.11), kind=kLoop, calls=%fused_computation.293 | loop fusion | bytes 1572864 | tf_op jit(solution)/shard_map/slice | solution.py:89
  108.9 1.6 copy.331
  110.6 0.7 gather_fusion.5
  112.5 1.6 copy.333
  114.6 0.8 dynamic_slice.160
  115.6 0.8 dynamic_slice.161
  116.5 0.8 dynamic_slice.162
  117.4 0.8 dynamic_slice.163
  118.4 0.8 dynamic_slice.164
  119.3 0.8 dynamic_slice.165
  120.2 0.8 dynamic_slice.166
  121.2 0.8 dynamic_slice.167
  122.2 8.7 %all_gather.9 = bf16[2,4,48,1024]{3,2,1,0:T(8,128)(2,1)S(1)} all-gather(bf16[2,4,48,256]{3,2,1,0:T(8,128)(2,1)S(1)} %pad_maximum_fusion), channel_id=1, replica_groups=mesh['zh'=4,'zl'=2,'xh'=2,'xl'=2,'c'=2,'head'=4] {'xl','c'}, dimensions={3}, use_global_device_ids=true | all-gather | bytes 983040 | tf_op jit(solution)/shard_map/all_gather | solution.py:82
  131.0 4.5 %gather_fusion.1 = s32[1024]{0:T(1024)S(1)} fusion(s32[1024]{0:T(1024)S(1)} %reshape.1167, s32[1024]{0:T(1024)S(1)} %broadcast_clamp_fusion.1), kind=kCustom, calls=%fused_computation.1 | custom fusion | bytes 12288 | tf_op jit(solution)/shard_map/gather | solution.py:67
  135.6 0.8 dynamic_slice.156
  136.6 0.8 dynamic_slice.157
  137.5 0.8 dynamic_slice.158
  138.4 0.8 dynamic_slice.159
  139.4 2.8 %fusion.7 = (f32[4,256]{1,0:T(4,128)S(1)}, f32[4,256,1024]{2,1,0:T(8,128)}) fusion(s32[4,1024]{1,0:T(4,128)S(1)} %get-tuple-element.11, s32[4,256]{1,0:T(4,128)S(1)} %convert_reduce_fusion.3, bf16[2,4,48,1024]{3,2,1,0:T(8,128)(2,1)S(1)} %all_gather.9, bf16[1,48,256]{2,1,0:T(8,128)(2,1)S(1)} %bitcast.382, bf16[1,48,256]{2,1,0:T(8,128)(2,1)S(1)} %bitcast.381, ...), kind=kOutput, calls=%fused_computation.17 | convolution fusion | flops 105004032 | bytes 4710400 | tf_op jit(solution)/shard_map/hdq,hdk->hqk/dot_general | solution.py:38
  142.2 2.9 %fusion.5 = f32[4,256]{1,0:T(4,128)S(1)} fusion(f32[4,256,1024]{2,1,0:T(8,128)} %get-tuple-element.91, f32[4,256]{1,0:T(4,128)S(1)} %get-tuple-element.90, s32[4,1024]{1,0:T(4,128)S(1)} %get-tuple-element.11, s32[4,256]{1,0:T(4,128)S(1)} %convert_reduce_fusion.3), kind=kLoop, calls=%fused_computation.15 | loop fusion | flops 5241856 | bytes 4222976 | tf_op jit(solution)/shard_map/reduce_sum | solution.py:42
  145.2 3.0 %fusion.8 = f32[4,48,256]{2,1,0:T(8,128)S(1)} fusion(f32[4,256,1024]{2,1,0:T(8,128)} %get-tuple-element.91, f32[4,256]{1,0:T(4,128)S(1)} %get-tuple-element.90, s32[4,1024]{1,0:T(4,128)S(1)} %get-tuple-element.11, s32[4,256]{1,0:T(4,128)S(1)} %convert_reduce_fusion.3, bf16[2,4,48,1024]{3,2,1,0:T(8,128)(2,1)S(1)} %all_gather.9), kind=kOutput, calls=%fused_computation.18 | convolution fusion | flops 105906176 | bytes 4808704 | tf_op jit(solution)/shard_map/hqk,hdk->hdq/dot_general | solution.py:43
  149.2 4.5 %gather_fusion = s32[1024]{0:T(1024)S(1)} fusion(s32[1024]{0:T(1024)S(1)} %reshape.1167, s32[1024]{0:T(1024)S(1)} %iota_clamp_fusion), kind=kCustom, calls=%fused_computation | custom fusion | bytes 12288 | tf_op jit(solution)/shard_map/gather | solution.py:67
  154.1 1.5 reshape_reshape.10
  156.4 4.0 %fusion.2 = (f32[4,1024]{1,0:T(4,128)S(1)}, f32[4,1024,1024]{1,2,0:T(8,128)S(1)}) fusion(s32[1024]{0:T(1024)S(1)} %convert_reduce_fusion.4, bf16[4,48,1024]{1,0,2:T(4,128)(2,1)} %reshape_reshape.10, bf16[4,48,1024]{1,0,2:T(4,128)(2,1)S(1)} %reshape_reshape.9), kind=kOutput, calls=%fused_computation.11 | convolution fusion | flops 419426304 | bytes 17584128 | tf_op jit(solution)/shard_map/hdq,hdk->hqk/dot_general | solution.py:38
  160.5 5.7 %copy-done = f32[4,1024,1024]{1,2,0:T(8,128)} copy-done((f32[4,1024,1024]{1,2,0:T(8,128)}, f32[4,1024,1024]{1,2,0:T(8,128)S(1)}, u32[]{:S(2)}) %copy-start) | copy-done | bytes 16777240
  166.2 4.0 %fusion = f32[4,1024]{1,0:T(4,128)S(1)} fusion(f32[4,1024,1024]{1,2,0:T(8,128)S(1)} %get-tuple-element.97, f32[4,1024]{1,0:T(4,128)S(1)} %get-tuple-element.96, s32[1024]{0:T(1024)S(1)} %convert_reduce_fusion.4), kind=kLoop, calls=%fused_computation.9 | loop fusion | flops 20967424 | bytes 16814080 | tf_op jit(solution)/shard_map/reduce_sum | solution.py:42
  171.1 8.3 %fusion.11 = f32[4,48,1024]{2,1,0:T(8,128)S(1)} fusion(f32[4,1024,1024]{1,2,0:T(8,128)} %copy-done, f32[4,1024]{1,0:T(4,128)S(1)} %get-tuple-element.96, s32[1024]{0:T(1024)S(1)} %convert_reduce_fusion.4, bf16[4,48,1024]{1,0,2:T(4,128)(2,1)S(1)} %reshape_reshape.11), kind=kOutput, calls=%fused_computation.21 | convolution fusion | flops 423624704 | bytes 17977344 | tf_op jit(solution)/shard_map/hqk,hdk->hdq/dot_general | solution.py:43
  179.8 0.7 fusion.143
  180.9 11.5 %psum.7 = f32[2,1024]{1,0:T(2,128)S(1)} all-reduce(f32[2,1024]{1,0:T(2,128)S(1)} %pad_maximum_fusion.3), channel_id=1, replica_groups=mesh['zh'=4,'zl'=2,'xh'=2,'xl'=2,'c'=2,'head'=4] {'head'}, use_global_device_ids=true, to_apply=%region_18.19 | all-reduce | flops 2048 | bytes 16384 | tf_op jit(solution)/shard_map/psum | solution.py:112
  192.6 0.9 copy.312
  193.5 0.9 div.54
  195.5 0.9 copy.314
  (207 shorter events, 19.7 us)
Async XLA Ops:
  0.0 2.2 %copy-start.13 = (bf16[192,1024]{1,0:T(8,128)(2,1)S(1)}, bf16[192,1024]{1,0:T(8,128)(2,1)}, u32[]{:S(2)}) copy-start(bf16[192,1024]{1,0:T(8,128)(2,1)} %param.8) | copy-start | bytes 1179652
  2.1 4.2 %copy-start.5 = (bf16[48,4,4,4,16]{0,4,3,2,1:T(8,128)(2,1)}, bf16[48,4,4,4,16]{0,4,3,2,1:T(8,128)(2,1)S(1)}, u32[]{:S(2)}) copy-start(bf16[48,4,4,4,16]{0,4,3,2,1:T(8,128)(2,1)S(1)} %copy.264) | copy-start | bytes 294916
  3.3 47.0 %copy-start.1 = (bf16[48,4,4,4,16]{0,4,3,2,1:T(8,128)(2,1)}, bf16[48,4,4,4,16]{0,4,3,2,1:T(8,128)(2,1)S(1)}, u32[]{:S(2)}) copy-start(bf16[48,4,4,4,16]{0,4,3,2,1:T(8,128)(2,1)S(1)} %copy.272) | copy-start | bytes 294916
  3.6 0.7 copy-start.6
  3.8 28.6 %copy-start.2 = (bf16[48,4,4,4,16]{0,4,3,2,1:T(8,128)(2,1)}, bf16[48,4,4,4,16]{0,4,3,2,1:T(8,128)(2,1)S(1)}, u32[]{:S(2)}) copy-start(bf16[48,4,4,4,16]{0,4,3,2,1:T(8,128)(2,1)S(1)} %copy.274) | copy-start | bytes 294916
  4.6 0.7 copy-start.7
  4.8 1.7 copy-start.3
  5.6 27.4 %copy-start.8 = (bf16[48,4,4,4,16]{0,4,3,2,1:T(8,128)(2,1)}, bf16[48,4,4,4,16]{0,4,3,2,1:T(8,128)(2,1)S(1)}, u32[]{:S(2)}) copy-start(bf16[48,4,4,4,16]{0,4,3,2,1:T(8,128)(2,1)S(1)} %copy.262) | copy-start | bytes 294916
  5.8 0.7 copy-start.4
  33.3 7.8 %copy-start.17 = (s32[64]{0:T(128)S(1)}, s32[64]{0:T(128)}, u32[]{:S(2)}) copy-start(s32[64]{0:T(128)} %param.9) | copy-start | bytes 772
  37.9 5.9 %copy-start.14 = (bf16[192,1024]{1,0:T(8,128)(2,1)S(1)}, bf16[192,1024]{1,0:T(8,128)(2,1)}, u32[]{:S(2)}) copy-start(bf16[192,1024]{1,0:T(8,128)(2,1)} %param.6) | copy-start | bytes 1179652
  44.9 0.7 copy-start.9
  45.9 0.7 copy-start.10
  46.2 0.7 copy-start.11
  46.5 0.7 copy-start.12
  160.5 5.7 %copy-start = (f32[4,1024,1024]{1,2,0:T(8,128)}, f32[4,1024,1024]{1,2,0:T(8,128)S(1)}, u32[]{:S(2)}) copy-start(f32[4,1024,1024]{1,2,0:T(8,128)S(1)} %get-tuple-element.97) | copy-start | bytes 50331652
  180.6 13.7 %copy-start.15 = (f32[192]{0:T(256)S(1)}, f32[192]{0:T(256)}, u32[]{:S(2)}) copy-start(f32[192]{0:T(256)} %param.11) | copy-start | bytes 2308
  180.7 13.7 %copy-start.16 = (f32[192]{0:T(256)S(1)}, f32[192]{0:T(256)}, u32[]{:S(2)}) copy-start(f32[192]{0:T(256)} %param.10) | copy-start | bytes 2308

commit v2 on v1

--- a/solution.py
+++ b/solution.py
@@ -44,6 +44,26 @@
     return m, l, o
 
 
+def collect(block, group, seq):
+    for bit in range(group.bit_length() - 1):
+        mask = 2**bit
+        pairs = [(i, i ^ mask) for i in range(64)]
+        partner = lax.ppermute(block, SEQ_AXES, pairs)
+        upper = seq // mask % 2 == 1
+        block = jnp.where(
+            upper,
+            jnp.concatenate([partner, block], axis=-1),
+            jnp.concatenate([block, partner], axis=-1),
+        )
+    return block
+
+
+def head_sum(x):
+    for mask in (1, 2):
+        x = x + lax.ppermute(x, "head", [(i, i ^ mask) for i in range(4)])
+    return x
+
+
 def merge(a, b):
     ma, la, oa = a
     mb, lb, ob = b
@@ -61,10 +81,10 @@
     q = to_digit_order(queries).reshape(heads, HD, 1024)
     k = to_digit_order(keys).reshape(heads, HD, 1024)
     v = to_digit_order(values).reshape(heads, HD, 1024)
-    local_pos = to_digit_order(jnp.arange(1024, dtype=jnp.int32))
 
     def pos_of(device, index):
-        return device * 1024 + local_pos[index]
+        local = 64 * (index % 16) + 16 * (index // 16 % 4) + 4 * (index // 64 % 4) + index // 256
+        return device * 1024 + local
 
     base0 = pos_of(seq, jnp.arange(1024))
     slide0 = slide_of(base0, slide_ends)
@@ -79,7 +99,7 @@
         qs = jnp.stack([lax.dynamic_slice_in_dim(q[j], starts[j], count, 1) for j in range(heads)])
         ks = jnp.stack([lax.dynamic_slice_in_dim(k[j], starts[j], count, 1) for j in range(heads)])
         vs = jnp.stack([lax.dynamic_slice_in_dim(v[j], starts[j], count, 1) for j in range(heads)])
-        kv = lax.all_gather(jnp.stack([ks, vs]), axes, axis=3, tiled=True)
+        kv = collect(jnp.stack([ks, vs]), group, seq)
         idx = jnp.stack([starts[j] + jnp.arange(count) for j in range(heads)])
         q_slide = slide_of(pos_of(seq, idx), slide_ends)
         first = seq // group * group
@@ -109,9 +129,7 @@
     total = jnp.concatenate(out_l, axis=0)
     part = jnp.concatenate(out_o, axis=0)
     attended = (part / total[:, None, :]).reshape(heads * HD, 1024)
-    sums = lax.psum(
-        jnp.stack([jnp.sum(attended, axis=0), jnp.sum(attended * attended, axis=0)]), "head"
-    )
+    sums = head_sum(jnp.stack([jnp.sum(attended, axis=0), jnp.sum(attended * attended, axis=0)]))
     mean = sums[0] / D
     var = sums[1] / D - mean * mean
     normed = (attended - mean[None, :]) * lax.rsqrt(var + 1e-05)[None, :]

time: 198 us -> 130 us (0.66)
  the two profiles are of different devices: /device:TPU:4 before, /device:TPU:42 now
where the time goes in v2:
time: 130 us; the launch traced here: 129 us
  local copies, waits for them, and re-layouts  40.5 us (31%)
  waiting for transfers between devices  30.8 us (24%)
  starting transfers between devices  20.6 us (16%)
  other arithmetic  19.7 us (15%)
  matrix products  16.4 us (13%)
    ppermute x12, waiting for transfers between devices, collect(): partner = lax.ppermute(block, SEQ_AXES, pairs)  25.9 us
    ppermute x12, starting transfers between devices, collect(): partner = lax.ppermute(block, SEQ_AXES, pairs)  18.3 us
    unnamed x63, local copies, waits for them, and re-layouts  10.8 us
    dot_general x4, matrix products, attend(): jnp.einsum('hqk,hdk->hdq', p.astype(jnp.bfloat16), v, preferred_element_t...  10.6 us
    dynamic_slice x12, local copies, waits for them, and re-layouts, per_device(): lax.dynamic_slice_in_dim(q[j], starts[j], count, 1)  6.43 us
    reduce_sum x4, other arithmetic, attend(): l = jnp.sum(p, axis=-1)  5.86 us
    dot_general x4, matrix products, attend(): jnp.einsum('hdq,hdk->hqk', q, k, preferred_element_type=jnp.float32) * scale  5.76 us
    ppermute x2, waiting for transfers between devices, head_sum(): x = x + lax.ppermute(x, 'head', [(i, i ^ mask) for i in range(4)])  4.9 us
  transfers between devices with their start and end apart: 14, of which 8 were waited for; matrix products, arithmetic and copies ran while one was open for 45% of the time, Pallas kernels for 0%

profile of v2, /device:TPU:42, one launch (start us, length us, event | category | flops | bytes accessed | tf_op | source)
XLA Modules:
  0.0 129.1 jit_solution(75259716124346234)
XLA Ops:
  0.0 1.2 copy.178
  4.4 0.9 copy.195
  5.4 0.7 constant_dynamic-slice_fusion.16
  7.4 0.7 fusion.89
  8.8 0.8 dynamic_slice.160
  10.5 0.7 pad_maximum_fusion
  13.9 1.2 copy.176
  18.0 0.7 broadcast_add_fusion.3
  20.1 0.7 broadcast_add_fusion.4
  20.9 0.7 add.1132
  21.6 0.7 copy.175
  25.1 0.9 copy.187
  26.0 0.8 convert_reduce_fusion.5
  26.8 0.8 convert_reduce_fusion.6
  28.9 1.5 %reshape_reshape.9 = bf16[4,48,1024]{1,0,2:T(4,128)(2,1)} reshape(bf16[192,4,4,4,16]{0,4,3,2,1:T(8,128)(2,1)S(1)} %copy.177) | data formatting | bytes 786432 | tf_op jit(solution)/shard_map/reshape;reshape | solution.py:81
  30.4 4.0 %fusion.2 = (f32[4,1024]{1,0:T(4,128)S(1)}, f32[4,1024,1024]{1,2,0:T(8,128)S(1)}) fusion(s32[1024]{0:T(1024)S(1)} %convert_reduce_fusion.4, bf16[4,48,1024]{1,0,2:T(4,128)(2,1)S(1)} %reshape_reshape.10, bf16[4,48,1024]{1,0,2:T(4,128)(2,1)} %reshape_reshape.9), kind=kOutput, calls=%fused_computation.4 | convolution fusion | flops 419426304 | bytes 17584128 | tf_op jit(solution)/shard_map/hdq,hdk->hqk/dot_general | solution.py:38
  34.5 5.7 %copy-done = f32[4,1024,1024]{1,2,0:T(8,128)} copy-done((f32[4,1024,1024]{1,2,0:T(8,128)}, f32[4,1024,1024]{1,2,0:T(8,128)S(1)}, u32[]{:S(2)}) %copy-start) | copy-done | bytes 16777240
  40.2 4.0 %fusion = f32[4,1024]{1,0:T(4,128)S(1)} fusion(f32[4,1024,1024]{1,2,0:T(8,128)S(1)} %get-tuple-element.99, f32[4,1024]{1,0:T(4,128)S(1)} %get-tuple-element.98, s32[1024]{0:T(1024)S(1)} %convert_reduce_fusion.4), kind=kLoop, calls=%fused_computation.2 | loop fusion | flops 20967424 | bytes 16814080 | tf_op jit(solution)/shard_map/reduce_sum | solution.py:42
  44.9 8.1 %fusion.11 = f32[4,48,1024]{2,1,0:T(8,128)S(1)} fusion(f32[4,1024,1024]{1,2,0:T(8,128)} %copy-done, f32[4,1024]{1,0:T(4,128)S(1)} %get-tuple-element.98, s32[1024]{0:T(1024)S(1)} %convert_reduce_fusion.4, bf16[4,48,1024]{1,0,2:T(4,128)(2,1)S(1)} %reshape_reshape.11), kind=kOutput, calls=%fused_computation.14 | convolution fusion | flops 423624704 | bytes 17977344 | tf_op jit(solution)/shard_map/hqk,hdk->hdq/dot_general | solution.py:43
  54.8 0.7 constant_dynamic-slice_fusion.24
  55.5 1.1 maximum_select_fusion.9
  57.9 0.8 dynamic_slice.157
  58.8 0.8 dynamic_slice.158
  59.6 0.8 dynamic_slice.159
  60.5 0.8 dynamic_slice.156
  62.3 2.5 %collective-permute-start.8 = (bf16[2,4,48,64]{3,2,1,0:T(8,128)(2,1)S(1)}, bf16[2,4,48,64]{3,2,1,0:T(8,128)(2,1)S(1)}, u32[]{:S(2)}, u32[]{:S(2)}) collective-permute-start(bf16[2,4,48,64]{3,2,1,0:T(8,128)(2,1)S(1)} %maximum_select_fusion.10), channel_id=1, source_target_pairs={{0,16},{4,20},{8,24},{12,28},{16,0},{20,4},{24,8},{28,12},{32,48},... | collective-permute-start | bytes 147464 | tf_op jit(solution)/shard_map/ppermute | solution.py:51
  64.8 1.1 maximum_select_fusion.8
  65.9 1.9 %collective-permute-start.3 = (bf16[2,4,48,128]{3,2,1,0:T(8,128)(2,1)S(1)}, bf16[2,4,48,128]{3,2,1,0:T(8,128)(2,1)S(1)}, u32[]{:S(2)}, u32[]{:S(2)}) collective-permute-start(bf16[2,4,48,128]{3,2,1,0:T(8,128)(2,1)S(1)} %maximum_select_fusion.8), channel_id=1, source_target_pairs={{0,8},{4,12},{8,0},{12,4},{16,24},{20,28},{24,16},{28,20},{32,40},... | collective-permute-start | bytes 294920 | tf_op jit(solution)/shard_map/ppermute | solution.py:51
  67.8 1.3 %collective-permute-done.8 = bf16[2,4,48,64]{3,2,1,0:T(8,128)(2,1)S(1)} collective-permute-done((bf16[2,4,48,64]{3,2,1,0:T(8,128)(2,1)S(1)}, bf16[2,4,48,64]{3,2,1,0:T(8,128)(2,1)S(1)}, u32[]{:S(2)}, u32[]{:S(2)}) %collective-permute-start.8) | collective-permute-done | bytes 49184 | tf_op jit(solution)/shard_map/ppermute | solution.py:51
  69.4 2.2 %collective-permute-done.3 = bf16[2,4,48,128]{3,2,1,0:T(8,128)(2,1)S(1)} collective-permute-done((bf16[2,4,48,128]{3,2,1,0:T(8,128)(2,1)S(1)}, bf16[2,4,48,128]{3,2,1,0:T(8,128)(2,1)S(1)}, u32[]{:S(2)}, u32[]{:S(2)}) %collective-permute-start.3) | collective-permute-done | bytes 98336 | tf_op jit(solution)/shard_map/ppermute | solution.py:51
  71.9 1.1 maximum_select_fusion.3
  73.1 2.4 %collective-permute-start.1 = (bf16[2,4,48,512]{3,2,1,0:T(8,128)(2,1)S(1)}, bf16[2,4,48,512]{3,2,1,0:T(8,128)(2,1)S(1)}, u32[]{:S(2)}, u32[]{:S(2)}) collective-permute-start(bf16[2,4,48,512]{3,2,1,0:T(8,128)(2,1)S(1)} %maximum_select_fusion.3), channel_id=1, source_target_pairs={{0,8},{4,12},{8,0},{12,4},{16,24},{20,28},{24,16},{28,20},{32,40},... | collective-permute-start | bytes 1179656 | tf_op jit(solution)/shard_map/ppermute | solution.py:51
  75.5 3.4 %collective-permute-start.10 = (bf16[2,4,48,256]{3,2,1,0:T(8,128)(2,1)S(1)}, bf16[2,4,48,256]{3,2,1,0:T(8,128)(2,1)S(1)}, u32[]{:S(2)}, u32[]{:S(2)}) collective-permute-start(bf16[2,4,48,256]{3,2,1,0:T(8,128)(2,1)S(1)} %maximum_select_fusion.7), channel_id=1, source_target_pairs={{0,64},{4,68},{8,72},{12,76},{16,80},{20,84},{24,88},{28,92},{32,9... | collective-permute-start | bytes 589832 | tf_op jit(solution)/shard_map/ppermute | solution.py:51
  79.5 1.5 %collective-permute-done.4 = bf16[2,4,48,256]{3,2,1,0:T(8,128)(2,1)S(1)} collective-permute-done((bf16[2,4,48,256]{3,2,1,0:T(8,128)(2,1)S(1)}, bf16[2,4,48,256]{3,2,1,0:T(8,128)(2,1)S(1)}, u32[]{:S(2)}, u32[]{:S(2)}) %collective-permute-start.4) | collective-permute-done | bytes 196640 | tf_op jit(solution)/shard_map/ppermute | solution.py:51
  81.7 3.9 %collective-permute-done.10 = bf16[2,4,48,256]{3,2,1,0:T(8,128)(2,1)S(1)} collective-permute-done((bf16[2,4,48,256]{3,2,1,0:T(8,128)(2,1)S(1)}, bf16[2,4,48,256]{3,2,1,0:T(8,128)(2,1)S(1)}, u32[]{:S(2)}, u32[]{:S(2)}) %collective-permute-start.10) | collective-permute-done | bytes 196640 | tf_op jit(solution)/shard_map/ppermute | solution.py:51
  85.7 6.0 %collective-permute-start.11 = (bf16[2,4,48,512]{3,2,1,0:T(8,128)(2,1)S(1)}, bf16[2,4,48,512]{3,2,1,0:T(8,128)(2,1)S(1)}, u32[]{:S(2)}, u32[]{:S(2)}) collective-permute-start(bf16[2,4,48,512]{3,2,1,0:T(8,128)(2,1)S(1)} %maximum_select_fusion.5), channel_id=1, source_target_pairs={{0,128},{4,132},{8,136},{12,140},{16,144},{20,148},{24,152},{28,15... | collective-permute-start | bytes 1179656 | tf_op jit(solution)/shard_map/ppermute | solution.py:51
  92.0 1.0 fusion.7
  93.0 1.8 %fusion.8 = f32[4,48,256]{2,1,0:T(8,128)S(1)} fusion(f32[4,256,1024]{2,1,0:T(8,128)S(1)} %get-tuple-element.93, f32[4,256]{1,0:T(4,128)S(1)} %get-tuple-element.92, s32[4,1024]{1,0:T(4,128)S(1)} %get-tuple-element.11, s32[4,256]{1,0:T(4,128)S(1)} %copy-done.14, bf16[2,4,48,1024]{3,2,1,0:T(8,128)(2,1)S(1)} %maximum_select_fusion), kind=kOutput, calls=%fused_computation.11 | convolution fusion | flops 105906176 | bytes 4808704 | tf_op jit(solution)/shard_map/hqk,hdk->hdq/dot_general | solution.py:43
  94.8 1.3 %fusion.5 = f32[4,256]{1,0:T(4,128)S(1)} fusion(f32[4,256,1024]{2,1,0:T(8,128)S(1)} %get-tuple-element.93, f32[4,256]{1,0:T(4,128)S(1)} %get-tuple-element.92, s32[4,1024]{1,0:T(4,128)S(1)} %get-tuple-element.11, s32[4,256]{1,0:T(4,128)S(1)} %copy-done.14), kind=kLoop, calls=%fused_computation.8 | loop fusion | flops 5241856 | bytes 4222976 | tf_op jit(solution)/shard_map/reduce_sum | solution.py:42
  96.2 2.3 %collective-permute-done.5 = bf16[2,4,48,512]{3,2,1,0:T(8,128)(2,1)S(1)} collective-permute-done((bf16[2,4,48,512]{3,2,1,0:T(8,128)(2,1)S(1)}, bf16[2,4,48,512]{3,2,1,0:T(8,128)(2,1)S(1)}, u32[]{:S(2)}, u32[]{:S(2)}) %collective-permute-start.5) | collective-permute-done | bytes 393248 | tf_op jit(solution)/shard_map/ppermute | solution.py:51
  100.1 14.6 %collective-permute-done.11 = bf16[2,4,48,512]{3,2,1,0:T(8,128)(2,1)S(1)} collective-permute-done((bf16[2,4,48,512]{3,2,1,0:T(8,128)(2,1)S(1)}, bf16[2,4,48,512]{3,2,1,0:T(8,128)(2,1)S(1)}, u32[]{:S(2)}, u32[]{:S(2)}) %collective-permute-start.11) | collective-permute-done | bytes 393248 | tf_op jit(solution)/shard_map/ppermute | solution.py:51
  116.0 1.1 dynamic_update_slice.10
  118.0 3.6 %collective-permute-done.12 = f32[2,1024]{1,0:T(2,128)S(1)} collective-permute-done((f32[2,1024]{1,0:T(2,128)S(1)}, f32[2,1024]{1,0:T(2,128)S(1)}, u32[]{:S(2)}, u32[]{:S(2)}) %collective-permute-start.12) | collective-permute-done | bytes 8224 | tf_op jit(solution)/shard_map/ppermute | solution.py:63
  121.6 2.2 %collective-permute-start.13 = (f32[2,1024]{1,0:T(2,128)S(1)}, f32[2,1024]{1,0:T(2,128)S(1)}, u32[]{:S(2)}, u32[]{:S(2)}) collective-permute-start(f32[2,1024]{1,0:T(2,128)S(1)} %fusion.154), channel_id=1, source_target_pairs={{0,2},{1,3},{2,0},{3,1},{4,6},{5,7},{6,4},{7,5},{8,10},{9,11},{10,... | collective-permute-start | bytes 24584 | tf_op jit(solution)/shard_map/ppermute | solution.py:63
  123.8 0.9 copy.242
  124.7 0.9 div.275
  125.6 1.3 collective-permute-done.13
  128.2 0.9 copy.244
  (207 shorter events, 28.4 us)
Async XLA Ops:
  0.0 2.2 %copy-start.4 = (bf16[192,1024]{1,0:T(8,128)(2,1)S(1)}, bf16[192,1024]{1,0:T(8,128)(2,1)}, u32[]{:S(2)}) copy-start(bf16[192,1024]{1,0:T(8,128)(2,1)} %param.8) | copy-start | bytes 1179652
  7.4 57.4 %collective-permute-start.2 = (bf16[2,4,48,64]{3,2,1,0:T(8,128)(2,1)}, bf16[2,4,48,64]{3,2,1,0:T(8,128)(2,1)}, u32[]{:S(2)}, u32[]{:S(2)}) collective-permute-start(bf16[2,4,48,64]{3,2,1,0:T(8,128)(2,1)} %pad_maximum_fusion.1), channel_id=1, source_target_pairs={{0,4},{4,0},{8,12},{12,8},{16,20},{20,16},{24,28},{28,24},{32,36},... | collective-permute-start | bytes 147464 | tf_op jit(solution)/shard_map/ppermute | solution.py:51
  8.3 47.3 %collective-permute-start.6 = (bf16[2,4,48,16]{3,2,1,0:T(8,128)(2,1)S(1)}, bf16[2,4,48,16]{3,2,1,0:T(8,128)(2,1)}, u32[]{:S(2)}, u32[]{:S(2)}) collective-permute-start(bf16[2,4,48,16]{3,2,1,0:T(8,128)(2,1)S(1)} %copy.223), channel_id=1, source_target_pairs={{0,4},{4,0},{8,12},{12,8},{16,20},{20,16},{24,28},{28,24},{32,36},... | collective-permute-start | bytes 36872 | tf_op jit(solution)/shard_map/ppermute | solution.py:51
  11.2 60.7 %collective-permute-start = (bf16[2,4,48,256]{3,2,1,0:T(8,128)(2,1)}, bf16[2,4,48,256]{3,2,1,0:T(8,128)(2,1)}, u32[]{:S(2)}, u32[]{:S(2)}) collective-permute-start(bf16[2,4,48,256]{3,2,1,0:T(8,128)(2,1)} %pad_maximum_fusion), channel_id=1, source_target_pairs={{0,4},{4,0},{8,12},{12,8},{16,20},{20,16},{24,28},{28,24},{32,36},... | collective-permute-start | bytes 589832 | tf_op jit(solution)/shard_map/ppermute | solution.py:51
  22.5 12.0 %copy-start.12 = (s32[64]{0:T(128)}, s32[64]{0:T(128)S(1)}, u32[]{:S(2)}) copy-start(s32[64]{0:T(128)S(1)} %reduce.2) | copy-start | bytes 772
  22.7 5.6 %copy-start.1 = (bf16[48,4,4,4,16]{0,4,3,2,1:T(8,128)(2,1)}, bf16[48,4,4,4,16]{0,4,3,2,1:T(8,128)(2,1)S(1)}, u32[]{:S(2)}) copy-start(bf16[48,4,4,4,16]{0,4,3,2,1:T(8,128)(2,1)S(1)} %copy.189) | copy-start | bytes 294916
  23.6 4.7 %copy-start.2 = (bf16[48,4,4,4,16]{0,4,3,2,1:T(8,128)(2,1)}, bf16[48,4,4,4,16]{0,4,3,2,1:T(8,128)(2,1)S(1)}, u32[]{:S(2)}) copy-start(bf16[48,4,4,4,16]{0,4,3,2,1:T(8,128)(2,1)S(1)} %copy.191) | copy-start | bytes 294916
  24.4 3.9 %copy-start.3 = (bf16[48,4,4,4,16]{0,4,3,2,1:T(8,128)(2,1)}, bf16[48,4,4,4,16]{0,4,3,2,1:T(8,128)(2,1)S(1)}, u32[]{:S(2)}) copy-start(bf16[48,4,4,4,16]{0,4,3,2,1:T(8,128)(2,1)S(1)} %copy.193) | copy-start | bytes 294916
  34.5 5.7 %copy-start = (f32[4,1024,1024]{1,2,0:T(8,128)}, f32[4,1024,1024]{1,2,0:T(8,128)S(1)}, u32[]{:S(2)}) copy-start(f32[4,1024,1024]{1,2,0:T(8,128)S(1)} %get-tuple-element.99) | copy-start | bytes 50331652
  34.5 10.3 %copy-start.10 = (f32[4,1024]{1,0:T(4,128)}, f32[4,1024]{1,0:T(4,128)S(1)}, u32[]{:S(2)}) copy-start(f32[4,1024]{1,0:T(4,128)S(1)} %get-tuple-element.98) | copy-start | bytes 49156
  44.8 9.3 %copy-start.15 = (s32[1024]{0:T(1024)S(1)}, s32[1024]{0:T(1024)}, u32[]{:S(2)}) copy-start(s32[1024]{0:T(1024)} %add.1099) | copy-start | bytes 12292
  44.8 9.3 %copy-start.9 = (s32[1,4,4,256]{3,1,2,0:T(4,128)S(1)}, s32[1,4,4,256]{3,1,2,0:T(4,128)}, u32[]{:S(2)}) copy-start(s32[1,4,4,256]{3,1,2,0:T(4,128)} %copy.276) | copy-start | bytes 49156
  44.8 9.3 %copy-start.17 = (s32[1,2,4,128]{3,1,2,0:T(2,128)S(1)}, s32[1,2,4,128]{3,1,2,0:T(2,128)}, u32[]{:S(2)}) copy-start(s32[1,2,4,128]{3,1,2,0:T(2,128)} %copy.275) | copy-start | bytes 12292
  44.8 9.3 %copy-start.5 = (s32[4,1024]{1,0:T(4,128)S(1)}, s32[4,1024]{1,0:T(4,128)}, u32[]{:S(2)}) copy-start(s32[4,1024]{1,0:T(4,128)} %add.1132) | copy-start | bytes 49156
  44.8 9.3 %copy-start.16 = (s32[1024]{0:T(1024)S(1)}, s32[1024]{0:T(1024)}, u32[]{:S(2)}) copy-start(s32[1024]{0:T(1024)} %add.1129) | copy-start | bytes 12292
  53.0 1.3 %copy-start.13 = (s32[64]{0:T(128)S(1)}, s32[64]{0:T(128)}, u32[]{:S(2)}) copy-start(s32[64]{0:T(128)} %copy-done.12) | copy-start | bytes 772
  53.0 8.4 %copy-start.11 = (f32[4,1024]{1,0:T(4,128)S(1)}, f32[4,1024]{1,0:T(4,128)}, u32[]{:S(2)}) copy-start(f32[4,1024]{1,0:T(4,128)} %copy-done.10) | copy-start | bytes 49156
  53.0 8.4 %copy-start.6 = (bf16[48,64]{0,1:T(8,128)(2,1)S(1)}, bf16[48,64]{0,1:T(8,128)(2,1)}, u32[]{:S(2)}) copy-start(bf16[48,64]{0,1:T(8,128)(2,1)} %constant_dynamic-slice_fusion.23) | copy-start | bytes 18436
  53.0 8.5 %copy-start.7 = (bf16[48,64]{0,1:T(8,128)(2,1)S(1)}, bf16[48,64]{0,1:T(8,128)(2,1)}, u32[]{:S(2)}) copy-start(bf16[48,64]{0,1:T(8,128)(2,1)} %constant_dynamic-slice_fusion.22) | copy-start | bytes 18436
  53.0 8.6 %copy-start.8 = (bf16[48,64]{0,1:T(8,128)(2,1)S(1)}, bf16[48,64]{0,1:T(8,128)(2,1)}, u32[]{:S(2)}) copy-start(bf16[48,64]{0,1:T(8,128)(2,1)} %constant_dynamic-slice_fusion.21) | copy-start | bytes 18436
  54.2 37.8 %copy-start.14 = (s32[4,256]{1,0:T(4,128)S(1)}, s32[4,256]{1,0:T(4,128)}, u32[]{:S(2)}) copy-start(s32[4,256]{1,0:T(4,128)} %convert_reduce_fusion.3) | copy-start | bytes 12292
  56.6 5.5 %collective-permute-start.7 = (bf16[2,4,48,32]{3,2,1,0:T(8,128)(2,1)S(1)}, bf16[2,4,48,32]{3,2,1,0:T(8,128)(2,1)S(1)}, u32[]{:S(2)}, u32[]{:S(2)}) collective-permute-start(bf16[2,4,48,32]{3,2,1,0:T(8,128)(2,1)S(1)} %maximum_select_fusion.9), channel_id=1, source_target_pairs={{0,8},{4,12},{8,0},{12,4},{16,24},{20,28},{24,16},{28,20},{32,40},... | collective-permute-start | bytes 73736 | tf_op jit(solution)/shard_map/ppermute | solution.py:51
  62.3 6.8 %collective-permute-start.8 = (bf16[2,4,48,64]{3,2,1,0:T(8,128)(2,1)S(1)}, bf16[2,4,48,64]{3,2,1,0:T(8,128)(2,1)S(1)}, u32[]{:S(2)}, u32[]{:S(2)}) collective-permute-start(bf16[2,4,48,64]{3,2,1,0:T(8,128)(2,1)S(1)} %maximum_select_fusion.10), channel_id=1, source_target_pairs={{0,16},{4,20},{8,24},{12,28},{16,0},{20,4},{24,8},{28,12},{32,48},... | collective-permute-start | bytes 147464 | tf_op jit(solution)/shard_map/ppermute | solution.py:51
  65.9 5.7 %collective-permute-start.3 = (bf16[2,4,48,128]{3,2,1,0:T(8,128)(2,1)S(1)}, bf16[2,4,48,128]{3,2,1,0:T(8,128)(2,1)S(1)}, u32[]{:S(2)}, u32[]{:S(2)}) collective-permute-start(bf16[2,4,48,128]{3,2,1,0:T(8,128)(2,1)S(1)} %maximum_select_fusion.8), channel_id=1, source_target_pairs={{0,8},{4,12},{8,0},{12,4},{16,24},{20,28},{24,16},{28,20},{32,40},... | collective-permute-start | bytes 294920 | tf_op jit(solution)/shard_map/ppermute | solution.py:51
  69.2 6.2 %collective-permute-start.9 = (bf16[2,4,48,128]{3,2,1,0:T(8,128)(2,1)S(1)}, bf16[2,4,48,128]{3,2,1,0:T(8,128)(2,1)S(1)}, u32[]{:S(2)}, u32[]{:S(2)}) collective-permute-start(bf16[2,4,48,128]{3,2,1,0:T(8,128)(2,1)S(1)} %maximum_select_fusion.11), channel_id=1, source_target_pairs={{0,32},{4,36},{8,40},{12,44},{16,48},{20,52},{24,56},{28,60},{32,0... | collective-permute-start | bytes 294920 | tf_op jit(solution)/shard_map/ppermute | solution.py:51
  71.7 9.4 %collective-permute-start.4 = (bf16[2,4,48,256]{3,2,1,0:T(8,128)(2,1)S(1)}, bf16[2,4,48,256]{3,2,1,0:T(8,128)(2,1)S(1)}, u32[]{:S(2)}, u32[]{:S(2)}) collective-permute-start(bf16[2,4,48,256]{3,2,1,0:T(8,128)(2,1)S(1)} %maximum_select_fusion.6), channel_id=1, source_target_pairs={{0,16},{4,20},{8,24},{12,28},{16,0},{20,4},{24,8},{28,12},{32,48},... | collective-permute-start | bytes 589832 | tf_op jit(solution)/shard_map/ppermute | solution.py:51
  73.1 18.7 %collective-permute-start.1 = (bf16[2,4,48,512]{3,2,1,0:T(8,128)(2,1)S(1)}, bf16[2,4,48,512]{3,2,1,0:T(8,128)(2,1)S(1)}, u32[]{:S(2)}, u32[]{:S(2)}) collective-permute-start(bf16[2,4,48,512]{3,2,1,0:T(8,128)(2,1)S(1)} %maximum_select_fusion.3), channel_id=1, source_target_pairs={{0,8},{4,12},{8,0},{12,4},{16,24},{20,28},{24,16},{28,20},{32,40},... | collective-permute-start | bytes 1179656 | tf_op jit(solution)/shard_map/ppermute | solution.py:51
  75.5 10.1 %collective-permute-start.10 = (bf16[2,4,48,256]{3,2,1,0:T(8,128)(2,1)S(1)}, bf16[2,4,48,256]{3,2,1,0:T(8,128)(2,1)S(1)}, u32[]{:S(2)}, u32[]{:S(2)}) collective-permute-start(bf16[2,4,48,256]{3,2,1,0:T(8,128)(2,1)S(1)} %maximum_select_fusion.7), channel_id=1, source_target_pairs={{0,64},{4,68},{8,72},{12,76},{16,80},{20,84},{24,88},{28,92},{32,9... | collective-permute-start | bytes 589832 | tf_op jit(solution)/shard_map/ppermute | solution.py:51
  81.2 17.3 %collective-permute-start.5 = (bf16[2,4,48,512]{3,2,1,0:T(8,128)(2,1)S(1)}, bf16[2,4,48,512]{3,2,1,0:T(8,128)(2,1)S(1)}, u32[]{:S(2)}, u32[]{:S(2)}) collective-permute-start(bf16[2,4,48,512]{3,2,1,0:T(8,128)(2,1)S(1)} %maximum_select_fusion.4), channel_id=1, source_target_pairs={{0,32},{4,36},{8,40},{12,44},{16,48},{20,52},{24,56},{28,60},{32,0... | collective-permute-start | bytes 1179656 | tf_op jit(solution)/shard_map/ppermute | solution.py:51
  85.7 29.0 %collective-permute-start.11 = (bf16[2,4,48,512]{3,2,1,0:T(8,128)(2,1)S(1)}, bf16[2,4,48,512]{3,2,1,0:T(8,128)(2,1)S(1)}, u32[]{:S(2)}, u32[]{:S(2)}) collective-permute-start(bf16[2,4,48,512]{3,2,1,0:T(8,128)(2,1)S(1)} %maximum_select_fusion.5), channel_id=1, source_target_pairs={{0,128},{4,132},{8,136},{12,140},{16,144},{20,148},{24,152},{28,15... | collective-permute-start | bytes 1179656 | tf_op jit(solution)/shard_map/ppermute | solution.py:51
  94.8 3.9 %copy-start.19 = (s32[4,64]{1,0:T(4,128)S(1)}, s32[4,64]{1,0:T(4,128)}, u32[]{:S(2)}) copy-start(s32[4,64]{1,0:T(4,128)} %convert_reduce_fusion.5) | copy-start | bytes 3076
  96.2 18.7 %copy-start.18 = (s32[4,16]{1,0:T(4,128)S(1)}, s32[4,16]{1,0:T(4,128)}, u32[]{:S(2)}) copy-start(s32[4,16]{1,0:T(4,128)} %convert_reduce_fusion.6) | copy-start | bytes 772
  117.6 9.5 %copy-start.20 = (f32[192]{0:T(256)S(1)}, f32[192]{0:T(256)}, u32[]{:S(2)}) copy-start(f32[192]{0:T(256)} %param.11) | copy-start | bytes 2308
  117.6 9.5 %copy-start.21 = (f32[192]{0:T(256)S(1)}, f32[192]{0:T(256)}, u32[]{:S(2)}) copy-start(f32[192]{0:T(256)} %param.10) | copy-start | bytes 2308
  117.9 3.7 %collective-permute-start.12 = (f32[2,1024]{1,0:T(2,128)S(1)}, f32[2,1024]{1,0:T(2,128)S(1)}, u32[]{:S(2)}, u32[]{:S(2)}) collective-permute-start(f32[2,1024]{1,0:T(2,128)S(1)} %pad_maximum_fusion.3), channel_id=1, source_target_pairs={{0,1},{1,0},{2,3},{3,2},{4,5},{5,4},{6,7},{7,6},{8,9},{9,8},{10,11... | collective-permute-start | bytes 24584 | tf_op jit(solution)/shard_map/ppermute | solution.py:63
  121.6 5.2 %collective-permute-start.13 = (f32[2,1024]{1,0:T(2,128)S(1)}, f32[2,1024]{1,0:T(2,128)S(1)}, u32[]{:S(2)}, u32[]{:S(2)}) collective-permute-start(f32[2,1024]{1,0:T(2,128)S(1)} %fusion.154), channel_id=1, source_target_pairs={{0,2},{1,3},{2,0},{3,1},{4,6},{5,7},{6,4},{7,5},{8,10},{9,11},{10,... | collective-permute-start | bytes 24584 | tf_op jit(solution)/shard_map/ppermute | solution.py:63

commit v3 on v1

v3 whole, which is shorter than its diff:
```python
import math

import jax
import jax.numpy as jnp
from jax import lax
from jax.experimental import pallas as pl
from jax.experimental.pallas import tpu as pltpu
from jax.sharding import PartitionSpec as P

D = 768
HD = 48
SEG = 1024
LOCAL = 1024
MESH = pl.DeviceIdType.MESH
BRANCHES = ((256, 4), (64, 16), (16, 64))


def to_token_major(x, heads):
    x = x.reshape(heads, HD, 16, 4, 4, 4)
    x = jnp.transpose(x, (0, 5, 4, 3, 2, 1))
    return x.reshape(heads, LOCAL, HD)


def from_token_major(x, heads):
    x = x.reshape(heads, 4, 4, 4, 16, HD)
    x = jnp.transpose(x, (0, 5, 4, 3, 2, 1))
    return x.reshape(heads * HD, LOCAL)


def pos_of(device, index):
    local = 64 * (index % 16) + 16 * (index // 16 % 4) + 4 * (index // 64 % 4) + index // 256
    return device * LOCAL + local


def slide_of(positions, slide_ends):
    return jnp.sum((positions[..., None] >= slide_ends).astype(jnp.int32), axis=-1)


def attention_kernel(
    q_ref, k_ref, v_ref, s1_ref, s2_ref, s3_ref,
    sq0_ref, sk0_ref, sq1_ref, sk1_ref, sq2_ref, sk2_ref, sq3_ref, sk3_ref,
    out_ref,
    kv1, kv2, kv3, m_acc, l_acc, send_sem, recv_sem, local_sem,
):
    heads = q_ref.shape[0]
    devices = lax.axis_size("seq")
    me = lax.axis_index("seq")
    hy = lax.axis_index("head")
    scale = 1.0 / math.sqrt(HD)
    sends = (s1_ref, s2_ref, s3_ref)
    bufs = (kv1, kv2, kv3)

    barrier = pltpu.get_barrier_semaphore()

    def greet(o, carry):
        pl.semaphore_signal(barrier, inc=1, device_id=(lax.rem(me + o, devices), hy), device_id_type=MESH)
        return carry

    lax.fori_loop(1, devices, greet, 0)
    pl.semaphore_wait(barrier, devices - 1)

    def window(b, start, rows):
        return bufs[b].at[:, :, pl.ds(start, rows), :]

    locals_ = []
    for b, (count, group) in enumerate(BRANCHES):
        member = lax.rem(me, group)
        cp = pltpu.make_async_copy(sends[b], window(b, pl.multiple_of(member * count, 16), count), local_sem.at[b])
        cp.start()
        locals_.append(cp)
    for b, (count, group) in enumerate(BRANCHES):
        member = lax.rem(me, group)
        first = me - member

        def push(o, carry, b=b, count=count, group=group, member=member, first=first):
            target = first + lax.rem(member + o, group)
            pltpu.make_async_remote_copy(
                src_ref=sends[b],
                dst_ref=window(b, pl.multiple_of(member * count, 16), count),
                send_sem=send_sem.at[b],
                recv_sem=recv_sem.at[b],
                device_id=(target, hy),
                device_id_type=MESH,
            ).start()
            return carry

        lax.fori_loop(1, group, push, 0)

    def attend(q, k, v, sq, sk):
        s = lax.dot_general(q, k, (((1,), (1,)), ((), ())), preferred_element_type=jnp.float32) * scale
        s = jnp.where(sq == sk, s, -1e30)
        m = jnp.max(s, axis=-1, keepdims=True)
        p = jnp.exp(s - m)
        l = jnp.sum(p, axis=-1, keepdims=True)
        o = jnp.dot(p.astype(jnp.bfloat16), v, preferred_element_type=jnp.float32)
        return m, l, o

    chunk = 256
    per_head = LOCAL // chunk

    def branch0(i, carry):
        j = i // per_head
        rows = pl.ds(pl.multiple_of(i % per_head * chunk, chunk), chunk)
        m, l, o = attend(q_ref[j, rows], k_ref[j], v_ref[j], sq0_ref[rows], sk0_ref[...])
        m_acc[j, rows] = m
        l_acc[j, rows] = l
        out_ref[j, rows] = o
        return carry

    lax.fori_loop(0, heads * per_head, branch0, 0)

    for b, (count, group) in enumerate(BRANCHES):
        locals_[b].wait()
        pltpu.make_async_copy(window(b, 0, (group - 1) * count), window(b, 0, (group - 1) * count), recv_sem.at[b]).wait()
        sq_ref, sk_ref = ((sq1_ref, sk1_ref), (sq2_ref, sk2_ref), (sq3_ref, sk3_ref))[b]

        def branch(j, carry, b=b, count=count, sq_ref=sq_ref, sk_ref=sk_ref):
            start = j * 256 + (hy * 64 if b >= 1 else 0)
            rows = pl.ds(pl.multiple_of(start, 16), count)
            m_new, l_new, o_new = attend(
                q_ref[j, rows], bufs[b][0, j], bufs[b][1, j], sq_ref[j], sk_ref[j]
            )
            m_old = m_acc[j, rows]
            mn = jnp.maximum(m_old, m_new)
            keep_old = jnp.exp(m_old - mn)
            keep_new = jnp.exp(m_new - mn)
            m_acc[j, rows] = mn
            l_acc[j, rows] = l_acc[j, rows] * keep_old + l_new * keep_new
            out_ref[j, rows] = out_ref[j, rows] * keep_old + o_new * keep_new
            return carry

        lax.fori_loop(0, heads, branch, 0)

    def finish(j, carry):
        out_ref[j] = out_ref[j] / l_acc[j]
        return carry

    lax.fori_loop(0, heads, finish, 0)

    for b, (count, group) in enumerate(BRANCHES):
        pltpu.make_async_copy(window(b, 0, (group - 1) * count), window(b, 0, (group - 1) * count), send_sem.at[b]).wait()


def head_sum(x):
    for mask in (1, 2):
        x = x + lax.ppermute(x, "head", [(i, i ^ mask) for i in range(4)])
    return x


def per_device(queries, keys, values, slide_lengths, norm_gain, norm_bias):
    heads = queries.shape[0] // HD
    seq = lax.axis_index("seq")
    hy = lax.axis_index("head")
    slide_ends = jnp.cumsum(slide_lengths)
    q = to_token_major(queries, heads)
    k = to_token_major(keys, heads)
    v = to_token_major(values, heads)

    slide0 = slide_of(pos_of(seq, jnp.arange(LOCAL)), slide_ends)
    sends, slides = [], []
    for b, (count, group) in enumerate(BRANCHES):
        starts = [j * 256 + (hy * 64 if b >= 1 else 0) for j in range(heads)]
        ks = jnp.stack([lax.dynamic_slice_in_dim(k[j], starts[j], count, 0) for j in range(heads)])
        vs = jnp.stack([lax.dynamic_slice_in_dim(v[j], starts[j], count, 0) for j in range(heads)])
        sends.append(jnp.stack([ks, vs]))
        idx = jnp.stack([starts[j] + jnp.arange(count) for j in range(heads)])
        q_slide = slide_of(pos_of(seq, idx), slide_ends)
        first = seq // group * group
        members = first + jnp.arange(group)
        k_slide = slide_of(pos_of(members[None, :, None], idx[:, None, :]), slide_ends)
        slides += [q_slide.reshape(heads, count, 1), k_slide.reshape(heads, 1, group * count)]

    vmem = pl.BlockSpec(memory_space=pltpu.VMEM)
    attended = pl.pallas_call(
        attention_kernel,
        out_shape=jax.ShapeDtypeStruct((heads, LOCAL, HD), jnp.float32),
        in_specs=[vmem] * 14,
        out_specs=vmem,
        scratch_shapes=[
            pltpu.VMEM((2, heads, LOCAL, HD), jnp.bfloat16),
            pltpu.VMEM((2, heads, LOCAL, HD), jnp.bfloat16),
            pltpu.VMEM((2, heads, LOCAL, HD), jnp.bfloat16),
            pltpu.VMEM((heads, LOCAL, 1), jnp.float32),
            pltpu.VMEM((heads, LOCAL, 1), jnp.float32),
            pltpu.SemaphoreType.DMA((3,)),
            pltpu.SemaphoreType.DMA((3,)),
            pltpu.SemaphoreType.DMA((3,)),
        ],
        compiler_params=pltpu.CompilerParams(
            collective_id=0, has_side_effects=True, vmem_limit_bytes=60 * 1024 * 1024
        ),
    )(q, k, v, *sends, slide0.reshape(LOCAL, 1), slide0.reshape(1, LOCAL), *slides)

    feats = jnp.sum(attended, axis=(0, 2))
    squares = jnp.sum(attended * attended, axis=(0, 2))
    sums = head_sum(jnp.stack([feats, squares]))
    mean = sums[0] / D
    var = sums[1] / D - mean * mean
    normed = (attended - mean[None, :, None]) * lax.rsqrt(var + 1e-05)[None, :, None]
    gain = norm_gain.reshape(heads, 1, HD)
    bias = norm_bias.reshape(heads, 1, HD)
    out = (normed * gain + bias).astype(jnp.bfloat16)
    return from_token_major(out, heads)


def solution(mesh):
    placed = (P("head", "seq"),) * 3 + (P(), P("head"), P("head"))
    return jax.shard_map(
        per_device, mesh=mesh, in_specs=placed, out_specs=P("head", "seq"), check_vma=False
    )
```

time: 198 us -> 157 us (0.79)
  the two profiles are of different devices: /device:TPU:4 before, /device:TPU:70 now
where the time goes in v3:
time: 157 us; the launch traced here: 156 us
  Pallas kernels  95.3 us (61%)
  local copies, waits for them, and re-layouts  39.2 us (25%)
  other arithmetic  12.6 us (8%)
  starting transfers between devices  4.94 us (3%)
  waiting for transfers between devices  3.86 us (2%)
    pallas_call x1, Pallas kernels, per_device(): pl.pallas_call(attention_kernel, out_shape=jax.ShapeDtypeStruct((heads, L...  95.3 us
    slice x5, local copies, waits for them, and re-layouts, per_device(): v[j]  7.97 us
    reduce_sum x7, other arithmetic, slide_of(): jnp.sum((positions[..., None] >= slide_ends).astype(jnp.int32), axis=-1)  7.91 us
    slice x5, local copies, waits for them, and re-layouts, per_device(): k[j]  6.35 us
    another operation x12, local copies, waits for them, and re-layouts, per_device(): jnp.stack([lax.dynamic_slice_in_dim(v[j], starts[j], count, 0) for j in r...  5.77 us
    transpose x3, local copies, waits for them, and re-layouts, to_token_major(): x = jnp.transpose(x, (0, 5, 4, 3, 2, 1))  4.99 us
    ppermute x2, starting transfers between devices, head_sum(): x = x + lax.ppermute(x, 'head', [(i, i ^ mask) for i in range(4)])  4.94 us
    ppermute x2, waiting for transfers between devices, head_sum(): x = x + lax.ppermute(x, 'head', [(i, i ^ mask) for i in range(4)])  3.86 us
  transfers between devices with their start and end apart: 2, of which 2 were waited for; matrix products, arithmetic and copies ran while one was open for 0% of the time, Pallas kernels for 0%

profile of v3, /device:TPU:70, one launch (start us, length us, event | category | flops | bytes accessed | tf_op | source)
XLA Modules:
  0.0 156.4 jit_solution(9824756381079005229)
XLA Ops:
  0.0 1.2 copy.129
  1.2 0.5 reshape.1676
  1.7 3.0 %fusion.58 = (bf16[1,4,4,4,16,48]{5,0,1,2,3,4:T(2,128)(2,1)S(1)}, bf16[1,4,4,4,16,48]{5,0,1,2,3,4:T(2,128)(2,1)S(1)}, bf16[1,4,4,4,16,48]{5,0,1,2,3,4:T(2,128)(2,1)}, bf16[1,4,4,4,16,48]{5,0,1,2,3,4:T(2,128)(2,1)}) fusion(bf16[4,4,4,4,16,48]{5,0,1,2,3,4:T(4,128)(2,1)S(1)} %bitcast.88), kind=kLoop, calls=%fused_computation.187 | loop fusion | bytes 786432 | tf_op jit(solution)/shard_map/slice | solution.py:163
  4.8 0.3 copy.152
  5.3 0.5 reshape.1678
  5.8 2.5 %fusion.59 = (bf16[1,4,4,4,16,48]{5,0,1,2,3,4:T(2,128)(2,1)S(1)}, bf16[1,4,4,4,16,48]{5,0,1,2,3,4:T(2,128)(2,1)S(1)}, bf16[1,4,4,4,16,48]{5,0,1,2,3,4:T(2,128)(2,1)}, bf16[1,4,4,4,16,48]{5,0,1,2,3,4:T(2,128)(2,1)}) fusion(bf16[4,4,4,4,16,48]{5,0,1,2,3,4:T(4,128)(2,1)S(1)} %bitcast.91), kind=kLoop, calls=%fused_computation.188 | loop fusion | bytes 786432 | tf_op jit(solution)/shard_map/slice | solution.py:164
  8.4 1.0 copy.156
  9.4 0.7 dynamic-slice_bitcast_fusion.8
  10.1 0.7 dynamic-slice_bitcast_fusion
  10.8 1.4 copy.151
  12.1 2.1 %copy.155 = bf16[1,4,4,4,16,48]{5,4,3,2,1,0:T(8,128)(2,1)} copy(bf16[1,4,4,4,16,48]{5,0,1,2,3,4:T(2,128)(2,1)} %get-tuple-element.19) | data formatting | bytes 196608 | tf_op jit(solution)/shard_map/slice | solution.py:164
  14.2 0.7 dynamic-slice_bitcast_fusion.9
  14.9 0.7 dynamic-slice_bitcast_fusion.1
  15.6 1.4 copy.150
  17.0 2.1 %copy.154 = bf16[1,4,4,4,16,48]{5,4,3,2,1,0:T(8,128)(2,1)} copy(bf16[1,4,4,4,16,48]{5,0,1,2,3,4:T(2,128)(2,1)} %get-tuple-element.20) | data formatting | bytes 196608 | tf_op jit(solution)/shard_map/slice | solution.py:164
  19.0 1.3 dynamic-slice_bitcast_fusion.10
  20.3 0.7 dynamic-slice_bitcast_fusion.2
  21.0 0.3 copy.149
  21.3 0.3 copy.153
  21.6 0.6 dynamic-slice_bitcast_fusion.11
  22.3 0.5 fusion.60
  22.8 0.5 fusion.61
  23.4 1.7 %copy.130 = bf16[4,4,4,4,16,48]{5,4,3,2,1,0:T(8,128)(2,1)} copy(bf16[4,4,4,4,16,48]{5,0,1,2,3,4:T(4,128)(2,1)S(1)} %bitcast.90) | data formatting | bytes 786432 | tf_op jit(solution)/shard_map/transpose | solution.py:20
  25.0 1.7 %copy.132 = bf16[4,4,4,4,16,48]{5,4,3,2,1,0:T(8,128)(2,1)} copy(bf16[4,4,4,4,16,48]{5,0,1,2,3,4:T(4,128)(2,1)S(1)} %bitcast.93) | data formatting | bytes 786432 | tf_op jit(solution)/shard_map/transpose | solution.py:20
  27.1 5.1 %convert_reduce_fusion = s32[4,64,16]{2,1,0:T(8,128)S(1)} fusion(s32[64]{0:T(128)S(1)} %reduce, s32[4,64,16]{2,1,0:T(8,128)S(1)} %broadcast_add_fusion), kind=kLoop, calls=%fused_computation.2 | loop fusion | flops 782336 | bytes 33024 | tf_op jit(solution)/shard_map/reduce_sum | solution.py:36
  32.2 0.7 reshape.1692.sk3_ref
  33.0 2.0 %convert_reduce_fusion.1 = s32[4,16,64]{2,1,0:T(8,128)S(1)} fusion(s32[64]{0:T(128)S(1)} %reduce, s32[4,16,64]{2,1,0:T(8,128)S(1)} %broadcast_add_fusion.1), kind=kLoop, calls=%fused_computation.3 | loop fusion | flops 782336 | bytes 33024 | tf_op jit(solution)/shard_map/reduce_sum | solution.py:36
  35.0 0.7 reshape.1687.sk2_ref
  36.0 0.6 reshape.1685.sk1_ref
  36.9 0.8 copy.161.sq2_ref
  37.9 0.7 copy.162.sq3_ref
  39.9 1.0 copy.158.s1_ref
  41.0 1.0 copy.160.sq1_ref
  42.1 1.0 copy.159.sq0_ref
  43.4 0.5 reshape.1674
  43.9 1.7 %copy.128 = bf16[4,4,4,4,16,48]{5,4,3,2,1,0:T(8,128)(2,1)} copy(bf16[4,4,4,4,16,48]{5,0,1,2,3,4:T(4,128)(2,1)S(1)} %bitcast.98) | data formatting | bytes 786432 | tf_op jit(solution)/shard_map/transpose | solution.py:20
  45.7 0.6 pad_maximum_fusion.2.s3_ref
  46.3 0.7 pad_maximum_fusion.1.s2_ref
  47.0 95.3 %shard_map.64 = f32[4,1024,48]{2,1,0:T(8,128)} custom-call(bf16[4,1024,48]{2,1,0:T(8,128)(2,1)} %bitcast.96, bf16[4,1024,48]{2,1,0:T(8,128)(2,1)} %bitcast.94, bf16[4,1024,48]{2,1,0:T(8,128)(2,1)} %bitcast.95, bf16[2,4,256,48]{3,2,1,0:T(8,128)(2,1)} %copy.158.s1_ref, bf16[2,4,64,48]{3,2,1,0:T(8,128)(2,1)} %pad_maximum_fusion.1.s2_ref, ...), custom_call_target="tpu_custom_call" | custom-call | tf_op jit(solution)/shard_map/pallas_call | solution.py:174
  142.4 2.2 %fusion.54 = (f32[1024]{0:T(1024)S(1)}, f32[1024]{0:T(1024)S(1)}) fusion(f32[4,1024,48]{2,1,0:T(8,128)} %shard_map.64), kind=kLoop, calls=%fused_computation.186 | loop fusion | flops 587776 | bytes 794624 | tf_op jit(solution)/shard_map/reduce_sum | solution.py:194
  144.6 1.7 %collective-permute-start = (f32[2,1024]{1,0:T(2,128)S(1)}, f32[2,1024]{1,0:T(2,128)S(1)}, u32[]{:S(2)}, u32[]{:S(2)}) collective-permute-start(f32[2,1024]{1,0:T(2,128)S(1)} %pad_maximum_fusion.3), channel_id=1, source_target_pairs={{0,1},{1,0},{2,3},{3,2},{4,5},{5,4},{6,7},{7,6},{8,9},{9,8},{10,11... | collective-permute-start | bytes 24584 | tf_op jit(solution)/shard_map/ppermute | solution.py:146
  146.2 2.1 %collective-permute-done = f32[2,1024]{1,0:T(2,128)S(1)} collective-permute-done((f32[2,1024]{1,0:T(2,128)S(1)}, f32[2,1024]{1,0:T(2,128)S(1)}, u32[]{:S(2)}, u32[]{:S(2)}) %collective-permute-start) | collective-permute-done | bytes 8224 | tf_op jit(solution)/shard_map/ppermute | solution.py:146
  148.3 3.3 %collective-permute-start.1 = (f32[2,1024]{1,0:T(2,128)S(1)}, f32[2,1024]{1,0:T(2,128)S(1)}, u32[]{:S(2)}, u32[]{:S(2)}) collective-permute-start(f32[2,1024]{1,0:T(2,128)S(1)} %fusion.53), channel_id=1, source_target_pairs={{0,2},{1,3},{2,0},{3,1},{4,6},{5,7},{6,4},{7,5},{8,10},{9,11},{10,... | collective-permute-start | bytes 24584 | tf_op jit(solution)/shard_map/ppermute | solution.py:146
  151.8 1.8 %collective-permute-done.1 = f32[2,1024]{1,0:T(2,128)S(1)} collective-permute-done((f32[2,1024]{1,0:T(2,128)S(1)}, f32[2,1024]{1,0:T(2,128)S(1)}, u32[]{:S(2)}, u32[]{:S(2)}) %collective-permute-start.1) | collective-permute-done | bytes 8224 | tf_op jit(solution)/shard_map/ppermute | solution.py:146
  153.6 0.4 add_convert_fusion
  154.1 0.8 copy.167
  154.9 0.6 reshape.1691
  155.5 0.9 copy.165
  (79 shorter events, 3.4 us)
Async XLA Ops:
  1.7 3.4 %copy-start.1 = (bf16[192,1024]{1,0:T(8,128)(2,1)S(1)}, bf16[192,1024]{1,0:T(8,128)(2,1)}, u32[]{:S(2)}) copy-start(bf16[192,1024]{1,0:T(8,128)(2,1)} %param.8) | copy-start | bytes 1179652
  23.4 3.3 %copy-start.10 = (s32[64]{0:T(128)S(1)}, s32[64]{0:T(128)}, u32[]{:S(2)}) copy-start(s32[64]{0:T(128)} %param.9) | copy-start | bytes 772
  39.0 4.2 %copy-start.2 = (bf16[192,1024]{1,0:T(8,128)(2,1)S(1)}, bf16[192,1024]{1,0:T(8,128)(2,1)}, u32[]{:S(2)}) copy-start(bf16[192,1024]{1,0:T(8,128)(2,1)} %param.6) | copy-start | bytes 1179652
  42.1 3.5 %copy-start.3 = (s32[1024]{0:T(1024)}, s32[1024]{0:T(1024)S(1)}, u32[]{:S(2)}) copy-start(s32[1024]{0:T(1024)S(1)} %convert_reduce_fusion.4) | copy-start | bytes 12292
  43.2 2.4 %copy-start.5 = (bf16[1,16,48]{2,1,0:T(8,128)(2,1)S(1)}, bf16[1,16,48]{2,1,0:T(8,128)(2,1)}, u32[]{:S(2)}) copy-start(bf16[1,16,48]{2,1,0:T(8,128)(2,1)} %get-tuple-element.44) | copy-start | bytes 4612
  43.2 2.4 %copy-start.7 = (bf16[1,16,48]{2,1,0:T(8,128)(2,1)S(1)}, bf16[1,16,48]{2,1,0:T(8,128)(2,1)}, u32[]{:S(2)}) copy-start(bf16[1,16,48]{2,1,0:T(8,128)(2,1)} %get-tuple-element.48) | copy-start | bytes 4612
  43.2 2.5 %copy-start.4 = (bf16[1,16,48]{2,1,0:T(8,128)(2,1)S(1)}, bf16[1,16,48]{2,1,0:T(8,128)(2,1)}, u32[]{:S(2)}) copy-start(bf16[1,16,48]{2,1,0:T(8,128)(2,1)} %get-tuple-element.43) | copy-start | bytes 4612
  43.2 2.5 %copy-start.6 = (bf16[1,16,48]{2,1,0:T(8,128)(2,1)S(1)}, bf16[1,16,48]{2,1,0:T(8,128)(2,1)}, u32[]{:S(2)}) copy-start(bf16[1,16,48]{2,1,0:T(8,128)(2,1)} %get-tuple-element.47) | copy-start | bytes 4612
  142.3 9.3 %copy-start.8 = (f32[192]{0:T(256)S(1)}, f32[192]{0:T(256)}, u32[]{:S(2)}) copy-start(f32[192]{0:T(256)} %param.11) | copy-start | bytes 2308
  142.3 9.3 %copy-start.9 = (f32[192]{0:T(256)S(1)}, f32[192]{0:T(256)}, u32[]{:S(2)}) copy-start(f32[192]{0:T(256)} %param.10) | copy-start | bytes 2308
  142.4 11.3 %copy-start = (f32[4,1024,48]{2,1,0:T(8,128)S(1)}, f32[4,1024,48]{2,1,0:T(8,128)}, u32[]{:S(2)}) copy-start(f32[4,1024,48]{2,1,0:T(8,128)} %shard_map.64) | copy-start | bytes 2359300
  144.6 3.7 %collective-permute-start = (f32[2,1024]{1,0:T(2,128)S(1)}, f32[2,1024]{1,0:T(2,128)S(1)}, u32[]{:S(2)}, u32[]{:S(2)}) collective-permute-start(f32[2,1024]{1,0:T(2,128)S(1)} %pad_maximum_fusion.3), channel_id=1, source_target_pairs={{0,1},{1,0},{2,3},{3,2},{4,5},{5,4},{6,7},{7,6},{8,9},{9,8},{10,11... | collective-permute-start | bytes 24584 | tf_op jit(solution)/shard_map/ppermute | solution.py:146
  148.3 5.2 %collective-permute-start.1 = (f32[2,1024]{1,0:T(2,128)S(1)}, f32[2,1024]{1,0:T(2,128)S(1)}, u32[]{:S(2)}, u32[]{:S(2)}) collective-permute-start(f32[2,1024]{1,0:T(2,128)S(1)} %fusion.53), channel_id=1, source_target_pairs={{0,2},{1,3},{2,0},{3,1},{4,6},{5,7},{6,4},{7,5},{8,10},{9,11},{10,... | collective-permute-start | bytes 24584 | tf_op jit(solution)/shard_map/ppermute | solution.py:146

commit v4 on v3

v4 whole, which is shorter than its diff:
```python
import math

import jax
import jax.numpy as jnp
from jax import lax
from jax.experimental import pallas as pl
from jax.experimental.pallas import tpu as pltpu
from jax.sharding import PartitionSpec as P

D = 768
HD = 48
SEG = 1024
LOCAL = 1024
MESH = pl.DeviceIdType.MESH
BRANCHES = ((256, 4), (64, 16), (16, 64))
SHIFT = 64


def to_token_major(x):
    f = x.shape[0]
    x = x.reshape(f, 16, 4, 4, 4)
    x = jnp.transpose(x, (4, 3, 2, 1, 0))
    return x.reshape(LOCAL, f)


def from_token_major(x):
    f = x.shape[1]
    x = x.reshape(4, 4, 4, 16, f)
    x = jnp.transpose(x, (4, 3, 2, 1, 0))
    return x.reshape(f, LOCAL)


def pos_of(device, index):
    local = 64 * (index % 16) + 16 * (index // 16 % 4) + 4 * (index // 64 % 4) + index // 256
    return device * LOCAL + local


def slide_of(positions, slide_ends):
    return jnp.sum((positions[..., None] >= slide_ends).astype(jnp.int32), axis=-1)


def attention_kernel(
    q_ref, kv_ref, s1_ref, s2_ref, s3_ref, sq_ref, sk_ref,
    out_ref,
    kv1, kv2, kv3, m_acc, l_acc, send_sem, recv_sem, local_sem,
):
    heads = 4
    me = lax.axis_index("seq")
    hy = lax.axis_index("head")
    devices = lax.axis_size("seq")
    scale = 1.0 / math.sqrt(HD)
    sends = (s1_ref, s2_ref, s3_ref)
    bufs = (kv1, kv2, kv3)
    width = heads * HD

    barrier = pltpu.get_barrier_semaphore()

    def greet(o, carry):
        pl.semaphore_signal(barrier, inc=1, device_id=(lax.rem(me + o, devices), hy), device_id_type=MESH)
        return carry

    lax.fori_loop(1, devices, greet, 0)
    pl.semaphore_wait(barrier, devices - 1)

    def window(b, start, rows):
        return bufs[b].at[pl.ds(pl.multiple_of(start, 16), rows), :]

    locals_ = []
    for b, (count, group) in enumerate(BRANCHES):
        member = lax.rem(me, group)
        cp = pltpu.make_async_copy(sends[b], window(b, member * count, count), local_sem.at[b])
        cp.start()
        locals_.append(cp)
    for b, (count, group) in enumerate(BRANCHES):
        member = lax.rem(me, group)
        first = me - member

        def push(o, carry, b=b, count=count, group=group, member=member, first=first):
            target = first + lax.rem(member + o, group)
            pltpu.make_async_remote_copy(
                src_ref=sends[b],
                dst_ref=window(b, member * count, count),
                send_sem=send_sem.at[b],
                recv_sem=recv_sem.at[b],
                device_id=(target, hy),
                device_id_type=MESH,
            ).start()
            return carry

        lax.fori_loop(1, group, push, 0)

    q_lane = lax.broadcasted_iota(jnp.int32, (1, 256), 1) // HD
    o_lane = (lax.broadcasted_iota(jnp.int32, (1, 256), 1) - SHIFT) // HD

    def attend(q, j, kv, same):
        qz = jnp.where(q_lane == j, q, jnp.zeros_like(q))
        s = lax.dot_general(qz, kv[:, :256], (((1,), (1,)), ((), ())), preferred_element_type=jnp.float32)
        s = jnp.where(same, s * scale, -1e30)
        m = jnp.max(s, axis=-1, keepdims=True)
        p = jnp.exp(s - m)
        l = jnp.sum(p, axis=-1, keepdims=True)
        o = jnp.dot(p.astype(jnp.bfloat16), kv[:, 128:], preferred_element_type=jnp.float32)
        return m, l, o

    chunk = 256

    def branch0(i, carry):
        rows = pl.ds(pl.multiple_of(i * chunk, chunk), chunk)
        q = q_ref[rows]
        kv = kv_ref[...]
        same = sq_ref[rows] == sk_ref[0]
        mm = ll = oo = None
        for j in range(heads):
            m, l, o = attend(q, j, kv, same)
            if j == 0:
                mm = jnp.broadcast_to(m, (chunk, 256))
                ll = jnp.broadcast_to(l, (chunk, 256))
                oo = o
            else:
                pick = o_lane == j
                mm = jnp.where(pick, m, mm)
                ll = jnp.where(pick, l, ll)
                oo = jnp.where(pick, o, oo)
        m_acc[rows] = mm
        l_acc[rows] = ll
        out_ref[rows] = oo
        return carry

    lax.fori_loop(0, LOCAL // chunk, branch0, 0)

    for b, (count, group) in enumerate(BRANCHES):
        locals_[b].wait()
        pltpu.make_async_copy(window(b, 0, (group - 1) * count), window(b, 0, (group - 1) * count), recv_sem.at[b]).wait()

        def branch(j, carry, b=b, count=count):
            start = j * 256 + (hy * 64 if b >= 1 else 0)
            rows = pl.ds(pl.multiple_of(start, 16), count)
            same = sq_ref[rows] == sk_ref[1 + b * heads + j]
            m_new, l_new, o_new = attend(q_ref[rows], j, bufs[b][...], same)
            m_old = m_acc[rows]
            mn = jnp.maximum(m_old, m_new)
            keep_old = jnp.exp(m_old - mn)
            keep_new = jnp.exp(m_new - mn)
            pick = o_lane == j
            m_acc[rows] = jnp.where(pick, mn, m_old)
            l_acc[rows] = jnp.where(pick, l_acc[rows] * keep_old + l_new * keep_new, l_acc[rows])
            out_ref[rows] = jnp.where(pick, out_ref[rows] * keep_old + o_new * keep_new, out_ref[rows])
            return carry

        lax.fori_loop(0, heads, branch, 0)

    def finish(i, carry):
        rows = pl.ds(pl.multiple_of(i * chunk, chunk), chunk)
        out_ref[rows] = out_ref[rows] / l_acc[rows]
        return carry

    lax.fori_loop(0, LOCAL // chunk, finish, 0)

    for b, (count, group) in enumerate(BRANCHES):
        pltpu.make_async_copy(window(b, 0, (group - 1) * count), window(b, 0, (group - 1) * count), send_sem.at[b]).wait()


def head_sum(x):
    for mask in (1, 2):
        x = x + lax.ppermute(x, "head", [(i, i ^ mask) for i in range(4)])
    return x


def per_device(queries, keys, values, slide_lengths, norm_gain, norm_bias):
    heads = queries.shape[0] // HD
    width = heads * HD
    seq = lax.axis_index("seq")
    hy = lax.axis_index("head")
    slide_ends = jnp.cumsum(slide_lengths)
    q = to_token_major(jnp.concatenate([queries, jnp.zeros((256 - width, LOCAL), queries.dtype)]))
    kv = to_token_major(jnp.concatenate([keys, values]))
    kv_lane = jnp.arange(2 * width) % width // HD

    positions = [pos_of(seq, jnp.arange(LOCAL))]
    sends = []
    for b, (count, group) in enumerate(BRANCHES):
        starts = [j * 256 + (hy * 64 if b >= 1 else 0) for j in range(heads)]
        chunk = jnp.zeros((count, 2 * width), kv.dtype)
        for j in range(heads):
            piece = lax.dynamic_slice_in_dim(kv, starts[j], count, 0)
            chunk = jnp.where(kv_lane[None, :] == j, piece, chunk)
        sends.append(chunk)
        first = seq // group * group
        members = first + jnp.arange(group)
        for j in range(heads):
            idx = starts[j] + jnp.arange(count)
            positions.append(pos_of(members[:, None], idx[None, :]).reshape(group * count))
    slides = slide_of(jnp.stack(positions), slide_ends)

    vmem = pl.BlockSpec(memory_space=pltpu.VMEM)
    acc = pl.pallas_call(
        attention_kernel,
        out_shape=jax.ShapeDtypeStruct((LOCAL, 256), jnp.float32),
        in_specs=[vmem] * 7,
        out_specs=vmem,
        scratch_shapes=[
            pltpu.VMEM((LOCAL, 2 * width), jnp.bfloat16),
            pltpu.VMEM((LOCAL, 2 * width), jnp.bfloat16),
            pltpu.VMEM((LOCAL, 2 * width), jnp.bfloat16),
            pltpu.VMEM((LOCAL, 256), jnp.float32),
            pltpu.VMEM((LOCAL, 256), jnp.float32),
            pltpu.SemaphoreType.DMA((3,)),
            pltpu.SemaphoreType.DMA((3,)),
            pltpu.SemaphoreType.DMA((3,)),
        ],
        compiler_params=pltpu.CompilerParams(
            collective_id=0, has_side_effects=True, vmem_limit_bytes=60 * 1024 * 1024
        ),
    )(q, kv, *sends, slides[0].reshape(LOCAL, 1), slides.reshape(-1, 1, LOCAL))

    attended = acc[:, SHIFT : SHIFT + width]
    feats = jnp.sum(attended, axis=1)
    squares = jnp.sum(attended * attended, axis=1)
    sums = head_sum(jnp.stack([feats, squares]))
    mean = sums[0] / D
    var = sums[1] / D - mean * mean
    normed = (attended - mean[:, None]) * lax.rsqrt(var + 1e-05)[:, None]
    out = (normed * norm_gain[None, :] + norm_bias[None, :]).astype(jnp.bfloat16)
    return from_token_major(out)


def solution(mesh):
    placed = (P("head", "seq"),) * 3 + (P(), P("head"), P("head"))
    return jax.shard_map(
        per_device, mesh=mesh, in_specs=placed, out_specs=P("head", "seq"), check_vma=False
    )
```

time: 157 us -> 67.8 us (0.43)
  the two profiles are of different devices: /device:TPU:70 before, /device:TPU:4 now
where the time goes in v4:
time: 67.8 us; the launch traced here: 67.3 us
  Pallas kernels  42.6 us (63%)
  local copies, waits for them, and re-layouts  8.37 us (12%)
  other arithmetic  7.02 us (10%)
  starting transfers between devices  4.94 us (7%)
  waiting for transfers between devices  4.03 us (6%)
    pallas_call x1, Pallas kernels, per_device(): pl.pallas_call(attention_kernel, out_shape=jax.ShapeDtypeStruct((LOCAL, 2...  42.6 us
    ppermute x2, starting transfers between devices, head_sum(): x = x + lax.ppermute(x, 'head', [(i, i ^ mask) for i in range(4)])  4.94 us
    ppermute x2, waiting for transfers between devices, head_sum(): x = x + lax.ppermute(x, 'head', [(i, i ^ mask) for i in range(4)])  4.03 us
    select_n x3, other arithmetic, per_device(): chunk = jnp.where(kv_lane[None, :] == j, piece, chunk)  2.07 us
    reduce_sum x1, other arithmetic, per_device(): feats = jnp.sum(attended, axis=1)  1.96 us
    dynamic_slice x5, local copies, waits for them, and re-layouts, per_device(): piece = lax.dynamic_slice_in_dim(kv, starts[j], count, 0)  1.61 us
    transpose x2, local copies, waits for them, and re-layouts, to_token_major(): x = jnp.transpose(x, (4, 3, 2, 1, 0))  1.56 us
  transfers between devices with their start and end apart: 2, of which 2 were waited for; matrix products, arithmetic and copies ran while one was open for 0% of the time, Pallas kernels for 0%

profile of v4, /device:TPU:4, one launch (start us, length us, event | category | flops | bytes accessed | tf_op | source)
XLA Modules:
  0.0 67.3 jit_solution(12618862034156892736)
XLA Ops:
  0.0 1.2 %pad_maximum_fusion = bf16[384,1024]{1,0:T(8,128)(2,1)S(1)} fusion(bf16[192,1024]{1,0:T(8,128)(2,1)} %param.8, bf16[192,1024]{1,0:T(8,128)(2,1)} %param.7), kind=kLoop, calls=%fused_computation.4 | loop fusion | flops 1572864 | bytes 1572864 | tf_op jit(solution)/shard_map/concatenate | solution.py:176
  1.2 0.4 copy.25
  1.5 0.2 reshape.2425
  1.7 0.5 copy.26
  2.2 0.0 copy-start.5
  2.2 1.1 %fusion.125 = (bf16[1,4,4,16,384]{4,0,1,2,3:T(2,128)(2,1)S(1)}, bf16[1,4,4,16,384]{4,0,1,2,3:T(2,128)(2,1)S(1)}, bf16[1,4,4,16,384]{4,0,1,2,3:T(2,128)(2,1)S(1)}, bf16[1,4,4,16,384]{4,0,1,2,3:T(2,128)(2,1)S(1)}) fusion(bf16[4,4,4,16,384]{4,0,1,2,3:T(4,128)(2,1)S(1)} %bitcast.52), kind=kLoop, calls=%fused_computation.392 | loop fusion | bytes 1572864 | tf_op jit(solution)/shard_map/dynamic_slice | solution.py:185
  3.3 0.0 copy-start.2
  3.4 0.7 select_select_fusion.s2_ref
  4.1 0.6 select_select_fusion.1.s3_ref
  4.9 0.1 add_bitcast_fusion
  5.1 0.1 broadcast_add_fusion.4
  5.2 0.1 add.1526
  5.2 0.1 add.1537
  5.3 0.1 add.1548
  5.4 0.1 add.1559
  5.5 0.1 broadcast_add_fusion
  5.6 0.1 add.1573
  5.6 0.1 add.1584
  5.7 0.1 add.1595
  5.8 0.1 add.1606
  5.9 0.1 copy.31
  6.0 0.1 reduce-window.8
  6.1 0.1 reduce
  6.2 0.1 stack.13
  6.3 0.5 convert_reduce_fusion
  6.8 0.7 reshape.2429.sk_ref
  7.5 0.2 copy.35
  7.7 0.1 concatenate.6.clone
  7.8 0.1 reshape.2423
  7.9 1.1 %copy.24 = bf16[4,4,4,16,256]{4,3,2,1,0:T(8,128)(2,1)} copy(bf16[4,4,4,16,256]{4,0,1,2,3:T(4,128)(2,1)S(1)} %bitcast.58) | data formatting | bytes 1048576 | tf_op jit(solution)/shard_map/transpose | solution.py:22
  9.0 0.1 copy.30
  9.1 0.1 copy.29
  9.3 0.1 copy.28
  9.4 0.1 copy.27
  9.5 1.0 %copy.32.sq_ref = s32[1024,1]{1,0:T(8,128)} copy(s32[1024,1]{0,1:T(1,128)S(1)} %slice_bitcast_fusion) | data formatting | bytes 8192 | tf_op jit(solution)/shard_map/reshape;squeeze | solution.py:214
  10.5 0.8 %fusion.2.s1_ref = bf16[256,384]{1,0:T(8,128)(2,1)} fusion(bf16[1,4,4,16,384]{4,3,2,1,0:T(8,128)(2,1)S(1)} %copy.30, bf16[1,4,4,16,384]{4,3,2,1,0:T(8,128)(2,1)S(1)} %copy.29, bf16[1,4,4,16,384]{4,3,2,1,0:T(8,128)(2,1)S(1)} %copy.28, bf16[1,4,4,16,384]{4,3,2,1,0:T(8,128)(2,1)S(1)} %copy.27, pred[384]{0:T(512)(128)(4,1)S(1)} %get-tuple-element.32, ...), kind=kLoop, calls=%fused_computation.9 | loop fusion | flops 393216 | bytes 984576 | tf_op jit(solution)/shard_map/jit(_where)/select_n | solution.py:186
  11.3 42.6 %shard_map.64 = f32[1024,256]{1,0:T(8,128)} custom-call(bf16[1024,256]{1,0:T(8,128)(2,1)} %bitcast.56, bf16[1024,384]{1,0:T(8,128)(2,1)} %bitcast.55, bf16[256,384]{1,0:T(8,128)(2,1)} %fusion.2.s1_ref, bf16[64,384]{1,0:T(8,128)(2,1)} %select_select_fusion.s2_ref, bf16[16,384]{1,0:T(8,128)(2,1)} %select_select_fusion.1.s3_ref, s32[1024,1]{1,0:T(8,128)} %copy.32.sq_ref, ...), custom_call_target="tpu_custom_call" | custom-call | tf_op jit(solution)/shard_map/pallas_call | solution.py:196
  53.9 0.0 copy-start.3
  54.0 0.0 copy-start.4
  54.0 2.0 %slice_reduce_fusion = (f32[1024]{0:T(1024)S(1)}, f32[1024]{0:T(1024)S(1)}) fusion(f32[1024,256]{1,0:T(8,128)} %shard_map.64), kind=kLoop, calls=%fused_computation.3 | loop fusion | flops 587776 | bytes 794624 | tf_op jit(solution)/shard_map/reduce_sum | solution.py:217
  56.0 1.7 %collective-permute-start = (f32[2,1024]{1,0:T(2,128)S(1)}, f32[2,1024]{1,0:T(2,128)S(1)}, u32[]{:S(2)}, u32[]{:S(2)}) collective-permute-start(f32[2,1024]{1,0:T(2,128)S(1)} %pad_maximum_fusion.1), channel_id=1, source_target_pairs={{0,1},{1,0},{2,3},{3,2},{4,5},{5,4},{6,7},{7,6},{8,9},{9,8},{10,11... | collective-permute-start | bytes 24584 | tf_op jit(solution)/shard_map/ppermute | solution.py:165
  57.6 2.1 %collective-permute-done = f32[2,1024]{1,0:T(2,128)S(1)} collective-permute-done((f32[2,1024]{1,0:T(2,128)S(1)}, f32[2,1024]{1,0:T(2,128)S(1)}, u32[]{:S(2)}, u32[]{:S(2)}) %collective-permute-start) | collective-permute-done | bytes 8224 | tf_op jit(solution)/shard_map/ppermute | solution.py:165
  59.7 3.3 %collective-permute-start.1 = (f32[2,1024]{1,0:T(2,128)S(1)}, f32[2,1024]{1,0:T(2,128)S(1)}, u32[]{:S(2)}, u32[]{:S(2)}) collective-permute-start(f32[2,1024]{1,0:T(2,128)S(1)} %fusion.124), channel_id=1, source_target_pairs={{0,2},{1,3},{2,0},{3,1},{4,6},{5,7},{6,4},{7,5},{8,10},{9,11},{10,... | collective-permute-start | bytes 24584 | tf_op jit(solution)/shard_map/ppermute | solution.py:165
  63.0 2.0 %collective-permute-done.1 = f32[2,1024]{1,0:T(2,128)S(1)} collective-permute-done((f32[2,1024]{1,0:T(2,128)S(1)}, f32[2,1024]{1,0:T(2,128)S(1)}, u32[]{:S(2)}, u32[]{:S(2)}) %collective-permute-start.1) | collective-permute-done | bytes 8224 | tf_op jit(solution)/shard_map/ppermute | solution.py:165
  65.0 0.6 add_convert_fusion
  65.7 0.4 copy.41
  66.1 0.3 reshape.2431
  66.4 0.9 %copy.34 = bf16[192,1024]{1,0:T(8,128)(2,1)} copy(bf16[192,1024]{0,1:T(8,128)(2,1)S(1)} %reshape.2431) | data formatting | bytes 786432 | tf_op jit(solution)/shard_map/reshape | solution.py:30
  (30 shorter events, 0.3 us)
Async XLA Ops:
  2.2 1.9 %copy-start.1 = (bf16[4,4,4,16,384]{4,3,2,1,0:T(8,128)(2,1)}, bf16[4,4,4,16,384]{4,3,2,1,0:T(8,128)(2,1)S(1)}, u32[]{:S(2)}) copy-start(bf16[4,4,4,16,384]{4,3,2,1,0:T(8,128)(2,1)S(1)} %copy.26) | copy-start | bytes 2359300
  2.2 3.7 %copy-start.5 = (s32[64]{0:T(128)S(1)}, s32[64]{0:T(128)}, u32[]{:S(2)}) copy-start(s32[64]{0:T(128)} %param.9) | copy-start | bytes 772
  3.3 4.1 %copy-start.2 = (bf16[192,1024]{1,0:T(8,128)(2,1)S(1)}, bf16[192,1024]{1,0:T(8,128)(2,1)}, u32[]{:S(2)}) copy-start(bf16[192,1024]{1,0:T(8,128)(2,1)} %param.6) | copy-start | bytes 1179652
  53.9 11.1 %copy-start = (f32[1024,256]{1,0:T(8,128)S(1)}, f32[1024,256]{1,0:T(8,128)}, u32[]{:S(2)}) copy-start(f32[1024,256]{1,0:T(8,128)} %shard_map.64) | copy-start | bytes 3145732
  53.9 11.1 %copy-start.3 = (f32[192]{0:T(256)S(1)}, f32[192]{0:T(256)}, u32[]{:S(2)}) copy-start(f32[192]{0:T(256)} %param.11) | copy-start | bytes 2308
  54.0 11.1 %copy-start.4 = (f32[192]{0:T(256)S(1)}, f32[192]{0:T(256)}, u32[]{:S(2)}) copy-start(f32[192]{0:T(256)} %param.10) | copy-start | bytes 2308
  56.0 3.7 %collective-permute-start = (f32[2,1024]{1,0:T(2,128)S(1)}, f32[2,1024]{1,0:T(2,128)S(1)}, u32[]{:S(2)}, u32[]{:S(2)}) collective-permute-start(f32[2,1024]{1,0:T(2,128)S(1)} %pad_maximum_fusion.1), channel_id=1, source_target_pairs={{0,1},{1,0},{2,3},{3,2},{4,5},{5,4},{6,7},{7,6},{8,9},{9,8},{10,11... | collective-permute-start | bytes 24584 | tf_op jit(solution)/shard_map/ppermute | solution.py:165
  59.7 5.2 %collective-permute-start.1 = (f32[2,1024]{1,0:T(2,128)S(1)}, f32[2,1024]{1,0:T(2,128)S(1)}, u32[]{:S(2)}, u32[]{:S(2)}) collective-permute-start(f32[2,1024]{1,0:T(2,128)S(1)} %fusion.124), channel_id=1, source_target_pairs={{0,2},{1,3},{2,0},{3,1},{4,6},{5,7},{6,4},{7,5},{8,10},{9,11},{10,... | collective-permute-start | bytes 24584 | tf_op jit(solution)/shard_map/ppermute | solution.py:165

commit v5 on v4

--- a/solution.py
+++ b/solution.py
@@ -42,7 +42,7 @@
 def attention_kernel(
     q_ref, kv_ref, s1_ref, s2_ref, s3_ref, sq_ref, sk_ref,
     out_ref,
-    kv1, kv2, kv3, m_acc, l_acc, send_sem, recv_sem, local_sem,
+    kv1, kv2, kv3, m_acc, l_acc, send_sem, recv_sem, local_sem, fwd_send, fwd_recv,
 ):
     heads = 4
     me = lax.axis_index("seq")
@@ -62,24 +62,27 @@
     lax.fori_loop(1, devices, greet, 0)
     pl.semaphore_wait(barrier, devices - 1)
 
-    def window(b, start, rows):
-        return bufs[b].at[pl.ds(pl.multiple_of(start, 16), rows), :]
-
+    def slot(b, half, pair):
+        return bufs[b].at[pair, half]
+
+    sibling = me + 1 - 2 * (me % 2)
+    side = me % 2
     locals_ = []
     for b, (count, group) in enumerate(BRANCHES):
         member = lax.rem(me, group)
-        cp = pltpu.make_async_copy(sends[b], window(b, member * count, count), local_sem.at[b])
+        cp = pltpu.make_async_copy(sends[b], slot(b, side, member // 2), local_sem.at[b])
         cp.start()
         locals_.append(cp)
     for b, (count, group) in enumerate(BRANCHES):
         member = lax.rem(me, group)
         first = me - member
-
-        def push(o, carry, b=b, count=count, group=group, member=member, first=first):
-            target = first + lax.rem(member + o, group)
+        pairs = group // 2
+
+        def push(o, carry, b=b, pairs=pairs, member=member, first=first):
+            target = first + 2 * lax.rem(member // 2 + o, pairs) + side
             pltpu.make_async_remote_copy(
                 src_ref=sends[b],
-                dst_ref=window(b, member * count, count),
+                dst_ref=slot(b, side, member // 2),
                 send_sem=send_sem.at[b],
                 recv_sem=recv_sem.at[b],
                 device_id=(target, hy),
@@ -87,7 +90,7 @@
             ).start()
             return carry
 
-        lax.fori_loop(1, group, push, 0)
+        lax.fori_loop(1, pairs, push, 0)
 
     q_lane = lax.broadcasted_iota(jnp.int32, (1, 256), 1) // HD
     o_lane = (lax.broadcasted_iota(jnp.int32, (1, 256), 1) - SHIFT) // HD
@@ -128,15 +131,33 @@
 
     lax.fori_loop(0, LOCAL // chunk, branch0, 0)
 
-    for b, (count, group) in enumerate(BRANCHES):
+    forwards = []
+    for b, (count, group) in enumerate(BRANCHES):
+        pairs = group // 2
         locals_[b].wait()
-        pltpu.make_async_copy(window(b, 0, (group - 1) * count), window(b, 0, (group - 1) * count), recv_sem.at[b]).wait()
+        if pairs > 1:
+            got = bufs[b].at[pl.ds(0, pairs - 1), side]
+            pltpu.make_async_copy(got, got, recv_sem.at[b]).wait()
+        cp = pltpu.make_async_remote_copy(
+            src_ref=bufs[b].at[:, side],
+            dst_ref=bufs[b].at[:, side],
+            send_sem=fwd_send.at[b],
+            recv_sem=fwd_recv.at[b],
+            device_id=(sibling, hy),
+            device_id_type=MESH,
+        )
+        cp.start()
+        forwards.append(cp)
+
+    for b, (count, group) in enumerate(BRANCHES):
+        other = bufs[b].at[:, 1 - side]
+        pltpu.make_async_copy(other, other, fwd_recv.at[b]).wait()
 
         def branch(j, carry, b=b, count=count):
             start = j * 256 + (hy * 64 if b >= 1 else 0)
             rows = pl.ds(pl.multiple_of(start, 16), count)
             same = sq_ref[rows] == sk_ref[1 + b * heads + j]
-            m_new, l_new, o_new = attend(q_ref[rows], j, bufs[b][...], same)
+            m_new, l_new, o_new = attend(q_ref[rows], j, bufs[b][...].reshape(LOCAL, 2 * width), same)
             m_old = m_acc[rows]
             mn = jnp.maximum(m_old, m_new)
             keep_old = jnp.exp(m_old - mn)
@@ -157,7 +178,11 @@
     lax.fori_loop(0, LOCAL // chunk, finish, 0)
 
     for b, (count, group) in enumerate(BRANCHES):
-        pltpu.make_async_copy(window(b, 0, (group - 1) * count), window(b, 0, (group - 1) * count), send_sem.at[b]).wait()
+        pairs = group // 2
+        if pairs > 1:
+            went = bufs[b].at[pl.ds(0, pairs - 1), side]
+            pltpu.make_async_copy(went, went, send_sem.at[b]).wait()
+        forwards[b].wait_send()
 
 
 def head_sum(x):
@@ -199,11 +224,11 @@
         in_specs=[vmem] * 7,
         out_specs=vmem,
         scratch_shapes=[
-            pltpu.VMEM((LOCAL, 2 * width), jnp.bfloat16),
-            pltpu.VMEM((LOCAL, 2 * width), jnp.bfloat16),
-            pltpu.VMEM((LOCAL, 2 * width), jnp.bfloat16),
+            *[pltpu.VMEM((group // 2, 2, count, 2 * width), jnp.bfloat16) for count, group in BRANCHES],
             pltpu.VMEM((LOCAL, 256), jnp.float32),
             pltpu.VMEM((LOCAL, 256), jnp.float32),
+            pltpu.SemaphoreType.DMA((3,)),
+            pltpu.SemaphoreType.DMA((3,)),
             pltpu.SemaphoreType.DMA((3,)),
             pltpu.SemaphoreType.DMA((3,)),
             pltpu.SemaphoreType.DMA((3,)),

time: 67.8 us -> 62.2 us (0.917)
  Pallas kernels: 42.6 us -> 36.8 us
    pallas_call x1, Pallas kernels: 42.6 us -> 36.8 us  [per_device(): pl.pallas_call(attention_kernel, out_shape=jax.ShapeDtypeStruct((LOCAL, 2...]
where the time goes in v5:
time: 62.2 us; the launch traced here: 61.5 us
  Pallas kernels  36.8 us (59%)
  local copies, waits for them, and re-layouts  8.37 us (13%)
  other arithmetic  7.02 us (11%)
  starting transfers between devices  4.95 us (8%)
  waiting for transfers between devices  4.03 us (6%)
    pallas_call x1, Pallas kernels, per_device(): pl.pallas_call(attention_kernel, out_shape=jax.ShapeDtypeStruct((LOCAL, 2...  36.8 us
    ppermute x2, starting transfers between devices, head_sum(): x = x + lax.ppermute(x, 'head', [(i, i ^ mask) for i in range(4)])  4.95 us
    ppermute x2, waiting for transfers between devices, head_sum(): x = x + lax.ppermute(x, 'head', [(i, i ^ mask) for i in range(4)])  4.03 us
    select_n x3, other arithmetic, per_device(): chunk = jnp.where(kv_lane[None, :] == j, piece, chunk)  2.07 us
    reduce_sum x1, other arithmetic, per_device(): feats = jnp.sum(attended, axis=1)  1.96 us
    dynamic_slice x5, local copies, waits for them, and re-layouts, per_device(): piece = lax.dynamic_slice_in_dim(kv, starts[j], count, 0)  1.61 us
    transpose x2, local copies, waits for them, and re-layouts, to_token_major(): x = jnp.transpose(x, (4, 3, 2, 1, 0))  1.56 us
    reshape x2, local copies, waits for them, and re-layouts, from_token_major(): return x.reshape(f, LOCAL)  1.25 us
  transfers between devices with their start and end apart: 2, of which 2 were waited for; matrix products, arithmetic and copies ran while one was open for 0% of the time, Pallas kernels for 0%

profile of v5, /device:TPU:4, one launch (start us, length us, event | category | flops | bytes accessed | tf_op | source)
XLA Modules:
  0.0 61.5 jit_solution(11892922017525802551)
XLA Ops:
  0.0 1.2 %pad_maximum_fusion = bf16[384,1024]{1,0:T(8,128)(2,1)S(1)} fusion(bf16[192,1024]{1,0:T(8,128)(2,1)} %param.8, bf16[192,1024]{1,0:T(8,128)(2,1)} %param.7), kind=kLoop, calls=%fused_computation.4 | loop fusion | flops 1572864 | bytes 1572864 | tf_op jit(solution)/shard_map/concatenate | solution.py:201
  1.2 0.4 copy.25
  1.5 0.2 reshape.2425
  1.7 0.5 copy.26
  2.2 0.0 copy-start.5
  2.2 1.1 %fusion.125 = (bf16[1,4,4,16,384]{4,0,1,2,3:T(2,128)(2,1)S(1)}, bf16[1,4,4,16,384]{4,0,1,2,3:T(2,128)(2,1)S(1)}, bf16[1,4,4,16,384]{4,0,1,2,3:T(2,128)(2,1)S(1)}, bf16[1,4,4,16,384]{4,0,1,2,3:T(2,128)(2,1)S(1)}) fusion(bf16[4,4,4,16,384]{4,0,1,2,3:T(4,128)(2,1)S(1)} %bitcast.52), kind=kLoop, calls=%fused_computation.392 | loop fusion | bytes 1572864 | tf_op jit(solution)/shard_map/dynamic_slice | solution.py:210
  3.3 0.0 copy-start.2
  3.4 0.7 %select_select_fusion.s2_ref = bf16[64,384]{1,0:T(8,128)(2,1)} fusion(bf16[1024,384]{1,0:T(8,128)(2,1)S(1)} %bitcast.53, s32[]{:T(128)S(6)} %select_n.847, s32[]{:T(128)S(6)} %select_n.846, s32[]{:T(128)S(6)} %select_n.845, s32[]{:T(128)S(6)} %select_n.844, pred[384]{0:T(512)(128)(4,1)S(1)} %get-tuple-element.32, pred[384]{0:T(512)(128)(4,1)S(1)} %get-tuple-element.31, ...), kind=kLoop, calls=%fused_computation.10 | loop fusion | flops 98304 | bytes 247312 | tf_op jit(solution)/shard_map/jit(_where)/select_n | solution.py:211
  4.1 0.6 select_select_fusion.1.s3_ref
  4.9 0.1 add_bitcast_fusion
  5.1 0.1 broadcast_add_fusion.4
  5.2 0.1 add.1526
  5.2 0.1 add.1537
  5.3 0.1 add.1548
  5.4 0.1 add.1559
  5.5 0.1 broadcast_add_fusion
  5.6 0.1 add.1573
  5.6 0.1 add.1584
  5.7 0.1 add.1595
  5.8 0.1 add.1606
  5.9 0.1 copy.31
  6.0 0.1 reduce-window.8
  6.1 0.1 reduce
  6.2 0.1 stack.13
  6.3 0.5 convert_reduce_fusion
  6.8 0.7 %reshape.2429.sk_ref = s32[13,1,1024]{2,1,0:T(1,128)} reshape(s32[13,1024]{1,0:T(8,128)S(1)} %convert_reduce_fusion) | data formatting | bytes 106496 | tf_op jit(solution)/shard_map/reshape | solution.py:239
  7.5 0.2 copy.35
  7.7 0.1 concatenate.6.clone
  7.8 0.1 reshape.2423
  7.9 1.1 %copy.24 = bf16[4,4,4,16,256]{4,3,2,1,0:T(8,128)(2,1)} copy(bf16[4,4,4,16,256]{4,0,1,2,3:T(4,128)(2,1)S(1)} %bitcast.58) | data formatting | bytes 1048576 | tf_op jit(solution)/shard_map/transpose | solution.py:22
  9.0 0.1 copy.30
  9.1 0.1 copy.29
  9.3 0.1 copy.28
  9.4 0.1 copy.27
  9.5 1.0 %copy.32.sq_ref = s32[1024,1]{1,0:T(8,128)} copy(s32[1024,1]{0,1:T(1,128)S(1)} %slice_bitcast_fusion) | data formatting | bytes 8192 | tf_op jit(solution)/shard_map/reshape;squeeze | solution.py:239
  10.5 0.8 %fusion.2.s1_ref = bf16[256,384]{1,0:T(8,128)(2,1)} fusion(bf16[1,4,4,16,384]{4,3,2,1,0:T(8,128)(2,1)S(1)} %copy.30, bf16[1,4,4,16,384]{4,3,2,1,0:T(8,128)(2,1)S(1)} %copy.29, bf16[1,4,4,16,384]{4,3,2,1,0:T(8,128)(2,1)S(1)} %copy.28, bf16[1,4,4,16,384]{4,3,2,1,0:T(8,128)(2,1)S(1)} %copy.27, pred[384]{0:T(512)(128)(4,1)S(1)} %get-tuple-element.32, ...), kind=kLoop, calls=%fused_computation.9 | loop fusion | flops 393216 | bytes 984576 | tf_op jit(solution)/shard_map/jit(_where)/select_n | solution.py:211
  11.3 36.8 %shard_map.64 = f32[1024,256]{1,0:T(8,128)} custom-call(bf16[1024,256]{1,0:T(8,128)(2,1)} %bitcast.56, bf16[1024,384]{1,0:T(8,128)(2,1)} %bitcast.55, bf16[256,384]{1,0:T(8,128)(2,1)} %fusion.2.s1_ref, bf16[64,384]{1,0:T(8,128)(2,1)} %select_select_fusion.s2_ref, bf16[16,384]{1,0:T(8,128)(2,1)} %select_select_fusion.1.s3_ref, s32[1024,1]{1,0:T(8,128)} %copy.32.sq_ref, ...), custom_call_target="tpu_custom_call" | custom-call | tf_op jit(solution)/shard_map/pallas_call | solution.py:221
  48.1 0.0 copy-start.3
  48.1 0.0 copy-start.4
  48.1 2.0 %slice_reduce_fusion = (f32[1024]{0:T(1024)S(1)}, f32[1024]{0:T(1024)S(1)}) fusion(f32[1024,256]{1,0:T(8,128)} %shard_map.64), kind=kLoop, calls=%fused_computation.3 | loop fusion | flops 587776 | bytes 794624 | tf_op jit(solution)/shard_map/reduce_sum | solution.py:242
  50.1 1.7 %collective-permute-start = (f32[2,1024]{1,0:T(2,128)S(1)}, f32[2,1024]{1,0:T(2,128)S(1)}, u32[]{:S(2)}, u32[]{:S(2)}) collective-permute-start(f32[2,1024]{1,0:T(2,128)S(1)} %pad_maximum_fusion.1), channel_id=1, source_target_pairs={{0,1},{1,0},{2,3},{3,2},{4,5},{5,4},{6,7},{7,6},{8,9},{9,8},{10,11... | collective-permute-start | bytes 24584 | tf_op jit(solution)/shard_map/ppermute | solution.py:190
  51.8 2.1 %collective-permute-done = f32[2,1024]{1,0:T(2,128)S(1)} collective-permute-done((f32[2,1024]{1,0:T(2,128)S(1)}, f32[2,1024]{1,0:T(2,128)S(1)}, u32[]{:S(2)}, u32[]{:S(2)}) %collective-permute-start) | collective-permute-done | bytes 8224 | tf_op jit(solution)/shard_map/ppermute | solution.py:190
  53.9 3.3 %collective-permute-start.1 = (f32[2,1024]{1,0:T(2,128)S(1)}, f32[2,1024]{1,0:T(2,128)S(1)}, u32[]{:S(2)}, u32[]{:S(2)}) collective-permute-start(f32[2,1024]{1,0:T(2,128)S(1)} %fusion.124), channel_id=1, source_target_pairs={{0,2},{1,3},{2,0},{3,1},{4,6},{5,7},{6,4},{7,5},{8,10},{9,11},{10,... | collective-permute-start | bytes 24584 | tf_op jit(solution)/shard_map/ppermute | solution.py:190
  57.1 2.0 %collective-permute-done.1 = f32[2,1024]{1,0:T(2,128)S(1)} collective-permute-done((f32[2,1024]{1,0:T(2,128)S(1)}, f32[2,1024]{1,0:T(2,128)S(1)}, u32[]{:S(2)}, u32[]{:S(2)}) %collective-permute-start.1) | collective-permute-done | bytes 8224 | tf_op jit(solution)/shard_map/ppermute | solution.py:190
  59.2 0.6 %add_convert_fusion = bf16[1024,192]{1,0:T(8,128)(2,1)S(1)} fusion(f32[1024,256]{1,0:T(8,128)S(1)} %copy-done, f32[192]{0:T(256)S(1)} %copy-done.3, f32[192]{0:T(256)S(1)} %copy-done.4, f32[1024]{0:T(1024)S(1)} %add_rsqrt_fusion, f32[1024]{0:T(1024)S(1)} %bitcast.67), kind=kLoop, calls=%fused_computation.1 | loop fusion | flops 983040 | bytes 1189376 | tf_op jit(solution)/shard_map/convert_element_type | solution.py:248
  59.8 0.4 copy.41
  60.2 0.3 reshape.2431
  60.6 0.9 %copy.34 = bf16[192,1024]{1,0:T(8,128)(2,1)} copy(bf16[192,1024]{0,1:T(8,128)(2,1)S(1)} %reshape.2431) | data formatting | bytes 786432 | tf_op jit(solution)/shard_map/reshape | solution.py:30
  (30 shorter events, 0.3 us)
Async XLA Ops:
  2.2 1.9 %copy-start.1 = (bf16[4,4,4,16,384]{4,3,2,1,0:T(8,128)(2,1)}, bf16[4,4,4,16,384]{4,3,2,1,0:T(8,128)(2,1)S(1)}, u32[]{:S(2)}) copy-start(bf16[4,4,4,16,384]{4,3,2,1,0:T(8,128)(2,1)S(1)} %copy.26) | copy-start | bytes 2359300
  2.2 3.7 %copy-start.5 = (s32[64]{0:T(128)S(1)}, s32[64]{0:T(128)}, u32[]{:S(2)}) copy-start(s32[64]{0:T(128)} %param.9) | copy-start | bytes 772
  3.3 4.1 %copy-start.2 = (bf16[192,1024]{1,0:T(8,128)(2,1)S(1)}, bf16[192,1024]{1,0:T(8,128)(2,1)}, u32[]{:S(2)}) copy-start(bf16[192,1024]{1,0:T(8,128)(2,1)} %param.6) | copy-start | bytes 1179652
  48.1 11.1 %copy-start = (f32[1024,256]{1,0:T(8,128)S(1)}, f32[1024,256]{1,0:T(8,128)}, u32[]{:S(2)}) copy-start(f32[1024,256]{1,0:T(8,128)} %shard_map.64) | copy-start | bytes 3145732
  48.1 11.1 %copy-start.3 = (f32[192]{0:T(256)S(1)}, f32[192]{0:T(256)}, u32[]{:S(2)}) copy-start(f32[192]{0:T(256)} %param.11) | copy-start | bytes 2308
  48.1 11.1 %copy-start.4 = (f32[192]{0:T(256)S(1)}, f32[192]{0:T(256)}, u32[]{:S(2)}) copy-start(f32[192]{0:T(256)} %param.10) | copy-start | bytes 2308
  50.1 3.7 %collective-permute-start = (f32[2,1024]{1,0:T(2,128)S(1)}, f32[2,1024]{1,0:T(2,128)S(1)}, u32[]{:S(2)}, u32[]{:S(2)}) collective-permute-start(f32[2,1024]{1,0:T(2,128)S(1)} %pad_maximum_fusion.1), channel_id=1, source_target_pairs={{0,1},{1,0},{2,3},{3,2},{4,5},{5,4},{6,7},{7,6},{8,9},{9,8},{10,11... | collective-permute-start | bytes 24584 | tf_op jit(solution)/shard_map/ppermute | solution.py:190
  53.9 5.2 %collective-permute-start.1 = (f32[2,1024]{1,0:T(2,128)S(1)}, f32[2,1024]{1,0:T(2,128)S(1)}, u32[]{:S(2)}, u32[]{:S(2)}) collective-permute-start(f32[2,1024]{1,0:T(2,128)S(1)} %fusion.124), channel_id=1, source_target_pairs={{0,2},{1,3},{2,0},{3,1},{4,6},{5,7},{6,4},{7,5},{8,10},{9,11},{10,... | collective-permute-start | bytes 24584 | tf_op jit(solution)/shard_map/ppermute | solution.py:190

commit v6 on v5

--- a/solution.py
+++ b/solution.py
@@ -40,9 +40,10 @@
 
 
 def attention_kernel(
-    q_ref, kv_ref, s1_ref, s2_ref, s3_ref, sq_ref, sk_ref,
+    q_ref, kv_ref, s1_ref, s2_ref, s3_ref, sq_ref, sk_ref, gain_ref, bias_ref,
     out_ref,
-    kv1, kv2, kv3, m_acc, l_acc, send_sem, recv_sem, local_sem, fwd_send, fwd_recv,
+    kv1, kv2, kv3, m_acc, l_acc, o_acc, stats, ybuf, cols,
+    send_sem, recv_sem, local_sem, fwd_send, fwd_recv, y_send, y_recv,
 ):
     heads = 4
     me = lax.axis_index("seq")
@@ -60,7 +61,10 @@
         return carry
 
     lax.fori_loop(1, devices, greet, 0)
-    pl.semaphore_wait(barrier, devices - 1)
+    ys = lax.axis_size("head")
+    for o in range(1, ys):
+        pl.semaphore_signal(barrier, inc=1, device_id=(me, lax.rem(hy + o, ys)), device_id_type=MESH)
+    pl.semaphore_wait(barrier, devices - 1 + ys - 1)
 
     def slot(b, half, pair):
         return bufs[b].at[pair, half]
@@ -126,7 +130,7 @@
                 oo = jnp.where(pick, o, oo)
         m_acc[rows] = mm
         l_acc[rows] = ll
-        out_ref[rows] = oo
+        o_acc[rows] = oo
         return carry
 
     lax.fori_loop(0, LOCAL // chunk, branch0, 0)
@@ -165,17 +169,60 @@
             pick = o_lane == j
             m_acc[rows] = jnp.where(pick, mn, m_old)
             l_acc[rows] = jnp.where(pick, l_acc[rows] * keep_old + l_new * keep_new, l_acc[rows])
-            out_ref[rows] = jnp.where(pick, out_ref[rows] * keep_old + o_new * keep_new, out_ref[rows])
+            o_acc[rows] = jnp.where(pick, o_acc[rows] * keep_old + o_new * keep_new, o_acc[rows])
             return carry
 
         lax.fori_loop(0, heads, branch, 0)
+
+    feature = lax.broadcasted_iota(jnp.int32, (8, 256), 1) >= SHIFT
+    ones = jnp.where(feature, 1.0, 0.0).astype(jnp.float32)
+    first_row = lax.broadcasted_iota(jnp.int32, (8, chunk), 0) == 0
 
     def finish(i, carry):
         rows = pl.ds(pl.multiple_of(i * chunk, chunk), chunk)
-        out_ref[rows] = out_ref[rows] / l_acc[rows]
+        att = o_acc[rows] / l_acc[rows]
+        o_acc[rows] = att
+        dims = (((1,), (1,)), ((), ()))
+        total = lax.dot_general(ones, att, dims, precision=lax.Precision.HIGHEST, preferred_element_type=jnp.float32)
+        square = lax.dot_general(ones, att * att, dims, precision=lax.Precision.HIGHEST, preferred_element_type=jnp.float32)
+        stats[:, rows] = jnp.where(first_row, total, square)
         return carry
 
     lax.fori_loop(0, LOCAL // chunk, finish, 0)
+    ybuf[hy] = stats[...]
+    shares = []
+    for o in range(1, ys):
+        cp = pltpu.make_async_remote_copy(
+            src_ref=stats,
+            dst_ref=ybuf.at[hy],
+            send_sem=y_send.at[o - 1],
+            recv_sem=y_recv.at[0],
+            device_id=(me, lax.rem(hy + o, ys)),
+            device_id_type=MESH,
+        )
+        cp.start()
+        shares.append(cp)
+    arrived = ybuf.at[pl.ds(0, ys - 1)]
+    pltpu.make_async_copy(arrived, arrived, y_recv.at[0]).wait()
+    for cp in shares:
+        cp.wait_send()
+    summed = ybuf[0]
+    for h in range(1, ys):
+        summed = summed + ybuf[h]
+    mean = summed[0:1] / D
+    var = summed[1:2] / D - mean * mean
+    rstd = lax.rsqrt(var + 1e-05)
+    pair = jnp.where(lax.broadcasted_iota(jnp.int32, (8, LOCAL), 0) == 0, mean, rstd)
+    cols[...] = jnp.transpose(pair)
+
+    def normalize(i, carry):
+        rows = pl.ds(pl.multiple_of(i * chunk, chunk), chunk)
+        col = cols[rows]
+        normed = (o_acc[rows] - col[:, 0:1]) * col[:, 1:2]
+        out_ref[rows] = (normed * gain_ref[...] + bias_ref[...]).astype(out_ref.dtype)
+        return carry
+
+    lax.fori_loop(0, LOCAL // chunk, normalize, 0)
 
     for b, (count, group) in enumerate(BRANCHES):
         pairs = group // 2
@@ -183,12 +230,6 @@
             went = bufs[b].at[pl.ds(0, pairs - 1), side]
             pltpu.make_async_copy(went, went, send_sem.at[b]).wait()
         forwards[b].wait_send()
-
-
-def head_sum(x):
-    for mask in (1, 2):
-        x = x + lax.ppermute(x, "head", [(i, i ^ mask) for i in range(4)])
-    return x
 
 
 def per_device(queries, keys, values, slide_lengths, norm_gain, norm_bias):
@@ -217,36 +258,36 @@
             positions.append(pos_of(members[:, None], idx[None, :]).reshape(group * count))
     slides = slide_of(jnp.stack(positions), slide_ends)
 
+    lead = jnp.zeros((SHIFT,), jnp.float32)
+    gain = jnp.concatenate([lead, norm_gain]).reshape(1, 256)
+    bias = jnp.concatenate([lead, norm_bias]).reshape(1, 256)
     vmem = pl.BlockSpec(memory_space=pltpu.VMEM)
-    acc = pl.pallas_call(
+    out = pl.pallas_call(
         attention_kernel,
-        out_shape=jax.ShapeDtypeStruct((LOCAL, 256), jnp.float32),
-        in_specs=[vmem] * 7,
+        out_shape=jax.ShapeDtypeStruct((LOCAL, 256), jnp.bfloat16),
+        in_specs=[vmem] * 9,
         out_specs=vmem,
         scratch_shapes=[
             *[pltpu.VMEM((group // 2, 2, count, 2 * width), jnp.bfloat16) for count, group in BRANCHES],
             pltpu.VMEM((LOCAL, 256), jnp.float32),
             pltpu.VMEM((LOCAL, 256), jnp.float32),
-            pltpu.SemaphoreType.DMA((3,)),
-            pltpu.SemaphoreType.DMA((3,)),
-            pltpu.SemaphoreType.DMA((3,)),
-            pltpu.SemaphoreType.DMA((3,)),
-            pltpu.SemaphoreType.DMA((3,)),
+            pltpu.VMEM((LOCAL, 256), jnp.float32),
+            pltpu.VMEM((8, LOCAL), jnp.float32),
+            pltpu.VMEM((4, 8, LOCAL), jnp.float32),
+            pltpu.VMEM((LOCAL, 8), jnp.float32),
+            pltpu.SemaphoreType.DMA((3,)),
+            pltpu.SemaphoreType.DMA((3,)),
+            pltpu.SemaphoreType.DMA((3,)),
+            pltpu.SemaphoreType.DMA((3,)),
+            pltpu.SemaphoreType.DMA((3,)),
+            pltpu.SemaphoreType.DMA((3,)),
+            pltpu.SemaphoreType.DMA((1,)),
         ],
         compiler_params=pltpu.CompilerParams(
             collective_id=0, has_side_effects=True, vmem_limit_bytes=60 * 1024 * 1024
         ),
-    )(q, kv, *sends, slides[0].reshape(LOCAL, 1), slides.reshape(-1, 1, LOCAL))
-
-    attended = acc[:, SHIFT : SHIFT + width]
-    feats = jnp.sum(attended, axis=1)
-    squares = jnp.sum(attended * attended, axis=1)
-    sums = head_sum(jnp.stack([feats, squares]))
-    mean = sums[0] / D
-    var = sums[1] / D - mean * mean
-    normed = (attended - mean[:, None]) * lax.rsqrt(var + 1e-05)[:, None]
-    out = (normed * norm_gain[None, :] + norm_bias[None, :]).astype(jnp.bfloat16)
-    return from_token_major(out)
+    )(q, kv, *sends, slides[0].reshape(LOCAL, 1), slides.reshape(-1, 1, LOCAL), gain, bias)
+    return from_token_major(out[:, SHIFT : SHIFT + width])
 
 
 def solution(mesh):

time: 62.2 us -> 61 us (0.981)
  Pallas kernels: 36.8 us -> 44.9 us
  starting transfers between devices: 4.95 us -> 0 us
  waiting for transfers between devices: 4.03 us -> 0 us
  other arithmetic: 7.02 us -> 3.27 us
  local copies, waits for them, and re-layouts: 8.37 us -> 12 us
    pallas_call x1, Pallas kernels: 36.8 us -> 44.9 us  [per_device(): pl.pallas_call(attention_kernel, out_shape=jax.ShapeDtypeStruct((LOCAL, 2...]
    ppermute x2 -> x0, starting transfers between devices: 4.95 us -> none  [head_sum(): x = x + lax.ppermute(x, 'head', [(i, i ^ mask) for i in range(4)])]
    ppermute x2 -> x0, waiting for transfers between devices: 4.03 us -> none  [head_sum(): x = x + lax.ppermute(x, 'head', [(i, i ^ mask) for i in range(4)])]
    reduce_sum x1 -> x0, other arithmetic: 1.96 us -> none  [per_device(): feats = jnp.sum(attended, axis=1)]
    concatenate x0 -> x2, local copies, waits for them, and re-layouts: none -> 1.31 us  [the longest x1 0.66 us: per_device(): gain = jnp.concatenate([lead, norm_gain]).reshape(1, 256)]
    slice x0 -> x1, local copies, waits for them, and re-layouts: none -> 1.29 us  [per_device(): return from_token_major(out[:, SHIFT:SHIFT + width])]
    concatenate x1, other arithmetic: 1.17 us -> 0.05 us  [per_device(): kv = to_token_major(jnp.concatenate([keys, values]))]
    unnamed x17, local copies, waits for them, and re-layouts: 0.26 us -> 1.26 us
  transfers between devices with their start and end apart: 2 -> 0, of which waited for: 2 -> 0; matrix products, arithmetic and copies ran while one was open for 0% -> 0% of each run, Pallas kernels for 0% -> 0%
where the time goes in v6:
time: 61 us; the launch traced here: 60.5 us
  Pallas kernels  44.9 us (74%)
  local copies, waits for them, and re-layouts  12 us (20%)
  other arithmetic  3.27 us (5%)
    pallas_call x1, Pallas kernels, per_device(): pl.pallas_call(attention_kernel, out_shape=jax.ShapeDtypeStruct((LOCAL, 2...  44.9 us
    select_n x3, other arithmetic, per_device(): chunk = jnp.where(kv_lane[None, :] == j, piece, chunk)  2.07 us
    dynamic_slice x5, local copies, waits for them, and re-layouts, per_device(): piece = lax.dynamic_slice_in_dim(kv, starts[j], count, 0)  1.61 us
    transpose x2, local copies, waits for them, and re-layouts, to_token_major(): x = jnp.transpose(x, (4, 3, 2, 1, 0))  1.55 us
    slice x1, local copies, waits for them, and re-layouts, per_device(): return from_token_major(out[:, SHIFT:SHIFT + width])  1.29 us
    unnamed x17, local copies, waits for them, and re-layouts  1.26 us
    reshape x2, local copies, waits for them, and re-layouts, from_token_major(): return x.reshape(f, LOCAL)  1.25 us

profile of v6, /device:TPU:4, one launch (start us, length us, event | category | flops | bytes accessed | tf_op | source)
XLA Modules:
  0.0 60.5 jit_solution(13397765010027084493)
XLA Ops:
  0.0 1.2 %copy.35 = bf16[192,1024]{0,1:T(8,128)(2,1)S(1)} copy(bf16[192,1024]{1,0:T(8,128)(2,1)} %param.6) | data formatting | bytes 786432
  1.2 0.1 concatenate.12.clone
  1.3 0.1 reshape.2406
  1.4 0.0 copy-start.1
  1.4 0.0 copy-start.2
  1.5 1.1 %copy.24 = bf16[4,4,4,16,256]{4,3,2,1,0:T(8,128)(2,1)} copy(bf16[4,4,4,16,256]{4,0,1,2,3:T(4,128)(2,1)S(1)} %bitcast.54) | data formatting | bytes 1048576 | tf_op jit(solution)/shard_map/transpose | solution.py:22
  2.5 0.0 copy-done.1
  2.6 0.1 pad_maximum_fusion
  2.6 0.4 copy.25
  3.0 0.2 reshape.2408
  3.2 0.5 copy.26
  3.6 0.0 copy-start
  3.6 1.1 %fusion.124 = (bf16[1,4,4,16,384]{4,0,1,2,3:T(2,128)(2,1)S(1)}, bf16[1,4,4,16,384]{4,0,1,2,3:T(2,128)(2,1)S(1)}, bf16[1,4,4,16,384]{4,0,1,2,3:T(2,128)(2,1)S(1)}, bf16[1,4,4,16,384]{4,0,1,2,3:T(2,128)(2,1)S(1)}) fusion(bf16[4,4,4,16,384]{4,0,1,2,3:T(4,128)(2,1)S(1)} %bitcast.50), kind=kLoop, calls=%fused_computation.384 | loop fusion | bytes 1572864 | tf_op jit(solution)/shard_map/dynamic_slice | solution.py:251
  4.8 0.1 copy.30
  4.9 0.1 copy.29
  5.0 0.1 copy.28
  5.2 0.1 copy.27
  5.3 0.0 copy-start.5
  5.3 0.8 %fusion.2.s1_ref = bf16[256,384]{1,0:T(8,128)(2,1)} fusion(bf16[1,4,4,16,384]{4,3,2,1,0:T(8,128)(2,1)S(1)} %copy.30, bf16[1,4,4,16,384]{4,3,2,1,0:T(8,128)(2,1)S(1)} %copy.29, bf16[1,4,4,16,384]{4,3,2,1,0:T(8,128)(2,1)S(1)} %copy.28, bf16[1,4,4,16,384]{4,3,2,1,0:T(8,128)(2,1)S(1)} %copy.27, pred[384]{0:T(512)(128)(4,1)S(1)} %get-tuple-element.28, ...), kind=kLoop, calls=%fused_computation.6 | loop fusion | flops 393216 | bytes 984576 | tf_op jit(solution)/shard_map/jit(_where)/select_n | solution.py:252
  6.1 0.7 %select_select_fusion.s2_ref = bf16[64,384]{1,0:T(8,128)(2,1)} fusion(bf16[1024,384]{1,0:T(8,128)(2,1)S(1)} %bitcast.51, s32[]{:T(128)S(6)} %select_n.847, s32[]{:T(128)S(6)} %select_n.846, s32[]{:T(128)S(6)} %select_n.845, s32[]{:T(128)S(6)} %select_n.844, pred[384]{0:T(512)(128)(4,1)S(1)} %get-tuple-element.28, pred[384]{0:T(512)(128)(4,1)S(1)} %get-tuple-element.27, ...), kind=kLoop, calls=%fused_computation.7 | loop fusion | flops 98304 | bytes 247312 | tf_op jit(solution)/shard_map/jit(_where)/select_n | solution.py:252
  6.8 0.6 %select_select_fusion.1.s3_ref = bf16[16,384]{1,0:T(8,128)(2,1)} fusion(bf16[1024,384]{1,0:T(8,128)(2,1)S(1)} %bitcast.52, s32[]{:T(128)S(6)} %select_n.847, s32[]{:T(128)S(6)} %select_n.846, s32[]{:T(128)S(6)} %select_n.845, s32[]{:T(128)S(6)} %select_n.844, pred[384]{0:T(512)(128)(4,1)S(1)} %get-tuple-element.28, pred[384]{0:T(512)(128)(4,1)S(1)} %get-tuple-element.27, ...), kind=kLoop, calls=%fused_computation.29 | loop fusion | flops 24576 | bytes 62992 | tf_op jit(solution)/shard_map/jit(_where)/select_n | solution.py:252
  7.5 0.0 copy-start.3
  7.5 0.0 copy-start.4
  7.5 0.1 add_bitcast_fusion
  7.7 0.1 broadcast_add_fusion.4
  7.8 0.1 add.1506
  7.9 0.1 add.1517
  8.0 0.1 add.1528
  8.1 0.1 add.1539
  8.2 0.1 broadcast_add_fusion
  8.3 0.1 add.1553
  8.4 0.1 add.1564
  8.5 0.1 add.1575
  8.6 0.1 add.1586
  8.7 0.1 stack.4
  8.8 0.1 copy.31
  8.9 0.1 reduce-window.8
  9.0 0.1 reduce
  9.1 0.5 convert_reduce_fusion
  9.6 1.0 %copy.32.sq_ref = s32[1024,1]{1,0:T(8,128)} copy(s32[1024,1]{0,1:T(1,128)S(1)} %slice_bitcast_fusion) | data formatting | bytes 8192 | tf_op jit(solution)/shard_map/reshape;squeeze | solution.py:289
  10.6 0.7 %reshape.2412.sk_ref = s32[13,1,1024]{2,1,0:T(1,128)} reshape(s32[13,1024]{1,0:T(8,128)S(1)} %convert_reduce_fusion) | data formatting | bytes 106496 | tf_op jit(solution)/shard_map/reshape | solution.py:289
  11.3 0.7 %concatenate.14 = f32[256]{0:T(256)} pad(f32[192]{0:T(256)S(1)} %copy-done.3, f32[]{:T(128)} %constant.625.clone.1), padding=64_0 | pad | bytes 1796 | tf_op jit(solution)/shard_map/concatenate | solution.py:262
  12.0 0.6 %concatenate.15 = f32[256]{0:T(256)} pad(f32[192]{0:T(256)S(1)} %copy-done.4, f32[]{:T(128)} %constant.625.clone.1), padding=64_0 | pad | bytes 1796 | tf_op jit(solution)/shard_map/concatenate | solution.py:263
  12.6 44.9 %shard_map.64 = bf16[1024,256]{1,0:T(8,128)(2,1)} custom-call(bf16[1024,256]{1,0:T(8,128)(2,1)} %bitcast.57, bf16[1024,384]{1,0:T(8,128)(2,1)} %bitcast.53, bf16[256,384]{1,0:T(8,128)(2,1)} %fusion.2.s1_ref, bf16[64,384]{1,0:T(8,128)(2,1)} %select_select_fusion.s2_ref, bf16[16,384]{1,0:T(8,128)(2,1)} %select_select_fusion.1.s3_ref, s32[1024,1]{1,0:T(8,128)} %copy.32.sq_ref, ...), custom_call_target="tpu_custom_call" | custom-call | tf_op jit(solution)/shard_map/pallas_call | solution.py:265
  57.5 1.3 %slice.11 = bf16[1024,192]{1,0:T(8,128)(2,1)S(1)} slice(bf16[1024,256]{1,0:T(8,128)(2,1)} %shard_map.64), slice={[0:1024], [64:256]} | slice | bytes 786432 | tf_op jit(solution)/shard_map/slice | solution.py:290
  58.8 0.4 copy.41
  59.3 0.3 reshape.2416
  59.6 0.9 %copy.34 = bf16[192,1024]{1,0:T(8,128)(2,1)} copy(bf16[192,1024]{0,1:T(8,128)(2,1)S(1)} %reshape.2416) | data formatting | bytes 786432 | tf_op jit(solution)/shard_map/reshape | solution.py:30
  (22 shorter events, 0.3 us)
Async XLA Ops:
  1.4 1.1 %copy-start.1 = (bf16[192,1024]{1,0:T(8,128)(2,1)S(1)}, bf16[192,1024]{1,0:T(8,128)(2,1)}, u32[]{:S(2)}) copy-start(bf16[192,1024]{1,0:T(8,128)(2,1)} %param.8) | copy-start | bytes 1179652
  1.4 1.1 %copy-start.2 = (bf16[192,1024]{1,0:T(8,128)(2,1)S(1)}, bf16[192,1024]{1,0:T(8,128)(2,1)}, u32[]{:S(2)}) copy-start(bf16[192,1024]{1,0:T(8,128)(2,1)} %param.7) | copy-start | bytes 1179652
  3.6 3.2 %copy-start = (bf16[4,4,4,16,384]{4,3,2,1,0:T(8,128)(2,1)}, bf16[4,4,4,16,384]{4,3,2,1,0:T(8,128)(2,1)S(1)}, u32[]{:S(2)}) copy-start(bf16[4,4,4,16,384]{4,3,2,1,0:T(8,128)(2,1)S(1)} %copy.26) | copy-start | bytes 2359300
  5.3 3.4 %copy-start.5 = (s32[64]{0:T(128)S(1)}, s32[64]{0:T(128)}, u32[]{:S(2)}) copy-start(s32[64]{0:T(128)} %param.9) | copy-start | bytes 772
  7.5 3.8 %copy-start.3 = (f32[192]{0:T(256)S(1)}, f32[192]{0:T(256)}, u32[]{:S(2)}) copy-start(f32[192]{0:T(256)} %param.10) | copy-start | bytes 2308
  7.5 4.4 %copy-start.4 = (f32[192]{0:T(256)S(1)}, f32[192]{0:T(256)}, u32[]{:S(2)}) copy-start(f32[192]{0:T(256)} %param.11) | copy-start | bytes 2308

commit v7 on v6

--- a/solution.py
+++ b/solution.py
@@ -102,12 +102,12 @@
     def attend(q, j, kv, same):
         qz = jnp.where(q_lane == j, q, jnp.zeros_like(q))
         s = lax.dot_general(qz, kv[:, :256], (((1,), (1,)), ((), ())), preferred_element_type=jnp.float32)
-        s = jnp.where(same, s * scale, -1e30)
+        s = jnp.where(same, s, -1e30)
         m = jnp.max(s, axis=-1, keepdims=True)
-        p = jnp.exp(s - m)
+        p = jnp.exp((s - m) * scale)
         l = jnp.sum(p, axis=-1, keepdims=True)
         o = jnp.dot(p.astype(jnp.bfloat16), kv[:, 128:], preferred_element_type=jnp.float32)
-        return m, l, o
+        return m * scale, l, o
 
     chunk = 256
 
@@ -133,10 +133,10 @@
         o_acc[rows] = oo
         return carry
 
-    lax.fori_loop(0, LOCAL // chunk, branch0, 0)
-
     forwards = []
-    for b, (count, group) in enumerate(BRANCHES):
+
+    def forward(b):
+        count, group = BRANCHES[b]
         pairs = group // 2
         locals_[b].wait()
         if pairs > 1:
@@ -153,11 +153,12 @@
         cp.start()
         forwards.append(cp)
 
-    for b, (count, group) in enumerate(BRANCHES):
+    def later(b):
+        count, group = BRANCHES[b]
         other = bufs[b].at[:, 1 - side]
         pltpu.make_async_copy(other, other, fwd_recv.at[b]).wait()
 
-        def branch(j, carry, b=b, count=count):
+        def branch(j, carry):
             start = j * 256 + (hy * 64 if b >= 1 else 0)
             rows = pl.ds(pl.multiple_of(start, 16), count)
             same = sq_ref[rows] == sk_ref[1 + b * heads + j]
@@ -173,6 +174,15 @@
             return carry
 
         lax.fori_loop(0, heads, branch, 0)
+
+    lax.fori_loop(0, 2, branch0, 0)
+    forward(0)
+    lax.fori_loop(2, LOCAL // chunk, branch0, 0)
+    forward(1)
+    later(0)
+    forward(2)
+    later(1)
+    later(2)
 
     feature = lax.broadcasted_iota(jnp.int32, (8, 256), 1) >= SHIFT
     ones = jnp.where(feature, 1.0, 0.0).astype(jnp.float32)

time: 61 us -> 61.2 us (level)
  no operation moved by 1% of the time
where the time goes in v7:
time: 61.2 us; the launch traced here: 60.1 us
  Pallas kernels  44.5 us (73%)
  local copies, waits for them, and re-layouts  12 us (20%)
  other arithmetic  3.27 us (5%)
    pallas_call x1, Pallas kernels, per_device(): pl.pallas_call(attention_kernel, out_shape=jax.ShapeDtypeStruct((LOCAL, 2...  44.5 us
    select_n x3, other arithmetic, per_device(): chunk = jnp.where(kv_lane[None, :] == j, piece, chunk)  2.07 us
    dynamic_slice x5, local copies, waits for them, and re-layouts, per_device(): piece = lax.dynamic_slice_in_dim(kv, starts[j], count, 0)  1.61 us
    transpose x2, local copies, waits for them, and re-layouts, to_token_major(): x = jnp.transpose(x, (4, 3, 2, 1, 0))  1.55 us
    slice x1, local copies, waits for them, and re-layouts, per_device(): return from_token_major(out[:, SHIFT:SHIFT + width])  1.29 us
    unnamed x17, local copies, waits for them, and re-layouts  1.26 us
    reshape x2, local copies, waits for them, and re-layouts, from_token_major(): return x.reshape(f, LOCAL)  1.25 us

profile of v7, /device:TPU:4, one launch (start us, length us, event | category | flops | bytes accessed | tf_op | source)
XLA Modules:
  0.0 60.1 jit_solution(9150650283441244974)
XLA Ops:
  0.0 1.2 %copy.35 = bf16[192,1024]{0,1:T(8,128)(2,1)S(1)} copy(bf16[192,1024]{1,0:T(8,128)(2,1)} %param.6) | data formatting | bytes 786432
  1.2 0.1 concatenate.12.clone
  1.3 0.1 reshape.2406
  1.4 0.0 copy-start.1
  1.4 0.0 copy-start.2
  1.5 1.1 %copy.24 = bf16[4,4,4,16,256]{4,3,2,1,0:T(8,128)(2,1)} copy(bf16[4,4,4,16,256]{4,0,1,2,3:T(4,128)(2,1)S(1)} %bitcast.54) | data formatting | bytes 1048576 | tf_op jit(solution)/shard_map/transpose | solution.py:22
  2.6 0.1 pad_maximum_fusion
  2.6 0.4 copy.25
  3.0 0.2 reshape.2408
  3.2 0.5 copy.26
  3.6 0.0 copy-start
  3.6 1.1 %fusion.124 = (bf16[1,4,4,16,384]{4,0,1,2,3:T(2,128)(2,1)S(1)}, bf16[1,4,4,16,384]{4,0,1,2,3:T(2,128)(2,1)S(1)}, bf16[1,4,4,16,384]{4,0,1,2,3:T(2,128)(2,1)S(1)}, bf16[1,4,4,16,384]{4,0,1,2,3:T(2,128)(2,1)S(1)}) fusion(bf16[4,4,4,16,384]{4,0,1,2,3:T(4,128)(2,1)S(1)} %bitcast.50), kind=kLoop, calls=%fused_computation.384 | loop fusion | bytes 1572864 | tf_op jit(solution)/shard_map/dynamic_slice | solution.py:261
  4.8 0.1 copy.30
  4.9 0.1 copy.29
  5.0 0.1 copy.28
  5.2 0.1 copy.27
  5.3 0.0 copy-start.5
  5.3 0.8 %fusion.2.s1_ref = bf16[256,384]{1,0:T(8,128)(2,1)} fusion(bf16[1,4,4,16,384]{4,3,2,1,0:T(8,128)(2,1)S(1)} %copy.30, bf16[1,4,4,16,384]{4,3,2,1,0:T(8,128)(2,1)S(1)} %copy.29, bf16[1,4,4,16,384]{4,3,2,1,0:T(8,128)(2,1)S(1)} %copy.28, bf16[1,4,4,16,384]{4,3,2,1,0:T(8,128)(2,1)S(1)} %copy.27, pred[384]{0:T(512)(128)(4,1)S(1)} %get-tuple-element.28, ...), kind=kLoop, calls=%fused_computation.6 | loop fusion | flops 393216 | bytes 984576 | tf_op jit(solution)/shard_map/jit(_where)/select_n | solution.py:262
  6.1 0.7 %select_select_fusion.s2_ref = bf16[64,384]{1,0:T(8,128)(2,1)} fusion(bf16[1024,384]{1,0:T(8,128)(2,1)S(1)} %bitcast.51, s32[]{:T(128)S(6)} %select_n.847, s32[]{:T(128)S(6)} %select_n.846, s32[]{:T(128)S(6)} %select_n.845, s32[]{:T(128)S(6)} %select_n.844, pred[384]{0:T(512)(128)(4,1)S(1)} %get-tuple-element.28, pred[384]{0:T(512)(128)(4,1)S(1)} %get-tuple-element.27, ...), kind=kLoop, calls=%fused_computation.7 | loop fusion | flops 98304 | bytes 247312 | tf_op jit(solution)/shard_map/jit(_where)/select_n | solution.py:262
  6.8 0.6 %select_select_fusion.1.s3_ref = bf16[16,384]{1,0:T(8,128)(2,1)} fusion(bf16[1024,384]{1,0:T(8,128)(2,1)S(1)} %bitcast.52, s32[]{:T(128)S(6)} %select_n.847, s32[]{:T(128)S(6)} %select_n.846, s32[]{:T(128)S(6)} %select_n.845, s32[]{:T(128)S(6)} %select_n.844, pred[384]{0:T(512)(128)(4,1)S(1)} %get-tuple-element.28, pred[384]{0:T(512)(128)(4,1)S(1)} %get-tuple-element.27, ...), kind=kLoop, calls=%fused_computation.29 | loop fusion | flops 24576 | bytes 62992 | tf_op jit(solution)/shard_map/jit(_where)/select_n | solution.py:262
  7.5 0.0 copy-start.3
  7.5 0.0 copy-start.4
  7.5 0.1 add_bitcast_fusion
  7.7 0.1 broadcast_add_fusion.4
  7.8 0.1 add.1506
  7.9 0.1 add.1517
  8.0 0.1 add.1528
  8.1 0.1 add.1539
  8.2 0.1 broadcast_add_fusion
  8.3 0.1 add.1553
  8.4 0.1 add.1564
  8.5 0.1 add.1575
  8.6 0.1 add.1586
  8.7 0.1 stack.4
  8.8 0.0 copy-done.5
  8.8 0.1 copy.31
  8.9 0.1 reduce-window.8
  9.0 0.1 reduce
  9.1 0.5 convert_reduce_fusion
  9.6 1.0 %copy.32.sq_ref = s32[1024,1]{1,0:T(8,128)} copy(s32[1024,1]{0,1:T(1,128)S(1)} %slice_bitcast_fusion) | data formatting | bytes 8192 | tf_op jit(solution)/shard_map/reshape;squeeze | solution.py:299
  10.6 0.7 %reshape.2412.sk_ref = s32[13,1,1024]{2,1,0:T(1,128)} reshape(s32[13,1024]{1,0:T(8,128)S(1)} %convert_reduce_fusion) | data formatting | bytes 106496 | tf_op jit(solution)/shard_map/reshape | solution.py:299
  11.3 0.7 %concatenate.14 = f32[256]{0:T(256)} pad(f32[192]{0:T(256)S(1)} %copy-done.3, f32[]{:T(128)} %constant.625.clone.1), padding=64_0 | pad | bytes 1796 | tf_op jit(solution)/shard_map/concatenate | solution.py:272
  12.0 0.6 %concatenate.15 = f32[256]{0:T(256)} pad(f32[192]{0:T(256)S(1)} %copy-done.4, f32[]{:T(128)} %constant.625.clone.1), padding=64_0 | pad | bytes 1796 | tf_op jit(solution)/shard_map/concatenate | solution.py:273
  12.6 44.5 %shard_map.64 = bf16[1024,256]{1,0:T(8,128)(2,1)} custom-call(bf16[1024,256]{1,0:T(8,128)(2,1)} %bitcast.57, bf16[1024,384]{1,0:T(8,128)(2,1)} %bitcast.53, bf16[256,384]{1,0:T(8,128)(2,1)} %fusion.2.s1_ref, bf16[64,384]{1,0:T(8,128)(2,1)} %select_select_fusion.s2_ref, bf16[16,384]{1,0:T(8,128)(2,1)} %select_select_fusion.1.s3_ref, s32[1024,1]{1,0:T(8,128)} %copy.32.sq_ref, ...), custom_call_target="tpu_custom_call" | custom-call | tf_op jit(solution)/shard_map/pallas_call | solution.py:275
  57.1 1.3 %slice.11 = bf16[1024,192]{1,0:T(8,128)(2,1)S(1)} slice(bf16[1024,256]{1,0:T(8,128)(2,1)} %shard_map.64), slice={[0:1024], [64:256]} | slice | bytes 786432 | tf_op jit(solution)/shard_map/slice | solution.py:300
  58.4 0.4 copy.41
  58.9 0.3 reshape.2416
  59.2 0.9 %copy.34 = bf16[192,1024]{1,0:T(8,128)(2,1)} copy(bf16[192,1024]{0,1:T(8,128)(2,1)S(1)} %reshape.2416) | data formatting | bytes 786432 | tf_op jit(solution)/shard_map/reshape | solution.py:30
  (22 shorter events, 0.3 us)
Async XLA Ops:
  1.4 1.1 %copy-start.1 = (bf16[192,1024]{1,0:T(8,128)(2,1)S(1)}, bf16[192,1024]{1,0:T(8,128)(2,1)}, u32[]{:S(2)}) copy-start(bf16[192,1024]{1,0:T(8,128)(2,1)} %param.8) | copy-start | bytes 1179652
  1.4 1.1 %copy-start.2 = (bf16[192,1024]{1,0:T(8,128)(2,1)S(1)}, bf16[192,1024]{1,0:T(8,128)(2,1)}, u32[]{:S(2)}) copy-start(bf16[192,1024]{1,0:T(8,128)(2,1)} %param.7) | copy-start | bytes 1179652
  3.6 3.2 %copy-start = (bf16[4,4,4,16,384]{4,3,2,1,0:T(8,128)(2,1)}, bf16[4,4,4,16,384]{4,3,2,1,0:T(8,128)(2,1)S(1)}, u32[]{:S(2)}) copy-start(bf16[4,4,4,16,384]{4,3,2,1,0:T(8,128)(2,1)S(1)} %copy.26) | copy-start | bytes 2359300
  5.3 3.4 %copy-start.5 = (s32[64]{0:T(128)S(1)}, s32[64]{0:T(128)}, u32[]{:S(2)}) copy-start(s32[64]{0:T(128)} %param.9) | copy-start | bytes 772
  7.5 3.8 %copy-start.3 = (f32[192]{0:T(256)S(1)}, f32[192]{0:T(256)}, u32[]{:S(2)}) copy-start(f32[192]{0:T(256)} %param.10) | copy-start | bytes 2308
  7.5 4.4 %copy-start.4 = (f32[192]{0:T(256)S(1)}, f32[192]{0:T(256)}, u32[]{:S(2)}) copy-start(f32[192]{0:T(256)} %param.11) | copy-start | bytes 2308

commit v8 on v7

--- a/solution.py
+++ b/solution.py
@@ -54,17 +54,7 @@
     bufs = (kv1, kv2, kv3)
     width = heads * HD
 
-    barrier = pltpu.get_barrier_semaphore()
-
-    def greet(o, carry):
-        pl.semaphore_signal(barrier, inc=1, device_id=(lax.rem(me + o, devices), hy), device_id_type=MESH)
-        return carry
-
-    lax.fori_loop(1, devices, greet, 0)
     ys = lax.axis_size("head")
-    for o in range(1, ys):
-        pl.semaphore_signal(barrier, inc=1, device_id=(me, lax.rem(hy + o, ys)), device_id_type=MESH)
-    pl.semaphore_wait(barrier, devices - 1 + ys - 1)
 
     def slot(b, half, pair):
         return bufs[b].at[pair, half]
@@ -294,7 +284,7 @@
             pltpu.SemaphoreType.DMA((1,)),
         ],
         compiler_params=pltpu.CompilerParams(
-            collective_id=0, has_side_effects=True, vmem_limit_bytes=60 * 1024 * 1024
+            has_side_effects=True, vmem_limit_bytes=60 * 1024 * 1024
         ),
     )(q, kv, *sends, slides[0].reshape(LOCAL, 1), slides.reshape(-1, 1, LOCAL), gain, bias)
     return from_token_major(out[:, SHIFT : SHIFT + width])

time: 61.2 us -> 66.1 us (1.080)
  Pallas kernels: 44.5 us -> 49.5 us
    pallas_call x1, Pallas kernels: 44.5 us -> 49.5 us  [per_device(): pl.pallas_call(attention_kernel, out_shape=jax.ShapeDtypeStruct((LOCAL, 2...]
where the time goes in v8:
time: 66.1 us; the launch traced here: 65.1 us
  Pallas kernels  49.5 us (75%)
  local copies, waits for them, and re-layouts  12 us (18%)
  other arithmetic  3.27 us (5%)
    pallas_call x1, Pallas kernels, per_device(): pl.pallas_call(attention_kernel, out_shape=jax.ShapeDtypeStruct((LOCAL, 2...  49.5 us
    select_n x3, other arithmetic, per_device(): chunk = jnp.where(kv_lane[None, :] == j, piece, chunk)  2.07 us
    dynamic_slice x5, local copies, waits for them, and re-layouts, per_device(): piece = lax.dynamic_slice_in_dim(kv, starts[j], count, 0)  1.61 us
    transpose x2, local copies, waits for them, and re-layouts, to_token_major(): x = jnp.transpose(x, (4, 3, 2, 1, 0))  1.55 us

profile of v8, /device:TPU:4, one launch (start us, length us, event | category | flops | bytes accessed | tf_op | source)
XLA Modules:
  0.0 65.1 jit_solution(8939885845288127506)
XLA Ops:
  0.0 1.2 %copy.35 = bf16[192,1024]{0,1:T(8,128)(2,1)S(1)} copy(bf16[192,1024]{1,0:T(8,128)(2,1)} %param.6) | data formatting | bytes 786432
  1.2 0.1 concatenate.12.clone
  1.3 0.1 reshape.2406
  1.4 0.0 copy-start.1
  1.4 0.0 copy-start.2
  1.5 1.1 %copy.24 = bf16[4,4,4,16,256]{4,3,2,1,0:T(8,128)(2,1)} copy(bf16[4,4,4,16,256]{4,0,1,2,3:T(4,128)(2,1)S(1)} %bitcast.54) | data formatting | bytes 1048576 | tf_op jit(solution)/shard_map/transpose | solution.py:22
  2.6 0.1 pad_maximum_fusion
  2.6 0.4 copy.25
  3.0 0.2 reshape.2408
  3.2 0.5 copy.26
  3.6 0.0 copy-start
  3.6 1.1 %fusion.124 = (bf16[1,4,4,16,384]{4,0,1,2,3:T(2,128)(2,1)S(1)}, bf16[1,4,4,16,384]{4,0,1,2,3:T(2,128)(2,1)S(1)}, bf16[1,4,4,16,384]{4,0,1,2,3:T(2,128)(2,1)S(1)}, bf16[1,4,4,16,384]{4,0,1,2,3:T(2,128)(2,1)S(1)}) fusion(bf16[4,4,4,16,384]{4,0,1,2,3:T(4,128)(2,1)S(1)} %bitcast.50), kind=kLoop, calls=%fused_computation.384 | loop fusion | bytes 1572864 | tf_op jit(solution)/shard_map/dynamic_slice | solution.py:251
  4.8 0.1 copy.30
  4.9 0.1 copy.29
  5.0 0.1 copy.28
  5.2 0.1 copy.27
  5.3 0.0 copy-start.5
  5.3 0.8 %fusion.2.s1_ref = bf16[256,384]{1,0:T(8,128)(2,1)} fusion(bf16[1,4,4,16,384]{4,3,2,1,0:T(8,128)(2,1)S(1)} %copy.30, bf16[1,4,4,16,384]{4,3,2,1,0:T(8,128)(2,1)S(1)} %copy.29, bf16[1,4,4,16,384]{4,3,2,1,0:T(8,128)(2,1)S(1)} %copy.28, bf16[1,4,4,16,384]{4,3,2,1,0:T(8,128)(2,1)S(1)} %copy.27, pred[384]{0:T(512)(128)(4,1)S(1)} %get-tuple-element.28, ...), kind=kLoop, calls=%fused_computation.6 | loop fusion | flops 393216 | bytes 984576 | tf_op jit(solution)/shard_map/jit(_where)/select_n | solution.py:252
  6.1 0.7 %select_select_fusion.s2_ref = bf16[64,384]{1,0:T(8,128)(2,1)} fusion(bf16[1024,384]{1,0:T(8,128)(2,1)S(1)} %bitcast.51, s32[]{:T(128)S(6)} %select_n.847, s32[]{:T(128)S(6)} %select_n.846, s32[]{:T(128)S(6)} %select_n.845, s32[]{:T(128)S(6)} %select_n.844, pred[384]{0:T(512)(128)(4,1)S(1)} %get-tuple-element.28, pred[384]{0:T(512)(128)(4,1)S(1)} %get-tuple-element.27, ...), kind=kLoop, calls=%fused_computation.7 | loop fusion | flops 98304 | bytes 247312 | tf_op jit(solution)/shard_map/jit(_where)/select_n | solution.py:252
  6.8 0.6 select_select_fusion.1.s3_ref
  7.5 0.0 copy-start.3
  7.5 0.0 copy-start.4
  7.5 0.1 add_bitcast_fusion
  7.7 0.1 broadcast_add_fusion.4
  7.8 0.1 add.1506
  7.9 0.1 add.1517
  8.0 0.1 add.1528
  8.1 0.1 add.1539
  8.2 0.1 broadcast_add_fusion
  8.3 0.1 add.1553
  8.4 0.1 add.1564
  8.5 0.1 add.1575
  8.6 0.1 add.1586
  8.7 0.1 stack.4
  8.8 0.0 copy-done.5
  8.8 0.1 copy.31
  8.9 0.1 reduce-window.8
  9.0 0.1 reduce
  9.1 0.5 convert_reduce_fusion
  9.6 1.0 %copy.32.sq_ref = s32[1024,1]{1,0:T(8,128)} copy(s32[1024,1]{0,1:T(1,128)S(1)} %slice_bitcast_fusion) | data formatting | bytes 8192 | tf_op jit(solution)/shard_map/reshape;squeeze | solution.py:289
  10.6 0.7 %reshape.2412.sk_ref = s32[13,1,1024]{2,1,0:T(1,128)} reshape(s32[13,1024]{1,0:T(8,128)S(1)} %convert_reduce_fusion) | data formatting | bytes 106496 | tf_op jit(solution)/shard_map/reshape | solution.py:289
  11.3 0.7 %concatenate.14 = f32[256]{0:T(256)} pad(f32[192]{0:T(256)S(1)} %copy-done.3, f32[]{:T(128)} %constant.625.clone.1), padding=64_0 | pad | bytes 1796 | tf_op jit(solution)/shard_map/concatenate | solution.py:262
  12.0 0.6 concatenate.15
  12.6 49.5 %shard_map.64 = bf16[1024,256]{1,0:T(8,128)(2,1)} custom-call(bf16[1024,256]{1,0:T(8,128)(2,1)} %bitcast.57, bf16[1024,384]{1,0:T(8,128)(2,1)} %bitcast.53, bf16[256,384]{1,0:T(8,128)(2,1)} %fusion.2.s1_ref, bf16[64,384]{1,0:T(8,128)(2,1)} %select_select_fusion.s2_ref, bf16[16,384]{1,0:T(8,128)(2,1)} %select_select_fusion.1.s3_ref, s32[1024,1]{1,0:T(8,128)} %copy.32.sq_ref, ...), custom_call_target="tpu_custom_call" | custom-call | tf_op jit(solution)/shard_map/pallas_call | solution.py:265
  62.2 1.3 %slice.11 = bf16[1024,192]{1,0:T(8,128)(2,1)S(1)} slice(bf16[1024,256]{1,0:T(8,128)(2,1)} %shard_map.64), slice={[0:1024], [64:256]} | slice | bytes 786432 | tf_op jit(solution)/shard_map/slice | solution.py:290
  63.4 0.4 copy.41
  63.9 0.3 reshape.2416
  64.2 0.9 %copy.34 = bf16[192,1024]{1,0:T(8,128)(2,1)} copy(bf16[192,1024]{0,1:T(8,128)(2,1)S(1)} %reshape.2416) | data formatting | bytes 786432 | tf_op jit(solution)/shard_map/reshape | solution.py:30
  (22 shorter events, 0.3 us)
Async XLA Ops:
  1.4 1.1 %copy-start.1 = (bf16[192,1024]{1,0:T(8,128)(2,1)S(1)}, bf16[192,1024]{1,0:T(8,128)(2,1)}, u32[]{:S(2)}) copy-start(bf16[192,1024]{1,0:T(8,128)(2,1)} %param.8) | copy-start | bytes 1179652
  1.4 1.1 %copy-start.2 = (bf16[192,1024]{1,0:T(8,128)(2,1)S(1)}, bf16[192,1024]{1,0:T(8,128)(2,1)}, u32[]{:S(2)}) copy-start(bf16[192,1024]{1,0:T(8,128)(2,1)} %param.7) | copy-start | bytes 1179652
  3.6 3.2 %copy-start = (bf16[4,4,4,16,384]{4,3,2,1,0:T(8,128)(2,1)}, bf16[4,4,4,16,384]{4,3,2,1,0:T(8,128)(2,1)S(1)}, u32[]{:S(2)}) copy-start(bf16[4,4,4,16,384]{4,3,2,1,0:T(8,128)(2,1)S(1)} %copy.26) | copy-start | bytes 2359300
  5.3 3.4 %copy-start.5 = (s32[64]{0:T(128)S(1)}, s32[64]{0:T(128)}, u32[]{:S(2)}) copy-start(s32[64]{0:T(128)} %param.9) | copy-start | bytes 772
  7.5 3.8 %copy-start.3 = (f32[192]{0:T(256)S(1)}, f32[192]{0:T(256)}, u32[]{:S(2)}) copy-start(f32[192]{0:T(256)} %param.10) | copy-start | bytes 2308
  7.5 4.4 %copy-start.4 = (f32[192]{0:T(256)S(1)}, f32[192]{0:T(256)}, u32[]{:S(2)}) copy-start(f32[192]{0:T(256)} %param.11) | copy-start | bytes 2308

commit v9 on v7

--- a/solution.py
+++ b/solution.py
@@ -56,45 +56,50 @@
 
     barrier = pltpu.get_barrier_semaphore()
 
+    side = me % 2
+    halves = devices // 2
+
     def greet(o, carry):
-        pl.semaphore_signal(barrier, inc=1, device_id=(lax.rem(me + o, devices), hy), device_id_type=MESH)
+        peer = 2 * lax.rem(me // 2 + o, halves) + side
+        pl.semaphore_signal(barrier, inc=1, device_id=(peer, hy), device_id_type=MESH)
         return carry
 
-    lax.fori_loop(1, devices, greet, 0)
+    lax.fori_loop(1, halves, greet, 0)
+    pl.semaphore_signal(barrier, inc=1, device_id=(me + 1 - 2 * side, hy), device_id_type=MESH)
     ys = lax.axis_size("head")
     for o in range(1, ys):
         pl.semaphore_signal(barrier, inc=1, device_id=(me, lax.rem(hy + o, ys)), device_id_type=MESH)
-    pl.semaphore_wait(barrier, devices - 1 + ys - 1)
 
     def slot(b, half, pair):
         return bufs[b].at[pair, half]
 
     sibling = me + 1 - 2 * (me % 2)
-    side = me % 2
     locals_ = []
     for b, (count, group) in enumerate(BRANCHES):
         member = lax.rem(me, group)
         cp = pltpu.make_async_copy(sends[b], slot(b, side, member // 2), local_sem.at[b])
         cp.start()
         locals_.append(cp)
-    for b, (count, group) in enumerate(BRANCHES):
-        member = lax.rem(me, group)
-        first = me - member
-        pairs = group // 2
-
-        def push(o, carry, b=b, pairs=pairs, member=member, first=first):
-            target = first + 2 * lax.rem(member // 2 + o, pairs) + side
-            pltpu.make_async_remote_copy(
-                src_ref=sends[b],
-                dst_ref=slot(b, side, member // 2),
-                send_sem=send_sem.at[b],
-                recv_sem=recv_sem.at[b],
-                device_id=(target, hy),
-                device_id_type=MESH,
-            ).start()
-            return carry
-
-        lax.fori_loop(1, pairs, push, 0)
+    def start_pushes():
+        for b, (count, group) in enumerate(BRANCHES):
+            member = lax.rem(me, group)
+            first = me - member
+            pairs = group // 2
+
+            def push(o, carry, b=b, pairs=pairs, member=member, first=first):
+                target = first + 2 * lax.rem(member // 2 + o, pairs) + side
+                pltpu.make_async_remote_copy(
+                    src_ref=sends[b],
+                    dst_ref=slot(b, side, member // 2),
+                    send_sem=send_sem.at[b],
+                    recv_sem=recv_sem.at[b],
+                    device_id=(target, hy),
+                    device_id_type=MESH,
+                ).start()
+                return carry
+
+            lax.fori_loop(1, pairs, push, 0)
+
 
     q_lane = lax.broadcasted_iota(jnp.int32, (1, 256), 1) // HD
     o_lane = (lax.broadcasted_iota(jnp.int32, (1, 256), 1) - SHIFT) // HD
@@ -175,9 +180,12 @@
 
         lax.fori_loop(0, heads, branch, 0)
 
-    lax.fori_loop(0, 2, branch0, 0)
+    lax.fori_loop(0, 1, branch0, 0)
+    pl.semaphore_wait(barrier, halves + ys - 1)
+    start_pushes()
+    lax.fori_loop(1, 3, branch0, 0)
     forward(0)
-    lax.fori_loop(2, LOCAL // chunk, branch0, 0)
+    lax.fori_loop(3, LOCAL // chunk, branch0, 0)
     forward(1)
     later(0)
     forward(2)

time: 61.2 us -> 58.5 us (0.956); the launches traced: 60.1 us -> 58.1 us
  Pallas kernels: 44.5 us -> 42.5 us
    pallas_call x1, Pallas kernels: 44.5 us -> 42.5 us  [per_device(): pl.pallas_call(attention_kernel, out_shape=jax.ShapeDtypeStruct((LOCAL, 2...]
where the time goes in v9:
time: 58.5 us; the launch traced here: 58.1 us
  Pallas kernels  42.5 us (73%)
  local copies, waits for them, and re-layouts  12 us (21%)
  other arithmetic  3.27 us (6%)
    pallas_call x1, Pallas kernels, per_device(): pl.pallas_call(attention_kernel, out_shape=jax.ShapeDtypeStruct((LOCAL, 2...  42.5 us
    select_n x3, other arithmetic, per_device(): chunk = jnp.where(kv_lane[None, :] == j, piece, chunk)  2.07 us
    dynamic_slice x5, local copies, waits for them, and re-layouts, per_device(): piece = lax.dynamic_slice_in_dim(kv, starts[j], count, 0)  1.61 us
    transpose x2, local copies, waits for them, and re-layouts, to_token_major(): x = jnp.transpose(x, (4, 3, 2, 1, 0))  1.55 us
    slice x1, local copies, waits for them, and re-layouts, per_device(): return from_token_major(out[:, SHIFT:SHIFT + width])  1.29 us
    unnamed x17, local copies, waits for them, and re-layouts  1.26 us
    reshape x2, local copies, waits for them, and re-layouts, from_token_major(): return x.reshape(f, LOCAL)  1.25 us

profile of v9, /device:TPU:4, one launch (start us, length us, event | category | flops | bytes accessed | tf_op | source)
XLA Modules:
  0.0 58.1 jit_solution(12435456756701732373)
XLA Ops:
  0.0 1.2 %copy.35 = bf16[192,1024]{0,1:T(8,128)(2,1)S(1)} copy(bf16[192,1024]{1,0:T(8,128)(2,1)} %param.6) | data formatting | bytes 786432
  1.2 0.1 concatenate.12.clone
  1.3 0.1 reshape.2406
  1.4 0.0 copy-start.1
  1.4 0.0 copy-start.2
  1.5 1.1 %copy.24 = bf16[4,4,4,16,256]{4,3,2,1,0:T(8,128)(2,1)} copy(bf16[4,4,4,16,256]{4,0,1,2,3:T(4,128)(2,1)S(1)} %bitcast.54) | data formatting | bytes 1048576 | tf_op jit(solution)/shard_map/transpose | solution.py:22
  2.6 0.1 pad_maximum_fusion
  2.6 0.4 copy.25
  3.0 0.2 reshape.2408
  3.2 0.5 copy.26
  3.6 0.0 copy-start
  3.6 1.1 %fusion.124 = (bf16[1,4,4,16,384]{4,0,1,2,3:T(2,128)(2,1)S(1)}, bf16[1,4,4,16,384]{4,0,1,2,3:T(2,128)(2,1)S(1)}, bf16[1,4,4,16,384]{4,0,1,2,3:T(2,128)(2,1)S(1)}, bf16[1,4,4,16,384]{4,0,1,2,3:T(2,128)(2,1)S(1)}) fusion(bf16[4,4,4,16,384]{4,0,1,2,3:T(4,128)(2,1)S(1)} %bitcast.50), kind=kLoop, calls=%fused_computation.384 | loop fusion | bytes 1572864 | tf_op jit(solution)/shard_map/dynamic_slice | solution.py:269
  4.8 0.1 copy.30
  4.9 0.1 copy.29
  5.0 0.1 copy.28
  5.2 0.1 copy.27
  5.3 0.0 copy-start.5
  5.3 0.8 %fusion.2.s1_ref = bf16[256,384]{1,0:T(8,128)(2,1)} fusion(bf16[1,4,4,16,384]{4,3,2,1,0:T(8,128)(2,1)S(1)} %copy.30, bf16[1,4,4,16,384]{4,3,2,1,0:T(8,128)(2,1)S(1)} %copy.29, bf16[1,4,4,16,384]{4,3,2,1,0:T(8,128)(2,1)S(1)} %copy.28, bf16[1,4,4,16,384]{4,3,2,1,0:T(8,128)(2,1)S(1)} %copy.27, pred[384]{0:T(512)(128)(4,1)S(1)} %get-tuple-element.28, ...), kind=kLoop, calls=%fused_computation.6 | loop fusion | flops 393216 | bytes 984576 | tf_op jit(solution)/shard_map/jit(_where)/select_n | solution.py:270
  6.1 0.7 %select_select_fusion.s2_ref = bf16[64,384]{1,0:T(8,128)(2,1)} fusion(bf16[1024,384]{1,0:T(8,128)(2,1)S(1)} %bitcast.51, s32[]{:T(128)S(6)} %select_n.847, s32[]{:T(128)S(6)} %select_n.846, s32[]{:T(128)S(6)} %select_n.845, s32[]{:T(128)S(6)} %select_n.844, pred[384]{0:T(512)(128)(4,1)S(1)} %get-tuple-element.28, pred[384]{0:T(512)(128)(4,1)S(1)} %get-tuple-element.27, ...), kind=kLoop, calls=%fused_computation.7 | loop fusion | flops 98304 | bytes 247312 | tf_op jit(solution)/shard_map/jit(_where)/select_n | solution.py:270
  6.8 0.6 %select_select_fusion.1.s3_ref = bf16[16,384]{1,0:T(8,128)(2,1)} fusion(bf16[1024,384]{1,0:T(8,128)(2,1)S(1)} %bitcast.52, s32[]{:T(128)S(6)} %select_n.847, s32[]{:T(128)S(6)} %select_n.846, s32[]{:T(128)S(6)} %select_n.845, s32[]{:T(128)S(6)} %select_n.844, pred[384]{0:T(512)(128)(4,1)S(1)} %get-tuple-element.28, pred[384]{0:T(512)(128)(4,1)S(1)} %get-tuple-element.27, ...), kind=kLoop, calls=%fused_computation.29 | loop fusion | flops 24576 | bytes 62992 | tf_op jit(solution)/shard_map/jit(_where)/select_n | solution.py:270
  7.5 0.0 copy-start.3
  7.5 0.0 copy-start.4
  7.5 0.1 add_bitcast_fusion
  7.7 0.1 broadcast_add_fusion.4
  7.8 0.1 add.1506
  7.9 0.1 add.1517
  8.0 0.1 add.1528
  8.1 0.1 add.1539
  8.2 0.1 broadcast_add_fusion
  8.3 0.1 add.1553
  8.4 0.1 add.1564
  8.5 0.1 add.1575
  8.6 0.1 add.1586
  8.7 0.1 stack.4
  8.8 0.0 copy-done.5
  8.8 0.1 copy.31
  8.9 0.1 reduce-window.8
  9.0 0.1 reduce
  9.1 0.5 convert_reduce_fusion
  9.6 1.0 %copy.32.sq_ref = s32[1024,1]{1,0:T(8,128)} copy(s32[1024,1]{0,1:T(1,128)S(1)} %slice_bitcast_fusion) | data formatting | bytes 8192 | tf_op jit(solution)/shard_map/reshape;squeeze | solution.py:307
  10.6 0.7 %reshape.2412.sk_ref = s32[13,1,1024]{2,1,0:T(1,128)} reshape(s32[13,1024]{1,0:T(8,128)S(1)} %convert_reduce_fusion) | data formatting | bytes 106496 | tf_op jit(solution)/shard_map/reshape | solution.py:307
  11.3 0.7 %concatenate.14 = f32[256]{0:T(256)} pad(f32[192]{0:T(256)S(1)} %copy-done.3, f32[]{:T(128)} %constant.625.clone.1), padding=64_0 | pad | bytes 1796 | tf_op jit(solution)/shard_map/concatenate | solution.py:280
  12.0 0.6 %concatenate.15 = f32[256]{0:T(256)} pad(f32[192]{0:T(256)S(1)} %copy-done.4, f32[]{:T(128)} %constant.625.clone.1), padding=64_0 | pad | bytes 1796 | tf_op jit(solution)/shard_map/concatenate | solution.py:281
  12.6 42.5 %shard_map.64 = bf16[1024,256]{1,0:T(8,128)(2,1)} custom-call(bf16[1024,256]{1,0:T(8,128)(2,1)} %bitcast.57, bf16[1024,384]{1,0:T(8,128)(2,1)} %bitcast.53, bf16[256,384]{1,0:T(8,128)(2,1)} %fusion.2.s1_ref, bf16[64,384]{1,0:T(8,128)(2,1)} %select_select_fusion.s2_ref, bf16[16,384]{1,0:T(8,128)(2,1)} %select_select_fusion.1.s3_ref, s32[1024,1]{1,0:T(8,128)} %copy.32.sq_ref, ...), custom_call_target="tpu_custom_call" | custom-call | tf_op jit(solution)/shard_map/pallas_call | solution.py:283
  55.1 1.3 %slice.11 = bf16[1024,192]{1,0:T(8,128)(2,1)S(1)} slice(bf16[1024,256]{1,0:T(8,128)(2,1)} %shard_map.64), slice={[0:1024], [64:256]} | slice | bytes 786432 | tf_op jit(solution)/shard_map/slice | solution.py:308
  56.4 0.4 copy.41
  56.8 0.3 reshape.2416
  57.1 0.9 %copy.34 = bf16[192,1024]{1,0:T(8,128)(2,1)} copy(bf16[192,1024]{0,1:T(8,128)(2,1)S(1)} %reshape.2416) | data formatting | bytes 786432 | tf_op jit(solution)/shard_map/reshape | solution.py:30
  (22 shorter events, 0.3 us)
Async XLA Ops:
  1.4 1.1 %copy-start.1 = (bf16[192,1024]{1,0:T(8,128)(2,1)S(1)}, bf16[192,1024]{1,0:T(8,128)(2,1)}, u32[]{:S(2)}) copy-start(bf16[192,1024]{1,0:T(8,128)(2,1)} %param.8) | copy-start | bytes 1179652
  1.4 1.1 %copy-start.2 = (bf16[192,1024]{1,0:T(8,128)(2,1)S(1)}, bf16[192,1024]{1,0:T(8,128)(2,1)}, u32[]{:S(2)}) copy-start(bf16[192,1024]{1,0:T(8,128)(2,1)} %param.7) | copy-start | bytes 1179652
  3.6 3.2 %copy-start = (bf16[4,4,4,16,384]{4,3,2,1,0:T(8,128)(2,1)}, bf16[4,4,4,16,384]{4,3,2,1,0:T(8,128)(2,1)S(1)}, u32[]{:S(2)}) copy-start(bf16[4,4,4,16,384]{4,3,2,1,0:T(8,128)(2,1)S(1)} %copy.26) | copy-start | bytes 2359300
  5.3 3.4 %copy-start.5 = (s32[64]{0:T(128)S(1)}, s32[64]{0:T(128)}, u32[]{:S(2)}) copy-start(s32[64]{0:T(128)} %param.9) | copy-start | bytes 772
  7.5 3.8 %copy-start.3 = (f32[192]{0:T(256)S(1)}, f32[192]{0:T(256)}, u32[]{:S(2)}) copy-start(f32[192]{0:T(256)} %param.10) | copy-start | bytes 2308
  7.5 4.4 %copy-start.4 = (f32[192]{0:T(256)S(1)}, f32[192]{0:T(256)}, u32[]{:S(2)}) copy-start(f32[192]{0:T(256)} %param.11) | copy-start | bytes 2308

commit v10 on v9

--- a/solution.py
+++ b/solution.py
@@ -40,9 +40,9 @@
 
 
 def attention_kernel(
-    q_ref, kv_ref, s1_ref, s2_ref, s3_ref, sq_ref, sk_ref, gain_ref, bias_ref,
+    q_ref, kv_ref, s1_ref, s2_ref, s3_ref, sk_ref, gain_ref, bias_ref,
     out_ref,
-    kv1, kv2, kv3, m_acc, l_acc, o_acc, stats, ybuf, cols,
+    kv1, kv2, kv3, m_acc, l_acc, o_acc, stats, ybuf, cols, sqcol,
     send_sem, recv_sem, local_sem, fwd_send, fwd_recv, y_send, y_recv,
 ):
     heads = 4
@@ -51,6 +51,7 @@
     devices = lax.axis_size("seq")
     scale = 1.0 / math.sqrt(HD)
     sends = (s1_ref, s2_ref, s3_ref)
+    sqcol[...] = jnp.transpose(sk_ref[pl.ds(0, 8), :])
     bufs = (kv1, kv2, kv3)
     width = heads * HD
 
@@ -101,17 +102,17 @@
             lax.fori_loop(1, pairs, push, 0)
 
 
-    q_lane = lax.broadcasted_iota(jnp.int32, (1, 256), 1) // HD
-    o_lane = (lax.broadcasted_iota(jnp.int32, (1, 256), 1) - SHIFT) // HD
+    q_lane = (lax.broadcasted_iota(jnp.int32, (1, 256), 1) - SHIFT) // HD
+    o_lane = lax.broadcasted_iota(jnp.int32, (1, 256), 1) // HD
 
     def attend(q, j, kv, same):
         qz = jnp.where(q_lane == j, q, jnp.zeros_like(q))
-        s = lax.dot_general(qz, kv[:, :256], (((1,), (1,)), ((), ())), preferred_element_type=jnp.float32)
+        s = lax.dot_general(qz, kv[:, 128:], (((1,), (1,)), ((), ())), preferred_element_type=jnp.float32)
         s = jnp.where(same, s, -1e30)
         m = jnp.max(s, axis=-1, keepdims=True)
         p = jnp.exp((s - m) * scale)
         l = jnp.sum(p, axis=-1, keepdims=True)
-        o = jnp.dot(p.astype(jnp.bfloat16), kv[:, 128:], preferred_element_type=jnp.float32)
+        o = jnp.dot(p.astype(jnp.bfloat16), kv[:, :256], preferred_element_type=jnp.float32)
         return m * scale, l, o
 
     chunk = 256
@@ -120,7 +121,7 @@
         rows = pl.ds(pl.multiple_of(i * chunk, chunk), chunk)
         q = q_ref[rows]
         kv = kv_ref[...]
-        same = sq_ref[rows] == sk_ref[0]
+        same = sqcol[rows, 0:1] == sk_ref[pl.ds(0, 1), :]
         mm = ll = oo = None
         for j in range(heads):
             m, l, o = attend(q, j, kv, same)
@@ -166,7 +167,7 @@
         def branch(j, carry):
             start = j * 256 + (hy * 64 if b >= 1 else 0)
             rows = pl.ds(pl.multiple_of(start, 16), count)
-            same = sq_ref[rows] == sk_ref[1 + b * heads + j]
+            same = sqcol[rows, 0:1] == sk_ref[pl.ds(1 + b * heads + j, 1), :]
             m_new, l_new, o_new = attend(q_ref[rows], j, bufs[b][...].reshape(LOCAL, 2 * width), same)
             m_old = m_acc[rows]
             mn = jnp.maximum(m_old, m_new)
@@ -192,7 +193,7 @@
     later(1)
     later(2)
 
-    feature = lax.broadcasted_iota(jnp.int32, (8, 256), 1) >= SHIFT
+    feature = lax.broadcasted_iota(jnp.int32, (8, 256), 1) < heads * HD
     ones = jnp.where(feature, 1.0, 0.0).astype(jnp.float32)
     first_row = lax.broadcasted_iota(jnp.int32, (8, chunk), 0) == 0
 
@@ -237,7 +238,7 @@
         rows = pl.ds(pl.multiple_of(i * chunk, chunk), chunk)
         col = cols[rows]
         normed = (o_acc[rows] - col[:, 0:1]) * col[:, 1:2]
-        out_ref[rows] = (normed * gain_ref[...] + bias_ref[...]).astype(out_ref.dtype)
+        out_ref[rows] = (normed[:, : heads * HD] * gain_ref[...] + bias_ref[...]).astype(out_ref.dtype)
         return carry
 
     lax.fori_loop(0, LOCAL // chunk, normalize, 0)
@@ -256,11 +257,22 @@
     seq = lax.axis_index("seq")
     hy = lax.axis_index("head")
     slide_ends = jnp.cumsum(slide_lengths)
-    q = to_token_major(jnp.concatenate([queries, jnp.zeros((256 - width, LOCAL), queries.dtype)]))
-    kv = to_token_major(jnp.concatenate([keys, values]))
+    q = to_token_major(jnp.concatenate([jnp.zeros((SHIFT, LOCAL), queries.dtype), queries]))
+    kv = to_token_major(jnp.concatenate([values, keys]))
     kv_lane = jnp.arange(2 * width) % width // HD
 
-    positions = [pos_of(seq, jnp.arange(LOCAL))]
+    counts, groups, offsets = [LOCAL], [1], [0]
+    for b, (count, group) in enumerate(BRANCHES):
+        for j in range(heads):
+            counts.append(count)
+            groups.append(group)
+            offsets.append(j * 256 + (hy * 64 if b >= 1 else 0))
+    counts = jnp.array(counts, jnp.int32)[:, None]
+    groups = jnp.array(groups, jnp.int32)[:, None]
+    offsets = jnp.stack([jnp.asarray(o, jnp.int32) for o in offsets])[:, None]
+    column = jnp.arange(LOCAL, dtype=jnp.int32)[None, :]
+    devices = seq - seq % groups + column // counts
+    slides = slide_of(pos_of(devices, offsets + column % counts), slide_ends)
     sends = []
     for b, (count, group) in enumerate(BRANCHES):
         starts = [j * 256 + (hy * 64 if b >= 1 else 0) for j in range(heads)]
@@ -269,21 +281,14 @@
             piece = lax.dynamic_slice_in_dim(kv, starts[j], count, 0)
             chunk = jnp.where(kv_lane[None, :] == j, piece, chunk)
         sends.append(chunk)
-        first = seq // group * group
-        members = first + jnp.arange(group)
-        for j in range(heads):
-            idx = starts[j] + jnp.arange(count)
-            positions.append(pos_of(members[:, None], idx[None, :]).reshape(group * count))
-    slides = slide_of(jnp.stack(positions), slide_ends)
-
-    lead = jnp.zeros((SHIFT,), jnp.float32)
-    gain = jnp.concatenate([lead, norm_gain]).reshape(1, 256)
-    bias = jnp.concatenate([lead, norm_bias]).reshape(1, 256)
+
+    gain = norm_gain.reshape(1, width)
+    bias = norm_bias.reshape(1, width)
     vmem = pl.BlockSpec(memory_space=pltpu.VMEM)
     out = pl.pallas_call(
         attention_kernel,
-        out_shape=jax.ShapeDtypeStruct((LOCAL, 256), jnp.bfloat16),
-        in_specs=[vmem] * 9,
+        out_shape=jax.ShapeDtypeStruct((LOCAL, width), jnp.bfloat16),
+        in_specs=[vmem] * 8,
         out_specs=vmem,
         scratch_shapes=[
             *[pltpu.VMEM((group // 2, 2, count, 2 * width), jnp.bfloat16) for count, group in BRANCHES],
@@ -293,6 +298,7 @@
             pltpu.VMEM((8, LOCAL), jnp.float32),
             pltpu.VMEM((4, 8, LOCAL), jnp.float32),
             pltpu.VMEM((LOCAL, 8), jnp.float32),
+            pltpu.VMEM((LOCAL, 8), jnp.int32),
             pltpu.SemaphoreType.DMA((3,)),
             pltpu.SemaphoreType.DMA((3,)),
             pltpu.SemaphoreType.DMA((3,)),
@@ -304,8 +310,8 @@
         compiler_params=pltpu.CompilerParams(
             collective_id=0, has_side_effects=True, vmem_limit_bytes=60 * 1024 * 1024
         ),
-    )(q, kv, *sends, slides[0].reshape(LOCAL, 1), slides.reshape(-1, 1, LOCAL), gain, bias)
-    return from_token_major(out[:, SHIFT : SHIFT + width])
+    )(q, kv, *sends, slides, gain, bias)
+    return from_token_major(out)
 
 
 def solution(mesh):

time: 58.5 us -> 56.6 us (0.968)
  local copies, waits for them, and re-layouts: 12 us -> 7.22 us
  other arithmetic: 3.27 us -> 5.83 us
    slice x1 -> x0, local copies, waits for them, and re-layouts: 1.29 us -> none  [per_device(): return from_token_major(out[:, SHIFT:SHIFT + width])]
    concatenate x4 -> x2, local copies, waits for them, and re-layouts: 1.75 us -> 0.58 us  [the longest x1 0.35 us: per_device(): kv = to_token_major(jnp.concatenate([values, keys]))]
    concatenate x1, other arithmetic: 0.05 us -> 1.17 us  [per_device(): kv = to_token_major(jnp.concatenate([values, keys]))]
    another operation x4 -> x3, local copies, waits for them, and re-layouts: 1.24 us -> 0.19 us  [the longest x2 1.04 us: per_device(): slides[0].reshape(LOCAL, 1)]
    reshape x1, local copies, waits for them, and re-layouts: 0.41 us -> 1.45 us  [from_token_major(): x = x.reshape(4, 4, 4, 16, f)]
    unnamed x17 -> x11, local copies, waits for them, and re-layouts: 1.26 us -> 0.29 us
    add x3 -> x1, other arithmetic: 0.18 us -> 0.92 us  [pos_of(): return device * LOCAL + local]
    reduce_sum x1, other arithmetic: 0.49 us -> 1.16 us  [slide_of(): jnp.sum((positions[..., None] >= slide_ends).astype(jnp.int32), axis=-1)]
where the time goes in v10:
time: 56.6 us; the launch traced here: 56.2 us
  Pallas kernels  42.9 us (76%)
  local copies, waits for them, and re-layouts  7.22 us (13%)
  other arithmetic  5.83 us (10%)
    pallas_call x1, Pallas kernels, per_device(): pl.pallas_call(attention_kernel, out_shape=jax.ShapeDtypeStruct((LOCAL, w...  42.9 us
    select_n x3, other arithmetic, per_device(): chunk = jnp.where(kv_lane[None, :] == j, piece, chunk)  2.2 us
    dynamic_slice x5, local copies, waits for them, and re-layouts, per_device(): piece = lax.dynamic_slice_in_dim(kv, starts[j], count, 0)  1.61 us
    transpose x2, local copies, waits for them, and re-layouts, to_token_major(): x = jnp.transpose(x, (4, 3, 2, 1, 0))  1.55 us
    reshape x1, local copies, waits for them, and re-layouts, from_token_major(): x = x.reshape(4, 4, 4, 16, f)  1.45 us
    reshape x2, local copies, waits for them, and re-layouts, from_token_major(): return x.reshape(f, LOCAL)  1.25 us
    concatenate x1, other arithmetic, per_device(): kv = to_token_major(jnp.concatenate([values, keys]))  1.17 us
    reduce_sum x1, other arithmetic, slide_of(): jnp.sum((positions[..., None] >= slide_ends).astype(jnp.int32), axis=-1)  1.16 us

profile of v10, /device:TPU:4, one launch (start us, length us, event | category | flops | bytes accessed | tf_op | source)
XLA Modules:
  0.0 56.2 jit_solution(5708405876130690182)
XLA Ops:
  0.0 1.2 %pad_maximum_fusion = bf16[384,1024]{1,0:T(8,128)(2,1)S(1)} fusion(bf16[192,1024]{1,0:T(8,128)(2,1)} %param.9, bf16[192,1024]{1,0:T(8,128)(2,1)} %param.10), kind=kLoop, calls=%fused_computation.1 | loop fusion | flops 1572864 | bytes 1572864 | tf_op jit(solution)/shard_map/concatenate | solution.py:261
  1.2 0.4 copy.26
  1.5 0.2 reshape.340
  1.7 0.0 copy-start.4
  1.7 0.0 copy-start.3
  1.7 0.0 copy-start.2
  1.8 0.5 copy.27
  2.2 0.0 copy-start
  2.3 0.8 %select_select_fusion.s2_ref = bf16[64,384]{1,0:T(8,128)(2,1)} fusion(bf16[1024,384]{1,0:T(8,128)(2,1)S(1)} %bitcast.37, s32[]{:T(128)S(6)} %select_n.227, s32[]{:T(128)S(6)} %select_n.226, s32[]{:T(128)S(6)} %select_n.225, s32[]{:T(128)S(6)} %select_n.224, pred[384]{0:T(512)(128)(4,1)S(1)} %get-tuple-element.12, pred[384]{0:T(512)(128)(4,1)S(1)} %get-tuple-element.11, ...), kind=kLoop, calls=%fused_computation.52 | loop fusion | flops 98304 | bytes 247312 | tf_op jit(solution)/shard_map/jit(_where)/select_n | solution.py:282
  3.1 0.6 %select_select_fusion.1.s3_ref = bf16[16,384]{1,0:T(8,128)(2,1)} fusion(bf16[1024,384]{1,0:T(8,128)(2,1)S(1)} %bitcast.38, s32[]{:T(128)S(6)} %select_n.227, s32[]{:T(128)S(6)} %select_n.226, s32[]{:T(128)S(6)} %select_n.225, s32[]{:T(128)S(6)} %select_n.224, pred[384]{0:T(512)(128)(4,1)S(1)} %get-tuple-element.12, pred[384]{0:T(512)(128)(4,1)S(1)} %get-tuple-element.11, ...), kind=kLoop, calls=%fused_computation.53 | loop fusion | flops 24576 | bytes 62992 | tf_op jit(solution)/shard_map/jit(_where)/select_n | solution.py:282
  3.7 0.1 stack.23
  3.8 0.0 copy-done.4
  3.8 0.1 fusion.31
  3.9 0.0 copy-done.3
  3.9 0.9 %fusion.5 = s32[13,1024]{1,0:T(8,128)S(1)} fusion(s32[13]{0:T(128)S(1)} %stack.23, s32[13]{0:T(128)S(1)} %copy-done.3, s32[13]{0:T(128)S(1)} %fusion.31, pred[1024]{0:T(1024)(128)(4,1)S(1)} %sign_compare_fusion.1), kind=kLoop, calls=%fused_computation.28 | loop fusion | flops 1078272 | bytes 54428 | tf_op jit(solution)/shard_map/add | solution.py:35
  4.9 0.0 copy-done.2
  4.9 0.1 copy.32
  5.0 0.1 reduce-window.8
  5.1 0.1 reduce
  5.2 1.2 %convert_reduce_fusion.sk_ref = s32[13,1024]{1,0:T(8,128)} fusion(s32[13,1024]{1,0:T(8,128)S(1)} %fusion.5, s32[64]{0:T(128)S(1)} %reduce), kind=kLoop, calls=%fused_computation | loop fusion | flops 2542592 | bytes 106752 | tf_op jit(solution)/shard_map/reduce_sum | solution.py:39
  6.3 1.1 %fusion.32 = (bf16[1,4,4,16,384]{4,0,1,2,3:T(2,128)(2,1)S(1)}, bf16[1,4,4,16,384]{4,0,1,2,3:T(2,128)(2,1)S(1)}, bf16[1,4,4,16,384]{4,0,1,2,3:T(2,128)(2,1)S(1)}, bf16[1,4,4,16,384]{4,0,1,2,3:T(2,128)(2,1)S(1)}) fusion(bf16[4,4,4,16,384]{4,0,1,2,3:T(4,128)(2,1)S(1)} %bitcast.36), kind=kLoop, calls=%fused_computation.70 | loop fusion | bytes 1572864 | tf_op jit(solution)/shard_map/dynamic_slice | solution.py:281
  7.5 0.0 copy-done
  7.5 0.1 copy.28
  7.6 0.1 copy.29
  7.7 0.1 copy.30
  7.8 0.0 copy-start.1
  7.9 0.1 copy.31
  8.0 0.8 %fusion.2.s1_ref = bf16[256,384]{1,0:T(8,128)(2,1)} fusion(bf16[1,4,4,16,384]{4,3,2,1,0:T(8,128)(2,1)S(1)} %copy.31, bf16[1,4,4,16,384]{4,3,2,1,0:T(8,128)(2,1)S(1)} %copy.30, bf16[1,4,4,16,384]{4,3,2,1,0:T(8,128)(2,1)S(1)} %copy.29, bf16[1,4,4,16,384]{4,3,2,1,0:T(8,128)(2,1)S(1)} %copy.28, pred[384]{0:T(512)(128)(4,1)S(1)} %get-tuple-element.12, ...), kind=kLoop, calls=%fused_computation.6 | loop fusion | flops 393216 | bytes 984576 | tf_op jit(solution)/shard_map/jit(_where)/select_n | solution.py:282
  8.8 0.1 copy-done.1
  8.8 0.2 copy.35
  9.1 0.2 concatenate.6.clone
  9.3 0.1 reshape.338
  9.4 1.1 %copy.25 = bf16[4,4,4,16,256]{4,3,2,1,0:T(8,128)(2,1)} copy(bf16[4,4,4,16,256]{4,0,1,2,3:T(4,128)(2,1)S(1)} %bitcast.42) | data formatting | bytes 1048576 | tf_op jit(solution)/shard_map/transpose | solution.py:22
  10.5 42.9 %shard_map.82 = bf16[1024,192]{1,0:T(8,128)(2,1)} custom-call(bf16[1024,256]{1,0:T(8,128)(2,1)} %bitcast.40, bf16[1024,384]{1,0:T(8,128)(2,1)} %bitcast.39, bf16[256,384]{1,0:T(8,128)(2,1)} %fusion.2.s1_ref, bf16[64,384]{1,0:T(8,128)(2,1)} %select_select_fusion.s2_ref, bf16[16,384]{1,0:T(8,128)(2,1)} %select_select_fusion.1.s3_ref, ...), custom_call_target="tpu_custom_call" | custom-call | tf_op jit(solution)/shard_map/pallas_call | solution.py:288
  53.5 1.4 %copy.37 = bf16[4,4,4,16,192]{4,0,1,2,3:T(4,128)(2,1)S(1)} copy(bf16[4,4,4,16,192]{4,3,2,1,0:T(8,128)(2,1)} %bitcast.41) | data formatting | bytes 786432 | tf_op jit(solution)/shard_map/reshape | solution.py:28
  54.9 0.3 reshape.347
  55.2 0.9 %copy.34 = bf16[192,1024]{1,0:T(8,128)(2,1)} copy(bf16[192,1024]{0,1:T(8,128)(2,1)S(1)} %reshape.347) | data formatting | bytes 786432 | tf_op jit(solution)/shard_map/reshape | solution.py:30
  (4 shorter events, 0.1 us)
Async XLA Ops:
  1.7 2.1 %copy-start.4 = (s32[13]{0:T(128)S(1)}, s32[13]{0:T(128)}, u32[]{:S(2)}) copy-start(s32[13]{0:T(128)} %constant.156) | copy-start | bytes 160
  1.7 2.2 %copy-start.3 = (s32[13]{0:T(128)S(1)}, s32[13]{0:T(128)}, u32[]{:S(2)}) copy-start(s32[13]{0:T(128)} %constant.151.clone) | copy-start | bytes 160
  1.7 3.1 %copy-start.2 = (s32[64]{0:T(128)S(1)}, s32[64]{0:T(128)}, u32[]{:S(2)}) copy-start(s32[64]{0:T(128)} %param.11) | copy-start | bytes 772
  2.2 5.2 %copy-start = (bf16[4,4,4,16,384]{4,3,2,1,0:T(8,128)(2,1)}, bf16[4,4,4,16,384]{4,3,2,1,0:T(8,128)(2,1)S(1)}, u32[]{:S(2)}) copy-start(bf16[4,4,4,16,384]{4,3,2,1,0:T(8,128)(2,1)S(1)} %copy.27) | copy-start | bytes 2359300
  7.8 1.0 %copy-start.1 = (bf16[192,1024]{1,0:T(8,128)(2,1)S(1)}, bf16[192,1024]{1,0:T(8,128)(2,1)}, u32[]{:S(2)}) copy-start(bf16[192,1024]{1,0:T(8,128)(2,1)} %param.8) | copy-start | bytes 1179652

commit v11 on v10

--- a/solution.py
+++ b/solution.py
@@ -40,7 +40,7 @@
 
 
 def attention_kernel(
-    q_ref, kv_ref, s1_ref, s2_ref, s3_ref, sk_ref, gain_ref, bias_ref,
+    q_ref, kv_ref, send_ref, sk_ref, gain_ref, bias_ref,
     out_ref,
     kv1, kv2, kv3, m_acc, l_acc, o_acc, stats, ybuf, cols, sqcol,
     send_sem, recv_sem, local_sem, fwd_send, fwd_recv, y_send, y_recv,
@@ -50,7 +50,7 @@
     hy = lax.axis_index("head")
     devices = lax.axis_size("seq")
     scale = 1.0 / math.sqrt(HD)
-    sends = (s1_ref, s2_ref, s3_ref)
+    sends = (send_ref.at[pl.ds(0, 256)], send_ref.at[pl.ds(256, 64)], send_ref.at[pl.ds(320, 16)])
     sqcol[...] = jnp.transpose(sk_ref[pl.ds(0, 8), :])
     bufs = (kv1, kv2, kv3)
     width = heads * HD
@@ -288,7 +288,7 @@
     out = pl.pallas_call(
         attention_kernel,
         out_shape=jax.ShapeDtypeStruct((LOCAL, width), jnp.bfloat16),
-        in_specs=[vmem] * 8,
+        in_specs=[vmem] * 6,
         out_specs=vmem,
         scratch_shapes=[
             *[pltpu.VMEM((group // 2, 2, count, 2 * width), jnp.bfloat16) for count, group in BRANCHES],
@@ -310,7 +310,7 @@
         compiler_params=pltpu.CompilerParams(
             collective_id=0, has_side_effects=True, vmem_limit_bytes=60 * 1024 * 1024
         ),
-    )(q, kv, *sends, slides, gain, bias)
+    )(q, kv, jnp.concatenate(sends), slides, gain, bias)
     return from_token_major(out)
 
 

time: 56.6 us -> 55.3 us (0.977)
  other arithmetic: 5.83 us -> 4.55 us
    select_n x3, other arithmetic: 2.2 us -> 0.2 us  [per_device(): chunk = jnp.where(kv_lane[None, :] == j, piece, chunk)]
    concatenate x0 -> x1, other arithmetic: none -> 0.72 us  [per_device(): jnp.concatenate(sends)]
where the time goes in v11:
time: 55.3 us; the launch traced here: 54.9 us
  Pallas kernels  42.9 us (78%)
  local copies, waits for them, and re-layouts  7.17 us (13%)
  other arithmetic  4.55 us (8%)
    pallas_call x1, Pallas kernels, per_device(): pl.pallas_call(attention_kernel, out_shape=jax.ShapeDtypeStruct((LOCAL, w...  42.9 us
    dynamic_slice x5, local copies, waits for them, and re-layouts, per_device(): piece = lax.dynamic_slice_in_dim(kv, starts[j], count, 0)  1.61 us
    transpose x2, local copies, waits for them, and re-layouts, to_token_major(): x = jnp.transpose(x, (4, 3, 2, 1, 0))  1.55 us
    reshape x1, local copies, waits for them, and re-layouts, from_token_major(): x = x.reshape(4, 4, 4, 16, f)  1.45 us
    reshape x2, local copies, waits for them, and re-layouts, from_token_major(): return x.reshape(f, LOCAL)  1.25 us
    concatenate x1, other arithmetic, per_device(): kv = to_token_major(jnp.concatenate([values, keys]))  1.17 us
    reduce_sum x1, other arithmetic, slide_of(): jnp.sum((positions[..., None] >= slide_ends).astype(jnp.int32), axis=-1)  1.16 us

profile of v11, /device:TPU:4, one launch (start us, length us, event | category | flops | bytes accessed | tf_op | source)
XLA Modules:
  0.0 54.9 jit_solution(1948937782493929621)
XLA Ops:
  0.0 1.2 %pad_maximum_fusion = bf16[384,1024]{1,0:T(8,128)(2,1)S(1)} fusion(bf16[192,1024]{1,0:T(8,128)(2,1)} %param.9, bf16[192,1024]{1,0:T(8,128)(2,1)} %param.10), kind=kLoop, calls=%fused_computation.1 | loop fusion | flops 1572864 | bytes 1572864 | tf_op jit(solution)/shard_map/concatenate | solution.py:261
  1.2 0.4 copy.26
  1.5 0.2 reshape.340
  1.7 0.5 copy.27
  2.2 0.0 copy-start
  2.3 1.1 %fusion.32 = (bf16[1,4,4,16,384]{4,0,1,2,3:T(2,128)(2,1)S(1)}, bf16[1,4,4,16,384]{4,0,1,2,3:T(2,128)(2,1)S(1)}, bf16[1,4,4,16,384]{4,0,1,2,3:T(2,128)(2,1)S(1)}, bf16[1,4,4,16,384]{4,0,1,2,3:T(2,128)(2,1)S(1)}) fusion(bf16[4,4,4,16,384]{4,0,1,2,3:T(4,128)(2,1)S(1)} %bitcast.36), kind=kLoop, calls=%fused_computation.71 | loop fusion | bytes 1572864 | tf_op jit(solution)/shard_map/dynamic_slice | solution.py:281
  3.5 0.0 copy-done
  3.5 0.1 copy.28
  3.6 0.1 copy.29
  3.7 0.1 copy.30
  3.9 0.1 copy.31
  4.0 0.0 copy-start.4
  4.0 0.0 copy-start.3
  4.0 0.0 copy-start.2
  4.0 0.0 copy-start.1
  4.0 0.1 fusion.2
  4.2 0.7 %pad_maximum_fusion.1.send_ref = bf16[336,384]{1,0:T(8,128)(2,1)} fusion(bf16[16,384]{1,0:T(8,128)(2,1)S(1)} %select_select_fusion.1, bf16[64,384]{1,0:T(8,128)(2,1)S(1)} %select_select_fusion, bf16[256,384]{1,0:T(8,128)(2,1)S(1)} %fusion.2), kind=kLoop, calls=%fused_computation.3 | loop fusion | flops 774144 | bytes 516096 | tf_op jit(solution)/shard_map/concatenate | solution.py:313
  4.9 0.1 stack.23
  5.0 0.0 copy-done.4
  5.0 0.1 fusion.31
  5.1 0.0 copy-done.3
  5.1 0.9 %fusion.5 = s32[13,1024]{1,0:T(8,128)S(1)} fusion(s32[13]{0:T(128)S(1)} %stack.23, s32[13]{0:T(128)S(1)} %copy-done.3, s32[13]{0:T(128)S(1)} %fusion.31, pred[1024]{0:T(1024)(128)(4,1)S(1)} %sign_compare_fusion.1), kind=kLoop, calls=%fused_computation.29 | loop fusion | flops 1078272 | bytes 54428 | tf_op jit(solution)/shard_map/add | solution.py:35
  6.1 0.0 copy-done.2
  6.1 0.1 copy.32
  6.2 0.1 reduce-window.8
  6.3 0.1 reduce
  6.4 1.2 %convert_reduce_fusion.sk_ref = s32[13,1024]{1,0:T(8,128)} fusion(s32[13,1024]{1,0:T(8,128)S(1)} %fusion.5, s32[64]{0:T(128)S(1)} %reduce), kind=kLoop, calls=%fused_computation | loop fusion | flops 2542592 | bytes 106752 | tf_op jit(solution)/shard_map/reduce_sum | solution.py:39
  7.5 0.0 copy-done.1
  7.5 0.2 copy.35
  7.7 0.2 concatenate.9.clone
  8.0 0.1 reshape.338
  8.1 1.1 %copy.25 = bf16[4,4,4,16,256]{4,3,2,1,0:T(8,128)(2,1)} copy(bf16[4,4,4,16,256]{4,0,1,2,3:T(4,128)(2,1)S(1)} %bitcast.42) | data formatting | bytes 1048576 | tf_op jit(solution)/shard_map/transpose | solution.py:22
  9.2 42.9 %shard_map.82 = bf16[1024,192]{1,0:T(8,128)(2,1)} custom-call(bf16[1024,256]{1,0:T(8,128)(2,1)} %bitcast.40, bf16[1024,384]{1,0:T(8,128)(2,1)} %bitcast.39, bf16[336,384]{1,0:T(8,128)(2,1)} %pad_maximum_fusion.1.send_ref, s32[13,1024]{1,0:T(8,128)} %convert_reduce_fusion.sk_ref, f32[1,192]{1,0:T(1,128)} %bitcast.44, f32[1,192]{1,0:T(1,128)} %bitcast.45), custom_call_target="tpu_custom_call" | custom-call | tf_op jit(solution)/shard_map/pallas_call | solution.py:288
  52.1 1.4 %copy.37 = bf16[4,4,4,16,192]{4,0,1,2,3:T(4,128)(2,1)S(1)} copy(bf16[4,4,4,16,192]{4,3,2,1,0:T(8,128)(2,1)} %bitcast.41) | data formatting | bytes 786432 | tf_op jit(solution)/shard_map/reshape | solution.py:28
  53.6 0.3 reshape.347
  53.9 0.9 %copy.34 = bf16[192,1024]{1,0:T(8,128)(2,1)} copy(bf16[192,1024]{0,1:T(8,128)(2,1)S(1)} %reshape.347) | data formatting | bytes 786432 | tf_op jit(solution)/shard_map/reshape | solution.py:30
  (6 shorter events, 0.1 us)
Async XLA Ops:
  2.2 1.3 %copy-start = (bf16[4,4,4,16,384]{4,3,2,1,0:T(8,128)(2,1)}, bf16[4,4,4,16,384]{4,3,2,1,0:T(8,128)(2,1)S(1)}, u32[]{:S(2)}) copy-start(bf16[4,4,4,16,384]{4,3,2,1,0:T(8,128)(2,1)S(1)} %copy.27) | copy-start | bytes 2359300
  4.0 1.0 %copy-start.4 = (s32[13]{0:T(128)S(1)}, s32[13]{0:T(128)}, u32[]{:S(2)}) copy-start(s32[13]{0:T(128)} %constant.156) | copy-start | bytes 160
  4.0 1.1 %copy-start.3 = (s32[13]{0:T(128)S(1)}, s32[13]{0:T(128)}, u32[]{:S(2)}) copy-start(s32[13]{0:T(128)} %constant.151.clone) | copy-start | bytes 160
  4.0 2.1 %copy-start.2 = (s32[64]{0:T(128)S(1)}, s32[64]{0:T(128)}, u32[]{:S(2)}) copy-start(s32[64]{0:T(128)} %param.11) | copy-start | bytes 772
  4.0 3.5 %copy-start.1 = (bf16[192,1024]{1,0:T(8,128)(2,1)S(1)}, bf16[192,1024]{1,0:T(8,128)(2,1)}, u32[]{:S(2)}) copy-start(bf16[192,1024]{1,0:T(8,128)(2,1)} %param.8) | copy-start | bytes 1179652

commit v12 on v11

--- a/solution.py
+++ b/solution.py
@@ -181,10 +181,9 @@
 
         lax.fori_loop(0, heads, branch, 0)
 
-    lax.fori_loop(0, 1, branch0, 0)
     pl.semaphore_wait(barrier, halves + ys - 1)
     start_pushes()
-    lax.fori_loop(1, 3, branch0, 0)
+    lax.fori_loop(0, 3, branch0, 0)
     forward(0)
     lax.fori_loop(3, LOCAL // chunk, branch0, 0)
     forward(1)

time: 55.3 us -> 55.4 us (level)
  no operation moved by 1% of the time
where the time goes in v12:
time: 55.4 us; the launch traced here: 54.9 us
  Pallas kernels  43 us (78%)
  local copies, waits for them, and re-layouts  7.17 us (13%)
  other arithmetic  4.55 us (8%)
    pallas_call x1, Pallas kernels, per_device(): pl.pallas_call(attention_kernel, out_shape=jax.ShapeDtypeStruct((LOCAL, w...  43 us
    dynamic_slice x5, local copies, waits for them, and re-layouts, per_device(): piece = lax.dynamic_slice_in_dim(kv, starts[j], count, 0)  1.61 us
    transpose x2, local copies, waits for them, and re-layouts, to_token_major(): x = jnp.transpose(x, (4, 3, 2, 1, 0))  1.55 us
    reshape x1, local copies, waits for them, and re-layouts, from_token_major(): x = x.reshape(4, 4, 4, 16, f)  1.45 us
    reshape x2, local copies, waits for them, and re-layouts, from_token_major(): return x.reshape(f, LOCAL)  1.25 us
    concatenate x1, other arithmetic, per_device(): kv = to_token_major(jnp.concatenate([values, keys]))  1.17 us
    reduce_sum x1, other arithmetic, slide_of(): jnp.sum((positions[..., None] >= slide_ends).astype(jnp.int32), axis=-1)  1.16 us

profile of v12, /device:TPU:4, one launch (start us, length us, event | category | flops | bytes accessed | tf_op | source)
XLA Modules:
  0.0 54.9 jit_solution(8911359727063156036)
XLA Ops:
  0.0 1.2 %pad_maximum_fusion = bf16[384,1024]{1,0:T(8,128)(2,1)S(1)} fusion(bf16[192,1024]{1,0:T(8,128)(2,1)} %param.9, bf16[192,1024]{1,0:T(8,128)(2,1)} %param.10), kind=kLoop, calls=%fused_computation.1 | loop fusion | flops 1572864 | bytes 1572864 | tf_op jit(solution)/shard_map/concatenate | solution.py:260
  1.2 0.4 copy.26
  1.5 0.2 reshape.340
  1.7 0.5 copy.27
  2.2 0.0 copy-start
  2.3 1.1 %fusion.32 = (bf16[1,4,4,16,384]{4,0,1,2,3:T(2,128)(2,1)S(1)}, bf16[1,4,4,16,384]{4,0,1,2,3:T(2,128)(2,1)S(1)}, bf16[1,4,4,16,384]{4,0,1,2,3:T(2,128)(2,1)S(1)}, bf16[1,4,4,16,384]{4,0,1,2,3:T(2,128)(2,1)S(1)}) fusion(bf16[4,4,4,16,384]{4,0,1,2,3:T(4,128)(2,1)S(1)} %bitcast.36), kind=kLoop, calls=%fused_computation.71 | loop fusion | bytes 1572864 | tf_op jit(solution)/shard_map/dynamic_slice | solution.py:280
  3.5 0.0 copy-done
  3.5 0.1 copy.28
  3.6 0.1 copy.29
  3.7 0.1 copy.30
  3.9 0.1 copy.31
  4.0 0.0 copy-start.4
  4.0 0.0 copy-start.3
  4.0 0.0 copy-start.2
  4.0 0.0 copy-start.1
  4.0 0.1 fusion.2
  4.2 0.7 %pad_maximum_fusion.1.send_ref = bf16[336,384]{1,0:T(8,128)(2,1)} fusion(bf16[16,384]{1,0:T(8,128)(2,1)S(1)} %select_select_fusion.1, bf16[64,384]{1,0:T(8,128)(2,1)S(1)} %select_select_fusion, bf16[256,384]{1,0:T(8,128)(2,1)S(1)} %fusion.2), kind=kLoop, calls=%fused_computation.3 | loop fusion | flops 774144 | bytes 516096 | tf_op jit(solution)/shard_map/concatenate | solution.py:312
  4.9 0.1 stack.23
  5.0 0.0 copy-done.4
  5.0 0.1 fusion.31
  5.1 0.0 copy-done.3
  5.1 0.9 %fusion.5 = s32[13,1024]{1,0:T(8,128)S(1)} fusion(s32[13]{0:T(128)S(1)} %stack.23, s32[13]{0:T(128)S(1)} %copy-done.3, s32[13]{0:T(128)S(1)} %fusion.31, pred[1024]{0:T(1024)(128)(4,1)S(1)} %sign_compare_fusion.1), kind=kLoop, calls=%fused_computation.29 | loop fusion | flops 1078272 | bytes 54428 | tf_op jit(solution)/shard_map/add | solution.py:35
  6.1 0.0 copy-done.2
  6.1 0.1 copy.32
  6.2 0.1 reduce-window.8
  6.3 0.1 reduce
  6.4 1.2 %convert_reduce_fusion.sk_ref = s32[13,1024]{1,0:T(8,128)} fusion(s32[13,1024]{1,0:T(8,128)S(1)} %fusion.5, s32[64]{0:T(128)S(1)} %reduce), kind=kLoop, calls=%fused_computation | loop fusion | flops 2542592 | bytes 106752 | tf_op jit(solution)/shard_map/reduce_sum | solution.py:39
  7.5 0.0 copy-done.1
  7.5 0.2 copy.35
  7.7 0.2 concatenate.9.clone
  8.0 0.1 reshape.338
  8.1 1.1 %copy.25 = bf16[4,4,4,16,256]{4,3,2,1,0:T(8,128)(2,1)} copy(bf16[4,4,4,16,256]{4,0,1,2,3:T(4,128)(2,1)S(1)} %bitcast.42) | data formatting | bytes 1048576 | tf_op jit(solution)/shard_map/transpose | solution.py:22
  9.2 43.0 %shard_map.82 = bf16[1024,192]{1,0:T(8,128)(2,1)} custom-call(bf16[1024,256]{1,0:T(8,128)(2,1)} %bitcast.40, bf16[1024,384]{1,0:T(8,128)(2,1)} %bitcast.39, bf16[336,384]{1,0:T(8,128)(2,1)} %pad_maximum_fusion.1.send_ref, s32[13,1024]{1,0:T(8,128)} %convert_reduce_fusion.sk_ref, f32[1,192]{1,0:T(1,128)} %bitcast.44, f32[1,192]{1,0:T(1,128)} %bitcast.45), custom_call_target="tpu_custom_call" | custom-call | tf_op jit(solution)/shard_map/pallas_call | solution.py:287
  52.2 1.4 %copy.37 = bf16[4,4,4,16,192]{4,0,1,2,3:T(4,128)(2,1)S(1)} copy(bf16[4,4,4,16,192]{4,3,2,1,0:T(8,128)(2,1)} %bitcast.41) | data formatting | bytes 786432 | tf_op jit(solution)/shard_map/reshape | solution.py:28
  53.7 0.3 reshape.347
  54.0 0.9 %copy.34 = bf16[192,1024]{1,0:T(8,128)(2,1)} copy(bf16[192,1024]{0,1:T(8,128)(2,1)S(1)} %reshape.347) | data formatting | bytes 786432 | tf_op jit(solution)/shard_map/reshape | solution.py:30
  (6 shorter events, 0.1 us)
Async XLA Ops:
  2.2 1.3 %copy-start = (bf16[4,4,4,16,384]{4,3,2,1,0:T(8,128)(2,1)}, bf16[4,4,4,16,384]{4,3,2,1,0:T(8,128)(2,1)S(1)}, u32[]{:S(2)}) copy-start(bf16[4,4,4,16,384]{4,3,2,1,0:T(8,128)(2,1)S(1)} %copy.27) | copy-start | bytes 2359300
  4.0 1.0 %copy-start.4 = (s32[13]{0:T(128)S(1)}, s32[13]{0:T(128)}, u32[]{:S(2)}) copy-start(s32[13]{0:T(128)} %constant.156) | copy-start | bytes 160
  4.0 1.1 %copy-start.3 = (s32[13]{0:T(128)S(1)}, s32[13]{0:T(128)}, u32[]{:S(2)}) copy-start(s32[13]{0:T(128)} %constant.151.clone) | copy-start | bytes 160
  4.0 2.1 %copy-start.2 = (s32[64]{0:T(128)S(1)}, s32[64]{0:T(128)}, u32[]{:S(2)}) copy-start(s32[64]{0:T(128)} %param.11) | copy-start | bytes 772
  4.0 3.5 %copy-start.1 = (bf16[192,1024]{1,0:T(8,128)(2,1)S(1)}, bf16[192,1024]{1,0:T(8,128)(2,1)}, u32[]{:S(2)}) copy-start(bf16[192,1024]{1,0:T(8,128)(2,1)} %param.8) | copy-start | bytes 1179652

commit v13 on v11

--- a/solution.py
+++ b/solution.py
@@ -40,9 +40,9 @@
 
 
 def attention_kernel(
-    q_ref, kv_ref, send_ref, sk_ref, gain_ref, bias_ref,
+    q_ref, kv_ref, send_ref, len_ref, gain_ref, bias_ref,
     out_ref,
-    kv1, kv2, kv3, m_acc, l_acc, o_acc, stats, ybuf, cols, sqcol,
+    kv1, kv2, kv3, m_acc, l_acc, o_acc, stats, ybuf, cols, sqcol, sk_ref,
     send_sem, recv_sem, local_sem, fwd_send, fwd_recv, y_send, y_recv,
 ):
     heads = 4
@@ -51,7 +51,6 @@
     devices = lax.axis_size("seq")
     scale = 1.0 / math.sqrt(HD)
     sends = (send_ref.at[pl.ds(0, 256)], send_ref.at[pl.ds(256, 64)], send_ref.at[pl.ds(320, 16)])
-    sqcol[...] = jnp.transpose(sk_ref[pl.ds(0, 8), :])
     bufs = (kv1, kv2, kv3)
     width = heads * HD
 
@@ -70,6 +69,25 @@
     ys = lax.axis_size("head")
     for o in range(1, ys):
         pl.semaphore_signal(barrier, inc=1, device_id=(me, lax.rem(hy + o, ys)), device_id_type=MESH)
+
+    row = lax.broadcasted_iota(jnp.int32, (16, LOCAL), 0)
+    column = lax.broadcasted_iota(jnp.int32, (16, LOCAL), 1)
+    shift = jnp.where(row == 0, 10, jnp.where(row <= 4, 8, jnp.where(row <= 8, 6, 4)))
+    group = jnp.where(row == 0, 1, jnp.where(row <= 4, 4, jnp.where(row <= 8, 16, 64)))
+    offset = jnp.where(row == 0, 0, ((row - 1) & 3) * 256 + jnp.where(row >= 5, hy * 64, 0))
+    device = me - (me & (group - 1)) + (column >> shift)
+    index = offset + (column & ((1 << shift) - 1))
+    local = ((index & 15) << 6) + (((index >> 4) & 3) << 4) + (((index >> 6) & 3) << 2) + (index >> 8)
+    position = device * LOCAL + local
+
+    def count_ends(k, carry):
+        end, acc = carry
+        end = end + len_ref[k]
+        return end, acc + jnp.where(position >= end, 1, 0)
+
+    _, slide = lax.fori_loop(0, len_ref.shape[0], count_ends, (jnp.int32(0), jnp.zeros((16, LOCAL), jnp.int32)))
+    sk_ref[...] = slide
+    sqcol[...] = jnp.transpose(slide[0:8])
 
     def slot(b, half, pair):
         return bufs[b].at[pair, half]
@@ -256,23 +274,10 @@
     width = heads * HD
     seq = lax.axis_index("seq")
     hy = lax.axis_index("head")
-    slide_ends = jnp.cumsum(slide_lengths)
     q = to_token_major(jnp.concatenate([jnp.zeros((SHIFT, LOCAL), queries.dtype), queries]))
     kv = to_token_major(jnp.concatenate([values, keys]))
     kv_lane = jnp.arange(2 * width) % width // HD
 
-    counts, groups, offsets = [LOCAL], [1], [0]
-    for b, (count, group) in enumerate(BRANCHES):
-        for j in range(heads):
-            counts.append(count)
-            groups.append(group)
-            offsets.append(j * 256 + (hy * 64 if b >= 1 else 0))
-    counts = jnp.array(counts, jnp.int32)[:, None]
-    groups = jnp.array(groups, jnp.int32)[:, None]
-    offsets = jnp.stack([jnp.asarray(o, jnp.int32) for o in offsets])[:, None]
-    column = jnp.arange(LOCAL, dtype=jnp.int32)[None, :]
-    devices = seq - seq % groups + column // counts
-    slides = slide_of(pos_of(devices, offsets + column % counts), slide_ends)
     sends = []
     for b, (count, group) in enumerate(BRANCHES):
         starts = [j * 256 + (hy * 64 if b >= 1 else 0) for j in range(heads)]
@@ -288,7 +293,7 @@
     out = pl.pallas_call(
         attention_kernel,
         out_shape=jax.ShapeDtypeStruct((LOCAL, width), jnp.bfloat16),
-        in_specs=[vmem] * 6,
+        in_specs=[vmem] * 3 + [pl.BlockSpec(memory_space=pltpu.SMEM)] + [vmem] * 2,
         out_specs=vmem,
         scratch_shapes=[
             *[pltpu.VMEM((group // 2, 2, count, 2 * width), jnp.bfloat16) for count, group in BRANCHES],
@@ -299,6 +304,7 @@
             pltpu.VMEM((4, 8, LOCAL), jnp.float32),
             pltpu.VMEM((LOCAL, 8), jnp.float32),
             pltpu.VMEM((LOCAL, 8), jnp.int32),
+            pltpu.VMEM((16, LOCAL), jnp.int32),
             pltpu.SemaphoreType.DMA((3,)),
             pltpu.SemaphoreType.DMA((3,)),
             pltpu.SemaphoreType.DMA((3,)),
@@ -310,7 +316,7 @@
         compiler_params=pltpu.CompilerParams(
             collective_id=0, has_side_effects=True, vmem_limit_bytes=60 * 1024 * 1024
         ),
-    )(q, kv, jnp.concatenate(sends), slides, gain, bias)
+    )(q, kv, jnp.concatenate(sends), slide_lengths, gain, bias)
     return from_token_major(out)
 
 

time: 55.3 us -> 52.6 us (0.951)
  other arithmetic: 4.55 us -> 2.14 us
    reduce_sum x1 -> x0, other arithmetic: 1.16 us -> none  [slide_of(): jnp.sum((positions[..., None] >= slide_ends).astype(jnp.int32), axis=-1)]
    add x1 -> x0, other arithmetic: 0.92 us -> none  [pos_of(): return device * LOCAL + local]
where the time goes in v13:
time: 52.6 us; the launch traced here: 52.4 us
  Pallas kernels  43 us (82%)
  local copies, waits for them, and re-layouts  7.08 us (13%)
  other arithmetic  2.14 us (4%)
    pallas_call x1, Pallas kernels, per_device(): pl.pallas_call(attention_kernel, out_shape=jax.ShapeDtypeStruct((LOCAL, w...  43 us
    dynamic_slice x5, local copies, waits for them, and re-layouts, per_device(): piece = lax.dynamic_slice_in_dim(kv, starts[j], count, 0)  1.61 us
    transpose x2, local copies, waits for them, and re-layouts, to_token_major(): x = jnp.transpose(x, (4, 3, 2, 1, 0))  1.55 us
    reshape x1, local copies, waits for them, and re-layouts, from_token_major(): x = x.reshape(4, 4, 4, 16, f)  1.45 us
    reshape x2, local copies, waits for them, and re-layouts, from_token_major(): return x.reshape(f, LOCAL)  1.25 us
    concatenate x1, other arithmetic, per_device(): kv = to_token_major(jnp.concatenate([values, keys]))  1.17 us

profile of v13, /device:TPU:4, one launch (start us, length us, event | category | flops | bytes accessed | tf_op | source)
XLA Modules:
  0.0 52.4 jit_solution(8368656802553728794)
XLA Ops:
  0.0 1.2 %pad_maximum_fusion = bf16[384,1024]{1,0:T(8,128)(2,1)S(1)} fusion(bf16[192,1024]{1,0:T(8,128)(2,1)} %param.7, bf16[192,1024]{1,0:T(8,128)(2,1)} %param.8), kind=kLoop, calls=%fused_computation | loop fusion | flops 1572864 | bytes 1572864 | tf_op jit(solution)/shard_map/concatenate | solution.py:278
  1.2 0.4 copy.12
  1.5 0.2 reshape.61
  1.7 0.5 copy.13
  2.2 0.0 copy-start
  2.3 1.1 %fusion.7 = (bf16[1,4,4,16,384]{4,0,1,2,3:T(2,128)(2,1)S(1)}, bf16[1,4,4,16,384]{4,0,1,2,3:T(2,128)(2,1)S(1)}, bf16[1,4,4,16,384]{4,0,1,2,3:T(2,128)(2,1)S(1)}, bf16[1,4,4,16,384]{4,0,1,2,3:T(2,128)(2,1)S(1)}) fusion(bf16[4,4,4,16,384]{4,0,1,2,3:T(4,128)(2,1)S(1)} %bitcast.31), kind=kLoop, calls=%fused_computation.22 | loop fusion | bytes 1572864 | tf_op jit(solution)/shard_map/dynamic_slice | solution.py:286
  3.5 0.0 copy-done
  3.5 0.1 copy.14
  3.6 0.1 copy.15
  3.7 0.1 copy.16
  3.9 0.1 copy.17
  4.0 0.0 copy-start.1
  4.0 0.1 fusion.2
  4.1 0.7 %pad_maximum_fusion.1.send_ref = bf16[336,384]{1,0:T(8,128)(2,1)} fusion(bf16[16,384]{1,0:T(8,128)(2,1)S(1)} %select_select_fusion.1, bf16[64,384]{1,0:T(8,128)(2,1)S(1)} %select_select_fusion, bf16[256,384]{1,0:T(8,128)(2,1)S(1)} %fusion.2), kind=kLoop, calls=%fused_computation.2 | loop fusion | flops 774144 | bytes 516096 | tf_op jit(solution)/shard_map/concatenate | solution.py:319
  4.9 0.1 copy-done.1
  5.0 0.2 copy.20
  5.2 0.2 concatenate.9.clone
  5.4 0.1 reshape.59
  5.6 1.1 %copy.11 = bf16[4,4,4,16,256]{4,3,2,1,0:T(8,128)(2,1)} copy(bf16[4,4,4,16,256]{4,0,1,2,3:T(4,128)(2,1)S(1)} %bitcast.35) | data formatting | bytes 1048576 | tf_op jit(solution)/shard_map/transpose | solution.py:22
  6.6 43.0 %shard_map.64 = bf16[1024,192]{1,0:T(8,128)(2,1)} custom-call(bf16[1024,256]{1,0:T(8,128)(2,1)} %bitcast.37, bf16[1024,384]{1,0:T(8,128)(2,1)} %bitcast.34, bf16[336,384]{1,0:T(8,128)(2,1)} %pad_maximum_fusion.1.send_ref, s32[64]{0:T(128)} %len_ref.1, f32[1,192]{1,0:T(1,128)} %bitcast.39, f32[1,192]{1,0:T(1,128)} %bitcast.40), custom_call_target="tpu_custom_call" | custom-call | tf_op jit(solution)/shard_map/pallas_call | solution.py:293
  49.7 1.4 %copy.22 = bf16[4,4,4,16,192]{4,0,1,2,3:T(4,128)(2,1)S(1)} copy(bf16[4,4,4,16,192]{4,3,2,1,0:T(8,128)(2,1)} %bitcast.38) | data formatting | bytes 786432 | tf_op jit(solution)/shard_map/reshape | solution.py:28
  51.1 0.3 reshape.66
  51.5 0.9 %copy.19 = bf16[192,1024]{1,0:T(8,128)(2,1)} copy(bf16[192,1024]{0,1:T(8,128)(2,1)S(1)} %reshape.66) | data formatting | bytes 786432 | tf_op jit(solution)/shard_map/reshape | solution.py:30
  (4 shorter events, 0.1 us)
Async XLA Ops:
  2.2 1.3 %copy-start = (bf16[4,4,4,16,384]{4,3,2,1,0:T(8,128)(2,1)}, bf16[4,4,4,16,384]{4,3,2,1,0:T(8,128)(2,1)S(1)}, u32[]{:S(2)}) copy-start(bf16[4,4,4,16,384]{4,3,2,1,0:T(8,128)(2,1)S(1)} %copy.13) | copy-start | bytes 2359300
  4.0 1.0 %copy-start.1 = (bf16[192,1024]{1,0:T(8,128)(2,1)S(1)}, bf16[192,1024]{1,0:T(8,128)(2,1)}, u32[]{:S(2)}) copy-start(bf16[192,1024]{1,0:T(8,128)(2,1)} %param.6) | copy-start | bytes 1179652

commit v14 on v13

--- a/solution.py
+++ b/solution.py
@@ -40,7 +40,7 @@
 
 
 def attention_kernel(
-    q_ref, kv_ref, send_ref, len_ref, gain_ref, bias_ref,
+    x_ref, send_ref, len_ref, gain_ref, bias_ref,
     out_ref,
     kv1, kv2, kv3, m_acc, l_acc, o_acc, stats, ybuf, cols, sqcol, sk_ref,
     send_sem, recv_sem, local_sem, fwd_send, fwd_recv, y_send, y_recv,
@@ -137,8 +137,8 @@
 
     def branch0(i, carry):
         rows = pl.ds(pl.multiple_of(i * chunk, chunk), chunk)
-        q = q_ref[rows]
-        kv = kv_ref[...]
+        q = x_ref[rows, pl.ds(0, 256)]
+        kv = x_ref[:, pl.ds(256, 384)]
         same = sqcol[rows, 0:1] == sk_ref[pl.ds(0, 1), :]
         mm = ll = oo = None
         for j in range(heads):
@@ -186,7 +186,7 @@
             start = j * 256 + (hy * 64 if b >= 1 else 0)
             rows = pl.ds(pl.multiple_of(start, 16), count)
             same = sqcol[rows, 0:1] == sk_ref[pl.ds(1 + b * heads + j, 1), :]
-            m_new, l_new, o_new = attend(q_ref[rows], j, bufs[b][...].reshape(LOCAL, 2 * width), same)
+            m_new, l_new, o_new = attend(x_ref[rows, pl.ds(0, 256)], j, bufs[b][...].reshape(LOCAL, 2 * width), same)
             m_old = m_acc[rows]
             mn = jnp.maximum(m_old, m_new)
             keep_old = jnp.exp(m_old - mn)
@@ -274,8 +274,8 @@
     width = heads * HD
     seq = lax.axis_index("seq")
     hy = lax.axis_index("head")
-    q = to_token_major(jnp.concatenate([jnp.zeros((SHIFT, LOCAL), queries.dtype), queries]))
-    kv = to_token_major(jnp.concatenate([values, keys]))
+    x = to_token_major(jnp.concatenate([jnp.zeros((SHIFT, LOCAL), queries.dtype), queries, values, keys]))
+    kv = x[:, 256:]
     kv_lane = jnp.arange(2 * width) % width // HD
 
     sends = []
@@ -293,7 +293,7 @@
     out = pl.pallas_call(
         attention_kernel,
         out_shape=jax.ShapeDtypeStruct((LOCAL, width), jnp.bfloat16),
-        in_specs=[vmem] * 3 + [pl.BlockSpec(memory_space=pltpu.SMEM)] + [vmem] * 2,
+        in_specs=[vmem] * 2 + [pl.BlockSpec(memory_space=pltpu.SMEM)] + [vmem] * 2,
         out_specs=vmem,
         scratch_shapes=[
             *[pltpu.VMEM((group // 2, 2, count, 2 * width), jnp.bfloat16) for count, group in BRANCHES],
@@ -316,7 +316,7 @@
         compiler_params=pltpu.CompilerParams(
             collective_id=0, has_side_effects=True, vmem_limit_bytes=60 * 1024 * 1024
         ),
-    )(q, kv, jnp.concatenate(sends), slide_lengths, gain, bias)
+    )(x, jnp.concatenate(sends), slide_lengths, gain, bias)
     return from_token_major(out)
 
 

time: 52.6 us -> 53.2 us (1.011)
    dynamic_slice x5 -> x0, local copies, waits for them, and re-layouts: 1.61 us -> none  [per_device(): piece = lax.dynamic_slice_in_dim(kv, starts[j], count, 0)]
    reshape x2 -> x1, local copies, waits for them, and re-layouts: 0.31 us -> 1.23 us  [to_token_major(): x = x.reshape(f, 16, 4, 4, 4)]
    transpose x2 -> x1, local copies, waits for them, and re-layouts: 1.55 us -> 2.06 us  [to_token_major(): x = jnp.transpose(x, (4, 3, 2, 1, 0))]
where the time goes in v14:
time: 53.2 us; the launch traced here: 53 us
  Pallas kernels  43 us (81%)
  local copies, waits for them, and re-layouts  7.58 us (14%)
  other arithmetic  2.39 us (4%)
    pallas_call x1, Pallas kernels, per_device(): pl.pallas_call(attention_kernel, out_shape=jax.ShapeDtypeStruct((LOCAL, w...  43 us
    transpose x1, local copies, waits for them, and re-layouts, to_token_major(): x = jnp.transpose(x, (4, 3, 2, 1, 0))  2.06 us
    concatenate x1, other arithmetic, per_device(): jnp.concatenate([jnp.zeros((SHIFT, LOCAL), queries.dtype), queries, value...  1.5 us
    reshape x1, local copies, waits for them, and re-layouts, from_token_major(): x = x.reshape(4, 4, 4, 16, f)  1.45 us
    reshape x2, local copies, waits for them, and re-layouts, from_token_major(): return x.reshape(f, LOCAL)  1.25 us
    reshape x1, local copies, waits for them, and re-layouts, to_token_major(): x = x.reshape(f, 16, 4, 4, 4)  1.23 us

profile of v14, /device:TPU:4, one launch (start us, length us, event | category | flops | bytes accessed | tf_op | source)
XLA Modules:
  0.0 53.0 jit_solution(8963936113059498407)
XLA Ops:
  0.0 1.5 %pad_maximum_fusion = bf16[640,1024]{1,0:T(8,128)(2,1)S(1)} fusion(bf16[192,1024]{1,0:T(8,128)(2,1)} %param.7, bf16[192,1024]{1,0:T(8,128)(2,1)} %param.8, bf16[192,1024]{1,0:T(8,128)(2,1)} %param.6, bf16[640]{0:T(1024)(128)(2,1)S(1)} %pad.3.clone), kind=kLoop, calls=%fused_computation | loop fusion | flops 5242880 | bytes 2491648 | tf_op jit(solution)/shard_map/concatenate | solution.py:277
  1.5 0.7 %copy.9 = bf16[640,1024]{0,1:T(8,128)(2,1)S(1)} copy(bf16[640,1024]{1,0:T(8,128)(2,1)S(1)} %pad_maximum_fusion) | data formatting | bytes 2621440 | tf_op jit(solution)/shard_map/concatenate | solution.py:277
  2.3 1.2 %reshape.49 = bf16[640,16,4,4,4]{0,4,3,2,1:T(4,128)(2,1)} reshape(bf16[640,1024]{0,1:T(8,128)(2,1)S(1)} %copy.9) | data formatting | bytes 2621440 | tf_op jit(solution)/shard_map/reshape | solution.py:21
  3.5 2.1 %copy.10 = bf16[4,4,4,16,640]{4,3,2,1,0:T(8,128)(2,1)S(1)} copy(bf16[4,4,4,16,640]{4,0,1,2,3:T(4,128)(2,1)} %bitcast.15) | data formatting | bytes 2621440 | tf_op jit(solution)/shard_map/transpose | solution.py:22
  5.6 0.0 copy-start
  5.6 0.1 slice.8
  5.8 0.1 fusion.2
  5.8 0.8 %copy-done = bf16[4,4,4,16,640]{4,3,2,1,0:T(8,128)(2,1)} copy-done((bf16[4,4,4,16,640]{4,3,2,1,0:T(8,128)(2,1)}, bf16[4,4,4,16,640]{4,3,2,1,0:T(8,128)(2,1)S(1)}, u32[]{:S(2)}) %copy-start) | copy-done | bytes 1310744
  6.6 0.7 %pad_maximum_fusion.1.send_ref = bf16[336,384]{1,0:T(8,128)(2,1)} fusion(bf16[16,384]{1,0:T(8,128)(2,1)S(1)} %select_select_fusion.1, bf16[64,384]{1,0:T(8,128)(2,1)S(1)} %select_select_fusion, bf16[256,384]{1,0:T(8,128)(2,1)S(1)} %fusion.2), kind=kLoop, calls=%fused_computation.2 | loop fusion | flops 774144 | bytes 516096 | tf_op jit(solution)/shard_map/concatenate | solution.py:319
  7.3 43.0 %shard_map.64 = bf16[1024,192]{1,0:T(8,128)(2,1)} custom-call(bf16[1024,640]{1,0:T(8,128)(2,1)} %bitcast.14, bf16[336,384]{1,0:T(8,128)(2,1)} %pad_maximum_fusion.1.send_ref, s32[64]{0:T(128)} %len_ref.1, f32[1,192]{1,0:T(1,128)} %bitcast.18, f32[1,192]{1,0:T(1,128)} %bitcast.19), custom_call_target="tpu_custom_call" | custom-call | tf_op jit(solution)/shard_map/pallas_call | solution.py:293
  50.3 1.4 %copy.14 = bf16[4,4,4,16,192]{4,0,1,2,3:T(4,128)(2,1)S(1)} copy(bf16[4,4,4,16,192]{4,3,2,1,0:T(8,128)(2,1)} %bitcast.17) | data formatting | bytes 786432 | tf_op jit(solution)/shard_map/reshape | solution.py:28
  51.8 0.3 reshape.54
  52.1 0.9 %copy.12 = bf16[192,1024]{1,0:T(8,128)(2,1)} copy(bf16[192,1024]{0,1:T(8,128)(2,1)S(1)} %reshape.54) | data formatting | bytes 786432 | tf_op jit(solution)/shard_map/reshape | solution.py:30
  (6 shorter events, 0.1 us)
Async XLA Ops:
  5.6 1.1 %copy-start = (bf16[4,4,4,16,640]{4,3,2,1,0:T(8,128)(2,1)}, bf16[4,4,4,16,640]{4,3,2,1,0:T(8,128)(2,1)S(1)}, u32[]{:S(2)}) copy-start(bf16[4,4,4,16,640]{4,3,2,1,0:T(8,128)(2,1)S(1)} %copy.10) | copy-start | bytes 3932164

commit v15 on v13

--- a/solution.py
+++ b/solution.py
@@ -23,6 +23,13 @@
     return x.reshape(LOCAL, f)
 
 
+def from_digit_order(x):
+    f = x.shape[0]
+    x = x.reshape(f, 4, 4, 4, 16)
+    x = jnp.transpose(x, (0, 4, 3, 2, 1))
+    return x.reshape(f, LOCAL)
+
+
 def from_token_major(x):
     f = x.shape[1]
     x = x.reshape(4, 4, 4, 16, f)
@@ -42,7 +49,7 @@
 def attention_kernel(
     q_ref, kv_ref, send_ref, len_ref, gain_ref, bias_ref,
     out_ref,
-    kv1, kv2, kv3, m_acc, l_acc, o_acc, stats, ybuf, cols, sqcol, sk_ref,
+    kv1, kv2, kv3, m_acc, l_acc, o_acc, stats, ybuf, cols, sqcol, sk_ref, zbuf,
     send_sem, recv_sem, local_sem, fwd_send, fwd_recv, y_send, y_recv,
 ):
     heads = 4
@@ -256,7 +263,8 @@
         rows = pl.ds(pl.multiple_of(i * chunk, chunk), chunk)
         col = cols[rows]
         normed = (o_acc[rows] - col[:, 0:1]) * col[:, 1:2]
-        out_ref[rows] = (normed[:, : heads * HD] * gain_ref[...] + bias_ref[...]).astype(out_ref.dtype)
+        zbuf[:, 0 : heads * HD] = normed[:, : heads * HD] * gain_ref[...] + bias_ref[...]
+        out_ref[:, rows] = jnp.transpose(zbuf[...])[0 : heads * HD].astype(out_ref.dtype)
         return carry
 
     lax.fori_loop(0, LOCAL // chunk, normalize, 0)
@@ -292,7 +300,7 @@
     vmem = pl.BlockSpec(memory_space=pltpu.VMEM)
     out = pl.pallas_call(
         attention_kernel,
-        out_shape=jax.ShapeDtypeStruct((LOCAL, width), jnp.bfloat16),
+        out_shape=jax.ShapeDtypeStruct((width, LOCAL), jnp.bfloat16),
         in_specs=[vmem] * 3 + [pl.BlockSpec(memory_space=pltpu.SMEM)] + [vmem] * 2,
         out_specs=vmem,
         scratch_shapes=[
@@ -305,6 +313,7 @@
             pltpu.VMEM((LOCAL, 8), jnp.float32),
             pltpu.VMEM((LOCAL, 8), jnp.int32),
             pltpu.VMEM((16, LOCAL), jnp.int32),
+            pltpu.VMEM((256, 256), jnp.float32),
             pltpu.SemaphoreType.DMA((3,)),
             pltpu.SemaphoreType.DMA((3,)),
             pltpu.SemaphoreType.DMA((3,)),
@@ -317,7 +326,7 @@
             collective_id=0, has_side_effects=True, vmem_limit_bytes=60 * 1024 * 1024
         ),
     )(q, kv, jnp.concatenate(sends), slide_lengths, gain, bias)
-    return from_token_major(out)
+    return from_digit_order(out)
 
 
 def solution(mesh):

time: 52.6 us -> 53.1 us (level)
    reshape x3 -> x2, local copies, waits for them, and re-layouts: 2.7 us -> 1.25 us  [from_digit_order(): return x.reshape(f, LOCAL)]
    pallas_call x0 -> x1, local copies, waits for them, and re-layouts: none -> 1.2 us  [per_device(): pl.pallas_call(attention_kernel, out_shape=jax.ShapeDtypeStruct((width, L...]
where the time goes in v15:
time: 53.1 us; the launch traced here: 52.9 us
  Pallas kernels  43.4 us (82%)
  local copies, waits for them, and re-layouts  7.24 us (14%)
  other arithmetic  2.14 us (4%)
    pallas_call x1, Pallas kernels, per_device(): pl.pallas_call(attention_kernel, out_shape=jax.ShapeDtypeStruct((width, L...  43.4 us
    dynamic_slice x5, local copies, waits for them, and re-layouts, per_device(): piece = lax.dynamic_slice_in_dim(kv, starts[j], count, 0)  1.61 us
    transpose x2, local copies, waits for them, and re-layouts, to_token_major(): x = jnp.transpose(x, (4, 3, 2, 1, 0))  1.55 us
    reshape x2, local copies, waits for them, and re-layouts, from_digit_order(): return x.reshape(f, LOCAL)  1.25 us
    pallas_call x1, local copies, waits for them, and re-layouts, per_device(): pl.pallas_call(attention_kernel, out_shape=jax.ShapeDtypeStruct((width, L...  1.2 us
    concatenate x1, other arithmetic, per_device(): kv = to_token_major(jnp.concatenate([values, keys]))  1.17 us

profile of v15, /device:TPU:4, one launch (start us, length us, event | category | flops | bytes accessed | tf_op | source)
XLA Modules:
  0.0 52.9 jit_solution(5225511649705547106)
XLA Ops:
  0.0 1.2 %pad_maximum_fusion = bf16[384,1024]{1,0:T(8,128)(2,1)S(1)} fusion(bf16[192,1024]{1,0:T(8,128)(2,1)} %param.7, bf16[192,1024]{1,0:T(8,128)(2,1)} %param.8), kind=kLoop, calls=%fused_computation | loop fusion | flops 1572864 | bytes 1572864 | tf_op jit(solution)/shard_map/concatenate | solution.py:286
  1.2 0.4 copy.12
  1.5 0.2 reshape.61
  1.7 0.5 copy.13
  2.2 0.0 copy-start
  2.3 1.1 %fusion.7 = (bf16[1,4,4,16,384]{4,0,1,2,3:T(2,128)(2,1)S(1)}, bf16[1,4,4,16,384]{4,0,1,2,3:T(2,128)(2,1)S(1)}, bf16[1,4,4,16,384]{4,0,1,2,3:T(2,128)(2,1)S(1)}, bf16[1,4,4,16,384]{4,0,1,2,3:T(2,128)(2,1)S(1)}) fusion(bf16[4,4,4,16,384]{4,0,1,2,3:T(4,128)(2,1)S(1)} %bitcast.30), kind=kLoop, calls=%fused_computation.21 | loop fusion | bytes 1572864 | tf_op jit(solution)/shard_map/dynamic_slice | solution.py:294
  3.5 0.0 copy-done
  3.5 0.1 copy.14
  3.6 0.1 copy.15
  3.7 0.1 copy.16
  3.9 0.1 copy.17
  4.0 0.0 copy-start.1
  4.0 0.1 fusion.2
  4.1 0.7 %pad_maximum_fusion.1.send_ref = bf16[336,384]{1,0:T(8,128)(2,1)} fusion(bf16[16,384]{1,0:T(8,128)(2,1)S(1)} %select_select_fusion.1, bf16[64,384]{1,0:T(8,128)(2,1)S(1)} %select_select_fusion, bf16[256,384]{1,0:T(8,128)(2,1)S(1)} %fusion.2), kind=kLoop, calls=%fused_computation.1 | loop fusion | flops 774144 | bytes 516096 | tf_op jit(solution)/shard_map/concatenate | solution.py:328
  4.9 0.1 copy-done.1
  5.0 0.2 copy.21
  5.2 0.2 concatenate.9.clone
  5.4 0.1 reshape.59
  5.6 1.1 %copy.11 = bf16[4,4,4,16,256]{4,3,2,1,0:T(8,128)(2,1)} copy(bf16[4,4,4,16,256]{4,0,1,2,3:T(4,128)(2,1)S(1)} %bitcast.36) | data formatting | bytes 1048576 | tf_op jit(solution)/shard_map/transpose | solution.py:22
  6.6 43.4 %shard_map.64 = bf16[192,1024]{1,0:T(8,128)(2,1)} custom-call(bf16[1024,256]{1,0:T(8,128)(2,1)} %bitcast.34, bf16[1024,384]{1,0:T(8,128)(2,1)} %bitcast.33, bf16[336,384]{1,0:T(8,128)(2,1)} %pad_maximum_fusion.1.send_ref, s32[64]{0:T(128)} %len_ref.1, f32[1,192]{1,0:T(1,128)} %bitcast.37, f32[1,192]{1,0:T(1,128)} %bitcast.38), custom_call_target="tpu_custom_call" | custom-call | tf_op jit(solution)/shard_map/pallas_call | solution.py:301
  50.0 1.2 %copy.18 = bf16[192,1024]{0,1:T(8,128)(2,1)S(1)} copy(bf16[192,1024]{1,0:T(8,128)(2,1)} %shard_map.64) | data formatting | bytes 786432 | tf_op jit(solution)/shard_map/pallas_call | solution.py:301
  51.2 0.4 copy.19
  51.6 0.3 reshape.66
  52.0 0.9 %copy.20 = bf16[192,1024]{1,0:T(8,128)(2,1)} copy(bf16[192,1024]{0,1:T(8,128)(2,1)S(1)} %reshape.66) | data formatting | bytes 786432 | tf_op jit(solution)/shard_map/reshape | solution.py:30
  (4 shorter events, 0.1 us)
Async XLA Ops:
  2.2 1.3 %copy-start = (bf16[4,4,4,16,384]{4,3,2,1,0:T(8,128)(2,1)}, bf16[4,4,4,16,384]{4,3,2,1,0:T(8,128)(2,1)S(1)}, u32[]{:S(2)}) copy-start(bf16[4,4,4,16,384]{4,3,2,1,0:T(8,128)(2,1)S(1)} %copy.13) | copy-start | bytes 2359300
  4.0 1.0 %copy-start.1 = (bf16[192,1024]{1,0:T(8,128)(2,1)S(1)}, bf16[192,1024]{1,0:T(8,128)(2,1)}, u32[]{:S(2)}) copy-start(bf16[192,1024]{1,0:T(8,128)(2,1)} %param.6) | copy-start | bytes 1179652

commit v16 on v13

--- a/solution.py
+++ b/solution.py
@@ -100,7 +100,7 @@
         cp.start()
         locals_.append(cp)
     def start_pushes():
-        for b, (count, group) in enumerate(BRANCHES):
+        for b, (count, group) in reversed(list(enumerate(BRANCHES))):
             member = lax.rem(me, group)
             first = me - member
             pairs = group // 2

time: 52.6 us -> 55.7 us (1.059); the launches traced: 52.4 us -> 54.8 us
  Pallas kernels: 43 us -> 45.5 us
    pallas_call x1, Pallas kernels: 43 us -> 45.5 us  [per_device(): pl.pallas_call(attention_kernel, out_shape=jax.ShapeDtypeStruct((LOCAL, w...]
where the time goes in v16:
time: 55.7 us; the launch traced here: 54.8 us
  Pallas kernels  45.5 us (82%)
  local copies, waits for them, and re-layouts  7.08 us (13%)
  other arithmetic  2.14 us (4%)
    pallas_call x1, Pallas kernels, per_device(): pl.pallas_call(attention_kernel, out_shape=jax.ShapeDtypeStruct((LOCAL, w...  45.5 us
    dynamic_slice x5, local copies, waits for them, and re-layouts, per_device(): piece = lax.dynamic_slice_in_dim(kv, starts[j], count, 0)  1.61 us
    transpose x2, local copies, waits for them, and re-layouts, to_token_major(): x = jnp.transpose(x, (4, 3, 2, 1, 0))  1.55 us
    reshape x1, local copies, waits for them, and re-layouts, from_token_major(): x = x.reshape(4, 4, 4, 16, f)  1.45 us
    reshape x2, local copies, waits for them, and re-layouts, from_token_major(): return x.reshape(f, LOCAL)  1.25 us
    concatenate x1, other arithmetic, per_device(): kv = to_token_major(jnp.concatenate([values, keys]))  1.17 us

profile of v16, /device:TPU:4, one launch (start us, length us, event | category | flops | bytes accessed | tf_op | source)
XLA Modules:
  0.0 54.8 jit_solution(2827610873487709143)
XLA Ops:
  0.0 1.2 %pad_maximum_fusion = bf16[384,1024]{1,0:T(8,128)(2,1)S(1)} fusion(bf16[192,1024]{1,0:T(8,128)(2,1)} %param.7, bf16[192,1024]{1,0:T(8,128)(2,1)} %param.8), kind=kLoop, calls=%fused_computation | loop fusion | flops 1572864 | bytes 1572864 | tf_op jit(solution)/shard_map/concatenate | solution.py:278
  1.2 0.4 copy.12
  1.5 0.2 reshape.61
  1.7 0.5 copy.13
  2.2 0.0 copy-start
  2.3 1.1 %fusion.7 = (bf16[1,4,4,16,384]{4,0,1,2,3:T(2,128)(2,1)S(1)}, bf16[1,4,4,16,384]{4,0,1,2,3:T(2,128)(2,1)S(1)}, bf16[1,4,4,16,384]{4,0,1,2,3:T(2,128)(2,1)S(1)}, bf16[1,4,4,16,384]{4,0,1,2,3:T(2,128)(2,1)S(1)}) fusion(bf16[4,4,4,16,384]{4,0,1,2,3:T(4,128)(2,1)S(1)} %bitcast.31), kind=kLoop, calls=%fused_computation.22 | loop fusion | bytes 1572864 | tf_op jit(solution)/shard_map/dynamic_slice | solution.py:286
  3.5 0.0 copy-done
  3.5 0.1 copy.14
  3.6 0.1 copy.15
  3.7 0.1 copy.16
  3.9 0.1 copy.17
  4.0 0.0 copy-start.1
  4.0 0.1 fusion.2
  4.1 0.7 %pad_maximum_fusion.1.send_ref = bf16[336,384]{1,0:T(8,128)(2,1)} fusion(bf16[16,384]{1,0:T(8,128)(2,1)S(1)} %select_select_fusion.1, bf16[64,384]{1,0:T(8,128)(2,1)S(1)} %select_select_fusion, bf16[256,384]{1,0:T(8,128)(2,1)S(1)} %fusion.2), kind=kLoop, calls=%fused_computation.2 | loop fusion | flops 774144 | bytes 516096 | tf_op jit(solution)/shard_map/concatenate | solution.py:319
  4.9 0.1 copy-done.1
  5.0 0.2 copy.20
  5.2 0.2 concatenate.9.clone
  5.4 0.1 reshape.59
  5.6 1.1 %copy.11 = bf16[4,4,4,16,256]{4,3,2,1,0:T(8,128)(2,1)} copy(bf16[4,4,4,16,256]{4,0,1,2,3:T(4,128)(2,1)S(1)} %bitcast.35) | data formatting | bytes 1048576 | tf_op jit(solution)/shard_map/transpose | solution.py:22
  6.6 45.5 %shard_map.64 = bf16[1024,192]{1,0:T(8,128)(2,1)} custom-call(bf16[1024,256]{1,0:T(8,128)(2,1)} %bitcast.37, bf16[1024,384]{1,0:T(8,128)(2,1)} %bitcast.34, bf16[336,384]{1,0:T(8,128)(2,1)} %pad_maximum_fusion.1.send_ref, s32[64]{0:T(128)} %len_ref.1, f32[1,192]{1,0:T(1,128)} %bitcast.39, f32[1,192]{1,0:T(1,128)} %bitcast.40), custom_call_target="tpu_custom_call" | custom-call | tf_op jit(solution)/shard_map/pallas_call | solution.py:293
  52.1 1.4 %copy.22 = bf16[4,4,4,16,192]{4,0,1,2,3:T(4,128)(2,1)S(1)} copy(bf16[4,4,4,16,192]{4,3,2,1,0:T(8,128)(2,1)} %bitcast.38) | data formatting | bytes 786432 | tf_op jit(solution)/shard_map/reshape | solution.py:28
  53.6 0.3 reshape.66
  53.9 0.9 %copy.19 = bf16[192,1024]{1,0:T(8,128)(2,1)} copy(bf16[192,1024]{0,1:T(8,128)(2,1)S(1)} %reshape.66) | data formatting | bytes 786432 | tf_op jit(solution)/shard_map/reshape | solution.py:30
  (4 shorter events, 0.1 us)
Async XLA Ops:
  2.2 1.3 %copy-start = (bf16[4,4,4,16,384]{4,3,2,1,0:T(8,128)(2,1)}, bf16[4,4,4,16,384]{4,3,2,1,0:T(8,128)(2,1)S(1)}, u32[]{:S(2)}) copy-start(bf16[4,4,4,16,384]{4,3,2,1,0:T(8,128)(2,1)S(1)} %copy.13) | copy-start | bytes 2359300
  4.0 1.0 %copy-start.1 = (bf16[192,1024]{1,0:T(8,128)(2,1)S(1)}, bf16[192,1024]{1,0:T(8,128)(2,1)}, u32[]{:S(2)}) copy-start(bf16[192,1024]{1,0:T(8,128)(2,1)} %param.6) | copy-start | bytes 1179652

commit v17 on v13

--- a/solution.py
+++ b/solution.py
@@ -202,9 +202,8 @@
     lax.fori_loop(0, 1, branch0, 0)
     pl.semaphore_wait(barrier, halves + ys - 1)
     start_pushes()
-    lax.fori_loop(1, 3, branch0, 0)
+    lax.fori_loop(1, LOCAL // chunk, branch0, 0)
     forward(0)
-    lax.fori_loop(3, LOCAL // chunk, branch0, 0)
     forward(1)
     later(0)
     forward(2)

time: 52.6 us -> 52.4 us (level)
  no operation moved by 1% of the time
where the time goes in v17:
time: 52.4 us; the launch traced here: 52.2 us
  Pallas kernels  42.8 us (82%)
  local copies, waits for them, and re-layouts  7.08 us (14%)
  other arithmetic  2.14 us (4%)
    pallas_call x1, Pallas kernels, per_device(): pl.pallas_call(attention_kernel, out_shape=jax.ShapeDtypeStruct((LOCAL, w...  42.8 us
    dynamic_slice x5, local copies, waits for them, and re-layouts, per_device(): piece = lax.dynamic_slice_in_dim(kv, starts[j], count, 0)  1.61 us
    transpose x2, local copies, waits for them, and re-layouts, to_token_major(): x = jnp.transpose(x, (4, 3, 2, 1, 0))  1.55 us
    reshape x1, local copies, waits for them, and re-layouts, from_token_major(): x = x.reshape(4, 4, 4, 16, f)  1.45 us
    reshape x2, local copies, waits for them, and re-layouts, from_token_major(): return x.reshape(f, LOCAL)  1.25 us
    concatenate x1, other arithmetic, per_device(): kv = to_token_major(jnp.concatenate([values, keys]))  1.17 us

profile of v17, /device:TPU:4, one launch (start us, length us, event | category | flops | bytes accessed | tf_op | source)
XLA Modules:
  0.0 52.2 jit_solution(14643720439862623851)
XLA Ops:
  0.0 1.2 %pad_maximum_fusion = bf16[384,1024]{1,0:T(8,128)(2,1)S(1)} fusion(bf16[192,1024]{1,0:T(8,128)(2,1)} %param.7, bf16[192,1024]{1,0:T(8,128)(2,1)} %param.8), kind=kLoop, calls=%fused_computation | loop fusion | flops 1572864 | bytes 1572864 | tf_op jit(solution)/shard_map/concatenate | solution.py:277
  1.2 0.4 copy.12
  1.5 0.2 reshape.61
  1.7 0.5 copy.13
  2.2 0.0 copy-start
  2.3 1.1 %fusion.7 = (bf16[1,4,4,16,384]{4,0,1,2,3:T(2,128)(2,1)S(1)}, bf16[1,4,4,16,384]{4,0,1,2,3:T(2,128)(2,1)S(1)}, bf16[1,4,4,16,384]{4,0,1,2,3:T(2,128)(2,1)S(1)}, bf16[1,4,4,16,384]{4,0,1,2,3:T(2,128)(2,1)S(1)}) fusion(bf16[4,4,4,16,384]{4,0,1,2,3:T(4,128)(2,1)S(1)} %bitcast.31), kind=kLoop, calls=%fused_computation.22 | loop fusion | bytes 1572864 | tf_op jit(solution)/shard_map/dynamic_slice | solution.py:285
  3.5 0.0 copy-done
  3.5 0.1 copy.14
  3.6 0.1 copy.15
  3.7 0.1 copy.16
  3.9 0.1 copy.17
  4.0 0.0 copy-start.1
  4.0 0.1 fusion.2
  4.1 0.7 %pad_maximum_fusion.1.send_ref = bf16[336,384]{1,0:T(8,128)(2,1)} fusion(bf16[16,384]{1,0:T(8,128)(2,1)S(1)} %select_select_fusion.1, bf16[64,384]{1,0:T(8,128)(2,1)S(1)} %select_select_fusion, bf16[256,384]{1,0:T(8,128)(2,1)S(1)} %fusion.2), kind=kLoop, calls=%fused_computation.2 | loop fusion | flops 774144 | bytes 516096 | tf_op jit(solution)/shard_map/concatenate | solution.py:318
  4.9 0.1 copy-done.1
  5.0 0.2 copy.20
  5.2 0.2 concatenate.9.clone
  5.4 0.1 reshape.59
  5.6 1.1 %copy.11 = bf16[4,4,4,16,256]{4,3,2,1,0:T(8,128)(2,1)} copy(bf16[4,4,4,16,256]{4,0,1,2,3:T(4,128)(2,1)S(1)} %bitcast.35) | data formatting | bytes 1048576 | tf_op jit(solution)/shard_map/transpose | solution.py:22
  6.6 42.8 %shard_map.64 = bf16[1024,192]{1,0:T(8,128)(2,1)} custom-call(bf16[1024,256]{1,0:T(8,128)(2,1)} %bitcast.37, bf16[1024,384]{1,0:T(8,128)(2,1)} %bitcast.34, bf16[336,384]{1,0:T(8,128)(2,1)} %pad_maximum_fusion.1.send_ref, s32[64]{0:T(128)} %len_ref.1, f32[1,192]{1,0:T(1,128)} %bitcast.39, f32[1,192]{1,0:T(1,128)} %bitcast.40), custom_call_target="tpu_custom_call" | custom-call | tf_op jit(solution)/shard_map/pallas_call | solution.py:292
  49.5 1.4 %copy.22 = bf16[4,4,4,16,192]{4,0,1,2,3:T(4,128)(2,1)S(1)} copy(bf16[4,4,4,16,192]{4,3,2,1,0:T(8,128)(2,1)} %bitcast.38) | data formatting | bytes 786432 | tf_op jit(solution)/shard_map/reshape | solution.py:28
  51.0 0.3 reshape.66
  51.3 0.9 %copy.19 = bf16[192,1024]{1,0:T(8,128)(2,1)} copy(bf16[192,1024]{0,1:T(8,128)(2,1)S(1)} %reshape.66) | data formatting | bytes 786432 | tf_op jit(solution)/shard_map/reshape | solution.py:30
  (4 shorter events, 0.1 us)
Async XLA Ops:
  2.2 1.3 %copy-start = (bf16[4,4,4,16,384]{4,3,2,1,0:T(8,128)(2,1)}, bf16[4,4,4,16,384]{4,3,2,1,0:T(8,128)(2,1)S(1)}, u32[]{:S(2)}) copy-start(bf16[4,4,4,16,384]{4,3,2,1,0:T(8,128)(2,1)S(1)} %copy.13) | copy-start | bytes 2359300
  4.0 1.0 %copy-start.1 = (bf16[192,1024]{1,0:T(8,128)(2,1)S(1)}, bf16[192,1024]{1,0:T(8,128)(2,1)}, u32[]{:S(2)}) copy-start(bf16[192,1024]{1,0:T(8,128)(2,1)} %param.6) | copy-start | bytes 1179652

commit v18 on v17

--- a/solution.py
+++ b/solution.py
@@ -204,8 +204,8 @@
     start_pushes()
     lax.fori_loop(1, LOCAL // chunk, branch0, 0)
     forward(0)
+    later(0)
     forward(1)
-    later(0)
     forward(2)
     later(1)
     later(2)

time: 52.4 us -> 52.7 us (level); the launches traced: 52.2 us -> 52 us
  no operation moved by 1% of the time
where the time goes in v18:
time: 52.7 us; the launch traced here: 52 us
  Pallas kernels  42.6 us (81%)
  local copies, waits for them, and re-layouts  7.08 us (13%)
  other arithmetic  2.14 us (4%)
    pallas_call x1, Pallas kernels, per_device(): pl.pallas_call(attention_kernel, out_shape=jax.ShapeDtypeStruct((LOCAL, w...  42.6 us
    dynamic_slice x5, local copies, waits for them, and re-layouts, per_device(): piece = lax.dynamic_slice_in_dim(kv, starts[j], count, 0)  1.61 us
    transpose x2, local copies, waits for them, and re-layouts, to_token_major(): x = jnp.transpose(x, (4, 3, 2, 1, 0))  1.55 us
    reshape x1, local copies, waits for them, and re-layouts, from_token_major(): x = x.reshape(4, 4, 4, 16, f)  1.45 us
    reshape x2, local copies, waits for them, and re-layouts, from_token_major(): return x.reshape(f, LOCAL)  1.25 us
    concatenate x1, other arithmetic, per_device(): kv = to_token_major(jnp.concatenate([values, keys]))  1.17 us

profile of v18, /device:TPU:4, one launch (start us, length us, event | category | flops | bytes accessed | tf_op | source)
XLA Modules:
  0.0 52.0 jit_solution(145741489241628780)
XLA Ops:
  0.0 1.2 %pad_maximum_fusion = bf16[384,1024]{1,0:T(8,128)(2,1)S(1)} fusion(bf16[192,1024]{1,0:T(8,128)(2,1)} %param.7, bf16[192,1024]{1,0:T(8,128)(2,1)} %param.8), kind=kLoop, calls=%fused_computation | loop fusion | flops 1572864 | bytes 1572864 | tf_op jit(solution)/shard_map/concatenate | solution.py:277
  1.2 0.4 copy.12
  1.5 0.2 reshape.61
  1.7 0.5 copy.13
  2.2 0.0 copy-start
  2.3 1.1 %fusion.7 = (bf16[1,4,4,16,384]{4,0,1,2,3:T(2,128)(2,1)S(1)}, bf16[1,4,4,16,384]{4,0,1,2,3:T(2,128)(2,1)S(1)}, bf16[1,4,4,16,384]{4,0,1,2,3:T(2,128)(2,1)S(1)}, bf16[1,4,4,16,384]{4,0,1,2,3:T(2,128)(2,1)S(1)}) fusion(bf16[4,4,4,16,384]{4,0,1,2,3:T(4,128)(2,1)S(1)} %bitcast.31), kind=kLoop, calls=%fused_computation.22 | loop fusion | bytes 1572864 | tf_op jit(solution)/shard_map/dynamic_slice | solution.py:285
  3.5 0.0 copy-done
  3.5 0.1 copy.14
  3.6 0.1 copy.15
  3.7 0.1 copy.16
  3.9 0.1 copy.17
  4.0 0.0 copy-start.1
  4.0 0.1 fusion.2
  4.1 0.7 %pad_maximum_fusion.1.send_ref = bf16[336,384]{1,0:T(8,128)(2,1)} fusion(bf16[16,384]{1,0:T(8,128)(2,1)S(1)} %select_select_fusion.1, bf16[64,384]{1,0:T(8,128)(2,1)S(1)} %select_select_fusion, bf16[256,384]{1,0:T(8,128)(2,1)S(1)} %fusion.2), kind=kLoop, calls=%fused_computation.2 | loop fusion | flops 774144 | bytes 516096 | tf_op jit(solution)/shard_map/concatenate | solution.py:318
  4.9 0.1 copy-done.1
  5.0 0.2 copy.20
  5.2 0.2 concatenate.9.clone
  5.4 0.1 reshape.59
  5.6 1.1 %copy.11 = bf16[4,4,4,16,256]{4,3,2,1,0:T(8,128)(2,1)} copy(bf16[4,4,4,16,256]{4,0,1,2,3:T(4,128)(2,1)S(1)} %bitcast.35) | data formatting | bytes 1048576 | tf_op jit(solution)/shard_map/transpose | solution.py:22
  6.6 42.6 %shard_map.64 = bf16[1024,192]{1,0:T(8,128)(2,1)} custom-call(bf16[1024,256]{1,0:T(8,128)(2,1)} %bitcast.37, bf16[1024,384]{1,0:T(8,128)(2,1)} %bitcast.34, bf16[336,384]{1,0:T(8,128)(2,1)} %pad_maximum_fusion.1.send_ref, s32[64]{0:T(128)} %len_ref.1, f32[1,192]{1,0:T(1,128)} %bitcast.39, f32[1,192]{1,0:T(1,128)} %bitcast.40), custom_call_target="tpu_custom_call" | custom-call | tf_op jit(solution)/shard_map/pallas_call | solution.py:292
  49.2 1.4 %copy.22 = bf16[4,4,4,16,192]{4,0,1,2,3:T(4,128)(2,1)S(1)} copy(bf16[4,4,4,16,192]{4,3,2,1,0:T(8,128)(2,1)} %bitcast.38) | data formatting | bytes 786432 | tf_op jit(solution)/shard_map/reshape | solution.py:28
  50.7 0.3 reshape.66
  51.0 0.9 %copy.19 = bf16[192,1024]{1,0:T(8,128)(2,1)} copy(bf16[192,1024]{0,1:T(8,128)(2,1)S(1)} %reshape.66) | data formatting | bytes 786432 | tf_op jit(solution)/shard_map/reshape | solution.py:30
  (4 shorter events, 0.1 us)
Async XLA Ops:
  2.2 1.3 %copy-start = (bf16[4,4,4,16,384]{4,3,2,1,0:T(8,128)(2,1)}, bf16[4,4,4,16,384]{4,3,2,1,0:T(8,128)(2,1)S(1)}, u32[]{:S(2)}) copy-start(bf16[4,4,4,16,384]{4,3,2,1,0:T(8,128)(2,1)S(1)} %copy.13) | copy-start | bytes 2359300
  4.0 1.0 %copy-start.1 = (bf16[192,1024]{1,0:T(8,128)(2,1)S(1)}, bf16[192,1024]{1,0:T(8,128)(2,1)}, u32[]{:S(2)}) copy-start(bf16[192,1024]{1,0:T(8,128)(2,1)} %param.6) | copy-start | bytes 1179652

commit v19 on v18

--- a/solution.py
+++ b/solution.py
@@ -229,8 +229,8 @@
     shares = []
     for o in range(1, ys):
         cp = pltpu.make_async_remote_copy(
-            src_ref=stats,
-            dst_ref=ybuf.at[hy],
+            src_ref=stats.at[pl.ds(0, 2)],
+            dst_ref=ybuf.at[hy, pl.ds(0, 2)],
             send_sem=y_send.at[o - 1],
             recv_sem=y_recv.at[0],
             device_id=(me, lax.rem(hy + o, ys)),
@@ -238,7 +238,7 @@
         )
         cp.start()
         shares.append(cp)
-    arrived = ybuf.at[pl.ds(0, ys - 1)]
+    arrived = ybuf.at[pl.ds(0, ys - 1), pl.ds(0, 2)]
     pltpu.make_async_copy(arrived, arrived, y_recv.at[0]).wait()
     for cp in shares:
         cp.wait_send()

time: 52.7 us -> 52.1 us (0.989)
  no operation moved by 1% of the time
where the time goes in v19:
time: 52.1 us; the launch traced here: 51.4 us
  Pallas kernels  42.1 us (81%)
  local copies, waits for them, and re-layouts  7.08 us (14%)
  other arithmetic  2.14 us (4%)
    pallas_call x1, Pallas kernels, per_device(): pl.pallas_call(attention_kernel, out_shape=jax.ShapeDtypeStruct((LOCAL, w...  42.1 us
    dynamic_slice x5, local copies, waits for them, and re-layouts, per_device(): piece = lax.dynamic_slice_in_dim(kv, starts[j], count, 0)  1.61 us
    transpose x2, local copies, waits for them, and re-layouts, to_token_major(): x = jnp.transpose(x, (4, 3, 2, 1, 0))  1.55 us
    reshape x1, local copies, waits for them, and re-layouts, from_token_major(): x = x.reshape(4, 4, 4, 16, f)  1.45 us
    reshape x2, local copies, waits for them, and re-layouts, from_token_major(): return x.reshape(f, LOCAL)  1.25 us
    concatenate x1, other arithmetic, per_device(): kv = to_token_major(jnp.concatenate([values, keys]))  1.17 us

profile of v19, /device:TPU:4, one launch (start us, length us, event | category | flops | bytes accessed | tf_op | source)
XLA Modules:
  0.0 51.4 jit_solution(11851557839585587403)
XLA Ops:
  0.0 1.2 %pad_maximum_fusion = bf16[384,1024]{1,0:T(8,128)(2,1)S(1)} fusion(bf16[192,1024]{1,0:T(8,128)(2,1)} %param.7, bf16[192,1024]{1,0:T(8,128)(2,1)} %param.8), kind=kLoop, calls=%fused_computation | loop fusion | flops 1572864 | bytes 1572864 | tf_op jit(solution)/shard_map/concatenate | solution.py:277
  1.2 0.4 copy.12
  1.5 0.2 reshape.61
  1.7 0.5 copy.13
  2.2 0.0 copy-start
  2.3 1.1 %fusion.7 = (bf16[1,4,4,16,384]{4,0,1,2,3:T(2,128)(2,1)S(1)}, bf16[1,4,4,16,384]{4,0,1,2,3:T(2,128)(2,1)S(1)}, bf16[1,4,4,16,384]{4,0,1,2,3:T(2,128)(2,1)S(1)}, bf16[1,4,4,16,384]{4,0,1,2,3:T(2,128)(2,1)S(1)}) fusion(bf16[4,4,4,16,384]{4,0,1,2,3:T(4,128)(2,1)S(1)} %bitcast.31), kind=kLoop, calls=%fused_computation.22 | loop fusion | bytes 1572864 | tf_op jit(solution)/shard_map/dynamic_slice | solution.py:285
  3.5 0.0 copy-done
  3.5 0.1 copy.14
  3.6 0.1 copy.15
  3.7 0.1 copy.16
  3.9 0.1 copy.17
  4.0 0.0 copy-start.1
  4.0 0.1 fusion.2
  4.1 0.7 %pad_maximum_fusion.1.send_ref = bf16[336,384]{1,0:T(8,128)(2,1)} fusion(bf16[16,384]{1,0:T(8,128)(2,1)S(1)} %select_select_fusion.1, bf16[64,384]{1,0:T(8,128)(2,1)S(1)} %select_select_fusion, bf16[256,384]{1,0:T(8,128)(2,1)S(1)} %fusion.2), kind=kLoop, calls=%fused_computation.2 | loop fusion | flops 774144 | bytes 516096 | tf_op jit(solution)/shard_map/concatenate | solution.py:318
  4.9 0.1 copy-done.1
  5.0 0.2 copy.20
  5.2 0.2 concatenate.9.clone
  5.4 0.1 reshape.59
  5.6 1.1 %copy.11 = bf16[4,4,4,16,256]{4,3,2,1,0:T(8,128)(2,1)} copy(bf16[4,4,4,16,256]{4,0,1,2,3:T(4,128)(2,1)S(1)} %bitcast.35) | data formatting | bytes 1048576 | tf_op jit(solution)/shard_map/transpose | solution.py:22
  6.6 42.1 %shard_map.64 = bf16[1024,192]{1,0:T(8,128)(2,1)} custom-call(bf16[1024,256]{1,0:T(8,128)(2,1)} %bitcast.37, bf16[1024,384]{1,0:T(8,128)(2,1)} %bitcast.34, bf16[336,384]{1,0:T(8,128)(2,1)} %pad_maximum_fusion.1.send_ref, s32[64]{0:T(128)} %len_ref.1, f32[1,192]{1,0:T(1,128)} %bitcast.39, f32[1,192]{1,0:T(1,128)} %bitcast.40), custom_call_target="tpu_custom_call" | custom-call | tf_op jit(solution)/shard_map/pallas_call | solution.py:292
  48.7 1.4 %copy.22 = bf16[4,4,4,16,192]{4,0,1,2,3:T(4,128)(2,1)S(1)} copy(bf16[4,4,4,16,192]{4,3,2,1,0:T(8,128)(2,1)} %bitcast.38) | data formatting | bytes 786432 | tf_op jit(solution)/shard_map/reshape | solution.py:28
  50.2 0.3 reshape.66
  50.5 0.9 %copy.19 = bf16[192,1024]{1,0:T(8,128)(2,1)} copy(bf16[192,1024]{0,1:T(8,128)(2,1)S(1)} %reshape.66) | data formatting | bytes 786432 | tf_op jit(solution)/shard_map/reshape | solution.py:30
  (4 shorter events, 0.1 us)
Async XLA Ops:
  2.2 1.3 %copy-start = (bf16[4,4,4,16,384]{4,3,2,1,0:T(8,128)(2,1)}, bf16[4,4,4,16,384]{4,3,2,1,0:T(8,128)(2,1)S(1)}, u32[]{:S(2)}) copy-start(bf16[4,4,4,16,384]{4,3,2,1,0:T(8,128)(2,1)S(1)} %copy.13) | copy-start | bytes 2359300
  4.0 1.0 %copy-start.1 = (bf16[192,1024]{1,0:T(8,128)(2,1)S(1)}, bf16[192,1024]{1,0:T(8,128)(2,1)}, u32[]{:S(2)}) copy-start(bf16[192,1024]{1,0:T(8,128)(2,1)} %param.6) | copy-start | bytes 1179652
